TPU v7x, 32 devices: a whole 2x2x4 slice. The times are simulated.
32 devices in a mesh: dom: 32 (over z, y, x, core), rep: 1.
Axes of the slice: x: 2, y: 2, z: 4, core: 2. Of those that a mesh axis runs over, the one named last changes fastest.
Arguments:
- query_fde: bfloat16 [256, 10240], P(('rep', 'dom')), may hold values from -6 to 6
- doc_fde: bfloat16 [16384, 10240], P('dom'), may hold values from -0.0625 to 0.0625
- frontier_owner: int32 [3, 256, 16], P(None, ('rep', 'dom')), may hold values from 0 to 31, all different within a row; in each aligned block of 8 rows (0 to 7, 8 to 15, ..., all dimensions but the last counted through in order) at most 8 rows name the same one
- frontier_slot: int32 [3, 256, 16], P(None, ('rep', 'dom')), may hold values from 0 to 511
- query_tokens: bfloat16 [256, 32, 128], P(('rep', 'dom')), may hold values from -6 to 6
- passage_tiles: bfloat16 [8192, 128, 128], P('dom'), may hold values from -0.5 to 0.5
- passage_len: int32 [8192], P('dom'), may hold values from 16 to 128
- cand_owner: int32 [256, 32, 1], P(('rep', 'dom')), may hold values from 0 to 31; in each aligned block of 256 rows (0 to 255, 256 to 511, ..., all dimensions but the last counted through in order) at most 16 rows name the same one
- cand_slot: int32 [256, 32], P(('rep', 'dom')), may hold values from 0 to 255
Outputs:
- beam_scores: float32 [3, 256, 16], P(None, ('rep', 'dom'))
- maxsim_scores: float32 [256, 32], P(('rep', 'dom'))
Inputs may be any that keep to these rules, and one draw needn't show every extreme that they name: `frontier_owner`: the 16 partitions of one query in one round are distinct. Among the queries of one index of dom in one round no partition is named by more than 8 queries, a bound that some block reaches. `cand_owner`: among the candidates of the queries of one index of dom no shard is named more than 16 times, a bound that some block reaches. Candidates may repeat.
All inputs are finite; a program needn't handle non-finite values.
Results may differ from a plain program's by a relative error of at most 0.0003.
Values may be sent and summed in bfloat16 or wider, within the bound.
No kernel may reach another device: no remote copies, remote signals or barrier semaphores. Data moves between devices by JAX's collectives and lax.ppermute only.
A program may use at most 256 MiB of HBM per device.

v0:
```python
import jax
import jax.numpy as jnp
from jax import lax
from jax.sharding import PartitionSpec as P

masked_value = -1e30


def bucket_slots(owners, groups):
    onehot = (owners[:, None] == jnp.arange(groups, dtype=jnp.int32)[None, :]).astype(jnp.int32)
    earlier = jnp.cumsum(onehot, axis=0) - onehot
    return jnp.sum(earlier * onehot, axis=1)


def pack_slots(owners, slot_ids, sources, payload, groups, capacity):
    position = bucket_slots(owners, groups)
    target = owners * capacity + position
    packed = (
        jnp.zeros((groups * capacity,) + payload.shape[1:], payload.dtype)
        .at[target]
        .set(payload[sources])
    )
    labels = jnp.zeros((groups * capacity,), jnp.int32).at[target].set(slot_ids)
    return (
        packed.reshape((groups, capacity) + payload.shape[1:]),
        labels.reshape(groups, capacity),
        target,
    )


def late_scores(tokens, tile_data, lengths):
    similarity = jnp.einsum(
        "gkqd,gktd->gkqt", tokens, tile_data, preferred_element_type=jnp.float32
    )
    is_valid = (
        jnp.arange(tile_data.shape[2], dtype=jnp.int32)[None, None, None, :]
        < lengths[:, :, None, None]
    )
    maxima = jnp.max(jnp.where(is_valid, similarity, masked_value), axis=3)
    return jnp.mean(maxima, axis=2)


def local(
    query_fde,
    doc_fde,
    frontier_owner,
    frontier_slot,
    query_tokens,
    passage_tiles,
    passage_len,
    cand_owner,
    cand_slot,
):
    groups = lax.axis_size("dom")
    rounds, query_count, frontier_width = frontier_owner.shape
    cap_beam = max(2, min(query_count, 2 * query_count * frontier_width // groups))
    entries = query_count * frontier_width
    sources = jnp.arange(entries, dtype=jnp.int32) // frontier_width
    every_query = lax.all_gather(query_fde, "dom", axis=0, tiled=True)
    global_ids = lax.axis_index("dom") * query_count + jnp.arange(query_count, dtype=jnp.int32)
    all_sources = jnp.tile(sources, rounds)
    packed, labels, target = pack_slots(
        frontier_owner.reshape(-1),
        frontier_slot.reshape(-1),
        all_sources,
        global_ids,
        groups,
        rounds * cap_beam,
    )
    query_ids = lax.all_to_all(packed, "dom", split_axis=0, concat_axis=0, tiled=True)
    slot_ids = lax.all_to_all(labels, "dom", split_axis=0, concat_axis=0, tiled=True)
    scored = jnp.einsum(
        "gkf,gkf->gk", every_query[query_ids], doc_fde[slot_ids], preferred_element_type=jnp.float32
    )
    returned = lax.all_to_all(scored, "dom", split_axis=0, concat_axis=0, tiled=True)
    beam_scores = returned.reshape(-1)[target].reshape(rounds, query_count, frontier_width)
    cand_count = cand_slot.shape[1]
    pair_count = query_count * cand_count
    cap_cand = max(2, min(pair_count, 2 * pair_count // groups))
    cand_sources = jnp.arange(pair_count, dtype=jnp.int32) // cand_count
    packed, labels, target = pack_slots(
        cand_owner[:, :, 0].reshape(-1),
        cand_slot.reshape(-1),
        cand_sources,
        query_tokens,
        groups,
        cap_cand,
    )
    requests = lax.all_to_all(labels, "dom", split_axis=0, concat_axis=0, tiled=True)
    replies = (
        lax.all_to_all(passage_tiles[requests], "dom", split_axis=0, concat_axis=0, tiled=True),
        lax.all_to_all(passage_len[requests], "dom", split_axis=0, concat_axis=0, tiled=True),
    )
    scored = late_scores(packed, replies[0], replies[1])
    maxsim_scores = scored.reshape(-1)[target].reshape(query_count, cand_count)
    return (beam_scores, maxsim_scores)


def solution(mesh):
    in_specs = (
        P(("rep", "dom"), None),
        P("dom", None),
        P(None, ("rep", "dom"), None),
        P(None, ("rep", "dom"), None),
        P(("rep", "dom"), None, None),
        P("dom", None, None),
        P("dom"),
        P(("rep", "dom"), None, None),
        P(("rep", "dom"), None),
    )
    out_specs = (P(None, ("rep", "dom"), None), P(("rep", "dom"), None))
    return jax.shard_map(local, mesh=mesh, in_specs=in_specs, out_specs=out_specs, check_vma=False)
```

profile of v0, /device:TPU:0, one launch (start us, length us, event | category | flops | bytes accessed | tf_op | source)
XLA Modules:
  0.0 565.8 jit_solution(7422721636747998464)
XLA Ops:
  7.9 0.8 eq.62
  10.0 1.4 fusion.17
  11.6 0.8 reshape.410
  12.4 1.4 scatter_custom_fusion.2
  14.5 7.3 %all-to-all-start.3 = ((s32[32,1,16]{2,1,0:T(1,128)}), s32[32,1,16]{2,1,0:T(1,128)S(1)}, u32[]{:S(2)}, u32[]{:S(2)}) async-start(s32[32,1,16]{2,1,0:T(1,128)} %bitcast.19), calls=%async_computation.3 | async-start | bytes 32768 | tf_op jit(solution)/shard_map/all_to_all | solution.py:89
  21.8 0.8 eq.54
  22.6 0.8 eq.50
  23.4 0.9 reduce-window.14
  24.5 0.7 broadcast_multiply_fusion.1
  26.1 4.3 fusion.13
  31.1 2.9 scatter_custom_fusion
  34.7 0.8 reshape.402
  35.5 2.9 scatter_custom_fusion.1
  39.1 5.8 %all-to-all-start = ((s32[32,1,24]{2,1,0:T(1,128)}), s32[32,1,24]{2,1,0:T(1,128)S(1)}, u32[]{:S(2)}, u32[]{:S(2)}) async-start(s32[32,1,24]{2,1,0:T(1,128)} %bitcast.9), calls=%async_computation | async-start | bytes 32768 | tf_op jit(solution)/shard_map/all_to_all | solution.py:70
  45.1 3.5 gather_fusion.3
  49.3 2.9 all-to-all-done
  52.2 2.9 all-to-all-start.1
  55.2 7.1 %all-to-all-done.1 = s32[32,1,24]{2,1,0:T(1,128)S(1)} async-done(((s32[32,1,24]{2,1,0:T(1,128)}), s32[32,1,24]{2,1,0:T(1,128)S(1)}, u32[]{:S(2)}, u32[]{:S(2)}) %all-to-all-start.1) | async-done | bytes 3104 | tf_op jit(solution)/shard_map/all_to_all | solution.py:71
  62.3 2.7 all-to-all-start.4
  65.1 32.4 %gather_fusion.1 = bf16[768,10240]{1,0:T(8,128)(2,1)} fusion(bf16[512,10240]{1,0:T(8,128)(2,1)} %param.10, s32[1024]{0:T(1024)S(1)} %pad_clamp_fusion.4), kind=kCustom, calls=%fused_computation.1 | custom fusion | bytes 31460352 | tf_op jit(solution)/shard_map/gather | solution.py:73
  97.5 30.4 %gather_fusion = bf16[768,10240]{1,0:T(8,128)(2,1)} fusion(bf16[256,10240]{1,0:T(8,128)(2,1)} %all-gather.2.cloned.1.call-done, s32[1024]{0:T(1024)S(1)} %pad_clamp_fusion.5), kind=kCustom, calls=%fused_computation | custom fusion | bytes 31460352 | tf_op jit(solution)/shard_map/gather | solution.py:73
  127.9 13.4 %fusion = f32[32,24]{1,0:T(8,128)} fusion(bf16[32,24,10240]{2,1,0:T(8,128)(2,1)} %bitcast.85, bf16[32,24,10240]{2,1,0:T(8,128)(2,1)} %bitcast.84), kind=kLoop, calls=%fused_computation.12 | loop fusion | flops 31456512 | bytes 31460352 | tf_op jit(solution)/shard_map/gkf,gkf->gk/dot_general | solution.py:72
  141.3 5.7 %all-to-all-start.2 = ((f32[32,1,24]{2,1,0:T(1,128)}), f32[32,1,24]{2,1,0:T(1,128)S(1)}, u32[]{:S(2)}, u32[]{:S(2)}) async-start(f32[32,1,24]{2,1,0:T(1,128)} %bitcast.15), calls=%async_computation.2 | async-start | bytes 32768 | tf_op jit(solution)/shard_map/all_to_all | solution.py:75
  147.0 16.8 %gather_fusion.5 = bf16[512,128,128]{2,1,0:T(8,128)(2,1)} fusion(bf16[256,128,128]{2,1,0:T(8,128)(2,1)} %param.14, s32[1024]{0:T(1024)S(1)} %pad_clamp_fusion.2), kind=kCustom, calls=%fused_computation.5 | custom fusion | bytes 33556480 | tf_op jit(solution)/shard_map/gather | solution.py:91
  163.8 6.4 %all-to-all-start.5 = ((bf16[32,16,128,128]{3,2,1,0:T(8,128)(2,1)}), bf16[32,16,128,128]{3,2,1,0:T(8,128)(2,1)}, u32[]{:S(2)}, u32[]{:S(2)}) async-start(bf16[32,16,128,128]{3,2,1,0:T(8,128)(2,1)} %bitcast.83), calls=%async_computation.5 | async-start | bytes 33554432 | tf_op jit(solution)/shard_map/all_to_all | solution.py:91
  170.3 1.0 gather_fusion.4
  171.3 2.6 broadcast_in_dim.14
  173.9 26.5 %scatter_fusion = bf16[512,32,128]{2,1,0:T(8,128)(2,1)} fusion(bf16[512,32,128]{2,1,0:T(8,128)(2,1)} %broadcast_in_dim.14, s32[256]{0:T(256)S(1)} %bitcast.93, bf16[256,32,128]{2,1,0:T(8,128)(2,1)S(1)} %gather_fusion.4), kind=kCustom, calls=%fused_computation.10 | custom fusion | bytes 6292480 | tf_op jit(solution)/shard_map/scatter | solution.py:21
  201.8 1.9 gather_fusion.2
  204.4 338.6 %all-to-all-done.5 = bf16[32,16,128,128]{3,2,1,0:T(8,128)(2,1)} async-done(((bf16[32,16,128,128]{3,2,1,0:T(8,128)(2,1)}), bf16[32,16,128,128]{3,2,1,0:T(8,128)(2,1)}, u32[]{:S(2)}, u32[]{:S(2)}) %all-to-all-start.5) | async-done | bytes 16777248 | tf_op jit(solution)/shard_map/all_to_all | solution.py:91
  542.9 13.2 %select_reduce_fusion = f32[32,16,32]{2,1,0:T(8,128)S(1)} fusion(pred[32,16,128]{2,1,0:T(8,128)(4,1)S(1)} %iota_compare_fusion, bf16[32,16,32,128]{3,2,1,0:T(8,128)(2,1)} %bitcast.86, bf16[32,16,128,128]{3,2,1,0:T(8,128)(2,1)} %all-to-all-done.5), kind=kOutput, calls=%fused_computation.13 | convolution fusion | flops 541048832 | bytes 21102592 | tf_op jit(solution)/shard_map/gkqd,gktd->gkqt/dot_general | solution.py:32
  556.3 1.9 gather_fusion.6
  (58 shorter events, 10.2 us)
Async XLA Ops:
  7.2 163.1 %copy-start = (bf16[8,32,128]{2,1,0:T(8,128)(2,1)S(1)}, bf16[8,32,128]{2,1,0:T(8,128)(2,1)}, u32[]{:S(2)}) copy-start(bf16[8,32,128]{2,1,0:T(8,128)(2,1)} %param.13) | copy-start | bytes 196612
  7.2 37.9 %copy-start.1 = (s32[256]{0:T(256)S(1)}, s32[256]{0:T(256)}, u32[]{:S(2)}) copy-start(s32[256]{0:T(256)} %param.15) | copy-start | bytes 3076
  7.2 90.3 %all-gather.2.cloned.1.call-start = ((), (), s32[]{:S(2)}) async-start(), calls=%async_computation.6 | async-start | bytes 5406720 | tf_op jit(solution)/shard_map/all_gather | solution.py:59
  14.5 24.6 %all-to-all-start.3 = ((s32[32,1,16]{2,1,0:T(1,128)}), s32[32,1,16]{2,1,0:T(1,128)S(1)}, u32[]{:S(2)}, u32[]{:S(2)}) async-start(s32[32,1,16]{2,1,0:T(1,128)} %bitcast.19), calls=%async_computation.3 | async-start | bytes 32768 | tf_op jit(solution)/shard_map/all_to_all | solution.py:89
  39.1 13.1 %all-to-all-start = ((s32[32,1,24]{2,1,0:T(1,128)}), s32[32,1,24]{2,1,0:T(1,128)S(1)}, u32[]{:S(2)}, u32[]{:S(2)}) async-start(s32[32,1,24]{2,1,0:T(1,128)} %bitcast.9), calls=%async_computation | async-start | bytes 32768 | tf_op jit(solution)/shard_map/all_to_all | solution.py:70
  52.2 10.1 %all-to-all-start.1 = ((s32[32,1,24]{2,1,0:T(1,128)}), s32[32,1,24]{2,1,0:T(1,128)S(1)}, u32[]{:S(2)}, u32[]{:S(2)}) async-start(s32[32,1,24]{2,1,0:T(1,128)} %bitcast.12), calls=%async_computation.1 | async-start | bytes 32768 | tf_op jit(solution)/shard_map/all_to_all | solution.py:71
  62.3 79.0 %all-to-all-start.4 = ((s32[32,1,16]{2,1,0:T(1,128)}), s32[32,1,16]{2,1,0:T(1,128)S(1)}, u32[]{:S(2)}, u32[]{:S(2)}) async-start(s32[32,1,16]{2,1,0:T(1,128)} %bitcast.21), calls=%async_computation.4 | async-start | bytes 32768 | tf_op jit(solution)/shard_map/all_to_all | solution.py:92
  141.3 22.5 %all-to-all-start.2 = ((f32[32,1,24]{2,1,0:T(1,128)}), f32[32,1,24]{2,1,0:T(1,128)S(1)}, u32[]{:S(2)}, u32[]{:S(2)}) async-start(f32[32,1,24]{2,1,0:T(1,128)} %bitcast.15), calls=%async_computation.2 | async-start | bytes 32768 | tf_op jit(solution)/shard_map/all_to_all | solution.py:75
  163.8 379.1 %all-to-all-start.5 = ((bf16[32,16,128,128]{3,2,1,0:T(8,128)(2,1)}), bf16[32,16,128,128]{3,2,1,0:T(8,128)(2,1)}, u32[]{:S(2)}, u32[]{:S(2)}) async-start(bf16[32,16,128,128]{3,2,1,0:T(8,128)(2,1)} %bitcast.83), calls=%async_computation.5 | async-start | bytes 33554432 | tf_op jit(solution)/shard_map/all_to_all | solution.py:91
Sparse Core Ops, SparseCore 0:
  10.9 68.3 all-gather.1
where the time goes:
time: 568 us; the launch traced here: 566 us
  waiting for transfers between devices  349 us (61%)
  local copies, waits for them, and re-layouts  135 us (24%)
  starting transfers between devices  30.8 us (5%)
  other arithmetic  23.3 us (4%)
  between operations  14.3 us (3%)
  matrix products  13.2 us (2%)
    all_to_all x1, waiting for transfers between devices, local(): lax.all_to_all(passage_tiles[requests], 'dom', split_axis=0, concat_axis=...  339 us
    gather x1, local copies, waits for them, and re-layouts, local(): doc_fde[slot_ids]  32.4 us
    gather x1, local copies, waits for them, and re-layouts, local(): every_query[query_ids]  30.4 us
    scatter x2, local copies, waits for them, and re-layouts, pack_slots(): packed = jnp.zeros((groups * capacity,) + payload.shape[1:], payload.dtyp...  29.4 us
    gather x1, local copies, waits for them, and re-layouts, local(): passage_tiles[requests]  16.8 us
    dot_general x1, other arithmetic, local(): jnp.einsum('gkf,gkf->gk', every_query[query_ids], doc_fde[slot_ids], pref...  13.4 us
    dot_general x1, matrix products, late_scores(): jnp.einsum('gkqd,gktd->gkqt', tokens, tile_data, preferred_element_type=j...  13.2 us
  transfers between devices with their start and end apart: 7, of which 3 were waited for; matrix products, arithmetic and copies ran while one was open for 27% of the time, Pallas kernels for 0%

commit v1 on v0

v1 whole, which is shorter than its diff:
```python
import functools
import math

import jax
import jax.numpy as jnp
from jax import lax
from jax.experimental import pallas as pl
from jax.experimental.pallas import tpu as pltpu
from jax.sharding import PartitionSpec as P

masked_value = -1e30
LANES = 128
GROUP = 4
VMEM = pl.BlockSpec(memory_space=pltpu.VMEM)
NT = (((1,), (1,)), ((), ()))


def sources_of(order):
    masks = [0]
    for bit in order:
        masks = masks + [m ^ bit for m in masks]
    return masks


def orders_of(n):
    bits = [1 << i for i in range(1, n.bit_length() - 1)]
    far, rest = bits[-1], bits[:-1]
    return [[far] + rest[i:] + rest[:i] for i in (0, len(rest) - 1, 1)]


def exchange(x, bit, n):
    return lax.ppermute(x, "dom", [(i, i ^ bit) for i in range(n)])


def place(values, offset):
    w = values.shape[1]
    where = lax.broadcasted_iota(jnp.int32, (w, LANES), 0) + offset
    lane = lax.broadcasted_iota(jnp.int32, (w, LANES), 1)
    return jnp.dot(
        values.astype(jnp.float32).astype(jnp.bfloat16),
        (where == lane).astype(jnp.float32).astype(jnp.bfloat16),
        preferred_element_type=jnp.float32,
    )


def prep_kernel(parts, fo, fs, co, cs, tok, out):
    rounds, _, front = fo.shape
    rows = tok.shape[0]
    cand_at = rounds * front
    first = place(co[...] * parts, cand_at)
    second = place(cs[...], cand_at)
    for r in range(rounds):
        first = first + place(fo[r] * parts + (fs[r] >> 8), r * front)
        second = second + place(fs[r] & 255, r * front)
    out[:rows, :] = tok[...]
    out[rows:, :] = jnp.concatenate([first, second], axis=0).astype(jnp.bfloat16)


def maxsim_kernel(cand_at, cands, stride, lst, cnt, lens, own, other, tiles, out):
    qt = (stride - 16) // 8
    blocks = own.shape[0] // stride
    pt = tiles.shape[1]
    cap = lst.shape[0] // (2 * blocks)
    width = stride - 16
    token = lax.broadcasted_iota(jnp.int32, (pt, width), 0)
    column = lax.broadcasted_iota(jnp.int32, (1, width), 1) // qt
    row = lax.broadcasted_iota(jnp.int32, (8, LANES), 0)
    lane = lax.broadcasted_iota(jnp.int32, (8, LANES), 1)
    for side, ref in enumerate((own, other)):

        def source(b, carry, side=side, ref=ref):
            at = side * blocks + b
            weights = ref[pl.ds(pl.multiple_of(b * stride, 16), width), :]
            held = cnt[at]

            def group(g, acc):
                entries = [lst[at * cap + g * GROUP + j] for j in range(GROUP)]
                slots = [e & 255 for e in entries]
                data = jnp.concatenate([tiles[s] for s in slots], axis=0)
                sim = lax.dot_general(data, weights, NT, preferred_element_type=jnp.float32)
                for j in range(GROUP):
                    pair = entries[j] >> 8
                    query, cand = pair // cands, pair % cands
                    part = sim[j * pt : (j + 1) * pt, :]
                    part = jnp.where(token < lens[slots[j]], part, masked_value)
                    top = jnp.max(part, axis=0, keepdims=True)
                    score = jnp.sum(jnp.where(column == query, top, 0.0), axis=1, keepdims=True) * (1.0 / qt)
                    there = jnp.where(g * GROUP + j < held, cand_at + cand, -1)
                    acc = acc + jnp.where((row == query) & (lane == there), score, 0.0)
                return acc

            out[at] = lax.fori_loop(0, (held + GROUP - 1) // GROUP, group, jnp.zeros((8, LANES), jnp.float32))
            return carry

        lax.fori_loop(0, blocks, source, 0)


def beam_kernel(own, other, doc, total):
    @pl.when(pl.program_id(0) == 0)
    def _():
        total[...] = jnp.zeros_like(total)

    left = jnp.concatenate([own[...], other[...]], axis=0)
    total[...] += lax.dot_general(left, doc[...], NT, preferred_element_type=jnp.float32)


def last_kernel(cfg, me_ref, own, other, doc, so_far, codes_own, codes_other, maxsim, out, total):
    order, first_order, code_order, parts, cand_at, stride = cfg
    blocks = len(order)
    half = blocks * 8

    @pl.when(pl.program_id(0) == 0)
    def _():
        for side in range(2):
            for p in range(blocks):
                q = first_order.index(order[p])
                total[side * half + p * 8 : side * half + p * 8 + 8, :] = so_far[
                    side * half + q * 8 : side * half + q * 8 + 8, :
                ]

    left = jnp.concatenate([own[...], other[...]], axis=0)
    total[...] += lax.dot_general(left, doc[...], NT, preferred_element_type=jnp.float32)

    @pl.when(pl.program_id(0) == pl.num_programs(0) - 1)
    def _():
        me = me_ref[0]
        lane = lax.broadcasted_iota(jnp.int32, (8, LANES), 1)
        nodes = total.shape[1]
        for side, ref in enumerate((codes_own, codes_other)):
            for p in range(blocks):
                t = code_order.index(order[p])
                codes = ref[t * stride + stride - 16 : (t + 1) * stride, :].astype(jnp.float32).astype(jnp.int32)
                owner, high, low = codes[:8] // parts, codes[:8] % parts, codes[8:]
                slot = high * 256 + low
                within, page = slot % LANES, slot // LANES
                rows = total[side * half + p * 8 : side * half + p * 8 + 8, :]
                found = jnp.zeros((8, LANES), jnp.float32)
                for g in range(nodes // LANES):
                    here = jnp.take_along_axis(rows[:, g * LANES : (g + 1) * LANES], within, axis=1)
                    found = jnp.where(page == g, here, found)
                found = jnp.where(owner == me, found, 0.0)
                out[me ^ (order[p] + side)] = jnp.where(lane < cand_at, found, maxsim[side * blocks + t])


def sum_kernel(rounds, front, cands, parts, beam, maxsim):
    total = parts[0]
    for i in range(1, parts.shape[0]):
        total = total + parts[i]
    for r in range(rounds):
        beam[r] = (total if r == 0 else pltpu.roll(total, LANES - r * front, axis=1))[:, :front]
    maxsim[...] = pltpu.roll(total, LANES - rounds * front, axis=1)[:, :cands]


def local(n, query_fde, doc_fde, frontier_owner, frontier_slot, query_tokens, passage_tiles, passage_len, cand_owner, cand_slot):
    rounds, queries, front = frontier_owner.shape
    cands = cand_slot.shape[1]
    nodes, fde = doc_fde.shape
    qt, dim = query_tokens.shape[1:]
    parts = nodes // 256
    cand_at = rounds * front
    assert n & (n - 1) == 0 and queries == 8 and dim == LANES and nodes % 256 == 0
    assert cand_at + cands <= LANES and n * parts <= 256 and passage_tiles.shape[0] <= 256
    me = lax.axis_index("dom").astype(jnp.int32)
    stride = queries * qt + 16
    blocks = n // 2
    orders = orders_of(n)
    masks = [sources_of(o) for o in orders]

    packed = pl.pallas_call(
        functools.partial(prep_kernel, parts),
        out_shape=jax.ShapeDtypeStruct((stride, dim), jnp.bfloat16),
        in_specs=[VMEM] * 5,
        out_specs=VMEM,
        name="pack",
    )(frontier_owner, frontier_slot, cand_owner.reshape(queries, cands), cand_slot, query_tokens.reshape(queries * qt, dim))

    half = fde // 2
    chunks = [packed, query_fde[:, :half], query_fde[:, half:]]
    for step in range(len(orders[0])):
        for k in range(3):
            chunks[k] = jnp.concatenate([chunks[k], exchange(chunks[k], orders[k][step], n)], axis=0)
    pairs = [(c, exchange(c, 1, n)) for c in chunks]
    (tok_own, tok_other), (a_own, a_other), (b_own, b_other) = pairs

    codes = jnp.stack(pairs[0]).reshape(n, stride, dim)[:, queries * qt :, cand_at : cand_at + cands]
    codes = codes.astype(jnp.int32)
    mine = (codes[:, :queries] // parts == me).reshape(n, queries * cands)
    slots = codes[:, queries:].reshape(n, queries * cands)
    cap = max(2, min(queries * cands, 2 * queries * cands // n))
    position = jnp.cumsum(mine.astype(jnp.int32), axis=1) - 1
    payload = jnp.arange(queries * cands, dtype=jnp.int32)[None] * 256 + slots
    chosen = mine[:, None, :] & (position[:, None, :] == jnp.arange(cap, dtype=jnp.int32)[None, :, None])
    entries = jnp.sum(jnp.where(chosen, payload[:, None, :], 0), axis=2)
    counts = jnp.sum(mine.astype(jnp.int32), axis=1)

    pairs_bound = n * cap
    maxsim = pl.pallas_call(
        functools.partial(maxsim_kernel, cand_at, cands, stride),
        out_shape=jax.ShapeDtypeStruct((n, 8, LANES), jnp.float32),
        grid_spec=pltpu.PrefetchScalarGridSpec(
            num_scalar_prefetch=3, grid=(), in_specs=[VMEM] * 3, out_specs=VMEM
        ),
        compiler_params=pltpu.CompilerParams(vmem_limit_bytes=24 << 20),
        cost_estimate=pl.CostEstimate(
            flops=2 * pairs_bound * 128 * 256 * 128, bytes_accessed=8 << 20, transcendentals=0
        ),
        name="maxsim",
    )(entries.reshape(-1), counts, passage_len, tok_own, tok_other, passage_tiles)

    block = math.gcd(half, 1280)
    steps = half // block
    rows = n * 8

    def beam_specs(first, prefetch):
        left = pl.BlockSpec((rows // 2, block), lambda i, *_: (0, i))
        return [left, left, pl.BlockSpec((nodes, block), lambda i, *_: (0, first + i))]

    whole = pl.BlockSpec((rows, nodes), lambda i, *_: (0, 0))
    cost = pl.CostEstimate(flops=2 * rows * nodes * half, bytes_accessed=2 * (rows + nodes) * half, transcendentals=0)
    so_far = pl.pallas_call(
        beam_kernel,
        out_shape=jax.ShapeDtypeStruct((rows, nodes), jnp.float32),
        grid=(steps,),
        in_specs=beam_specs(0, 0),
        out_specs=whole,
        compiler_params=pltpu.CompilerParams(vmem_limit_bytes=16 << 20),
        cost_estimate=cost,
        name="beam",
    )(a_own, a_other, doc_fde)
    cfg = (masks[2], masks[1], masks[0], parts, cand_at, stride)
    full = lambda shape: pl.BlockSpec(shape, lambda i, *_: (0,) * len(shape))
    scored = pl.pallas_call(
        functools.partial(last_kernel, cfg),
        out_shape=jax.ShapeDtypeStruct((n, 8, LANES), jnp.float32),
        grid_spec=pltpu.PrefetchScalarGridSpec(
            num_scalar_prefetch=1,
            grid=(steps,),
            in_specs=beam_specs(steps, 1)
            + [whole, full(tok_own.shape), full(tok_own.shape), full((n, 8, LANES))],
            out_specs=full((n, 8, LANES)),
            scratch_shapes=[pltpu.VMEM((rows, nodes), jnp.float32)],
        ),
        compiler_params=pltpu.CompilerParams(vmem_limit_bytes=24 << 20),
        cost_estimate=cost,
        name="beam_last",
    )(me.reshape(1), b_own, b_other, doc_fde, so_far, tok_own, tok_other, maxsim)

    returned = lax.all_to_all(scored, "dom", split_axis=0, concat_axis=0, tiled=True)
    return pl.pallas_call(
        functools.partial(sum_kernel, rounds, front, cands),
        out_shape=(
            jax.ShapeDtypeStruct((rounds, queries, front), jnp.float32),
            jax.ShapeDtypeStruct((queries, cands), jnp.float32),
        ),
        in_specs=[VMEM],
        out_specs=(VMEM, VMEM),
        name="collect",
    )(returned)


def solution(mesh):
    in_specs = (
        P(("rep", "dom"), None),
        P("dom", None),
        P(None, ("rep", "dom"), None),
        P(None, ("rep", "dom"), None),
        P(("rep", "dom"), None, None),
        P("dom", None, None),
        P("dom"),
        P(("rep", "dom"), None, None),
        P(("rep", "dom"), None),
    )
    out_specs = (P(None, ("rep", "dom"), None), P(("rep", "dom"), None))
    return jax.shard_map(
        functools.partial(local, mesh.shape["dom"]), mesh=mesh, in_specs=in_specs, out_specs=out_specs, check_vma=False
    )
```

time: 568 us -> 122 us (0.21)
  waiting for transfers between devices: 349 us -> 16.2 us
  local copies, waits for them, and re-layouts: 135 us -> 14.6 us
  blocking collectives: 0 us -> 35.4 us
  Pallas kernels: 0 us -> 29.3 us
  other arithmetic: 23.3 us -> 3.45 us
  between operations: 14.3 us -> 0.83 us
  matrix products: 13.2 us -> 0 us
  starting transfers between devices: 30.8 us -> 21.2 us
    all_to_all x6 -> x0, waiting for transfers between devices: 349 us -> none  [the longest x1 339 us: local(): lax.all_to_all(passage_tiles[requests], 'dom', split_axis=0, concat_axis=...]
    gather x8 -> x0, local copies, waits for them, and re-layouts: 88.6 us -> none  [the longest x1 32.4 us: local(): doc_fde[slot_ids]]
    all_to_all x0 -> x1, blocking collectives: none -> 35.4 us  [local(): lax.all_to_all(scored, 'dom', split_axis=0, concat_axis=0, tiled=True)]
    scatter x4 -> x0, local copies, waits for them, and re-layouts: 33.7 us -> none  [the longest x2 29.4 us: pack_slots(): packed = jnp.zeros((groups * capacity,) + payload.shape[1:], payload.dtyp...]
    all_to_all x6 -> x0, starting transfers between devices: 30.8 us -> none  [the longest x2 10.2 us: local(): lax.all_to_all(labels, 'dom', split_axis=0, concat_axis=0, tiled=True)]
    pallas_call x0 -> x5, Pallas kernels: none -> 29.3 us  [the longest x1 17.7 us: local(): pl.pallas_call(functools.partial(maxsim_kernel, cand_at, cands, stride),...]
    ppermute x0 -> x15, starting transfers between devices: none -> 21.2 us  [exchange(): return lax.ppermute(x, 'dom', [(i, i ^ bit) for i in range(n)])]
    ppermute x0 -> x15, waiting for transfers between devices: none -> 16.2 us  [exchange(): return lax.ppermute(x, 'dom', [(i, i ^ bit) for i in range(n)])]
  transfers between devices with their start and end apart: 7 -> 15, of which waited for: 3 -> 8; matrix products, arithmetic and copies ran while one was open for 27% -> 10% of each run, Pallas kernels for 0% -> 18%
where the time goes in v1:
time: 122 us; the launch traced here: 121 us
  blocking collectives  35.4 us (29%)
  Pallas kernels  29.3 us (24%)
  starting transfers between devices  21.2 us (17%)
  waiting for transfers between devices  16.2 us (13%)
  local copies, waits for them, and re-layouts  14.6 us (12%)
  other arithmetic  3.45 us (3%)
    all_to_all x1, blocking collectives, local(): lax.all_to_all(scored, 'dom', split_axis=0, concat_axis=0, tiled=True)  35.4 us
    ppermute x15, starting transfers between devices, exchange(): return lax.ppermute(x, 'dom', [(i, i ^ bit) for i in range(n)])  21.2 us
    pallas_call x1, Pallas kernels, local(): pl.pallas_call(functools.partial(maxsim_kernel, cand_at, cands, stride),...  17.7 us
    ppermute x15, waiting for transfers between devices, exchange(): return lax.ppermute(x, 'dom', [(i, i ^ bit) for i in range(n)])  16.2 us
    unnamed x26, local copies, waits for them, and re-layouts  10.6 us
    pallas_call x1, Pallas kernels, local(): pl.pallas_call(functools.partial(last_kernel, cfg), out_shape=jax.ShapeDt...  4.36 us
    pallas_call x1, Pallas kernels, local(): pl.pallas_call(beam_kernel, out_shape=jax.ShapeDtypeStruct((rows, nodes),...  3.98 us
  transfers between devices with their start and end apart: 15, of which 8 were waited for; matrix products, arithmetic and copies ran while one was open for 10% of the time, Pallas kernels for 18%

profile of v1, /device:TPU:0, one launch (start us, length us, event | category | flops | bytes accessed | tf_op | source)
XLA Modules:
  0.0 121.0 jit_solution(1259496052669016683)
XLA Ops:
  0.6 1.7 %pack.1 = bf16[272,128]{1,0:T(8,128)(2,1)} custom-call(s32[3,8,16]{2,1,0:T(8,128)} %fo.1, s32[3,8,16]{2,1,0:T(8,128)} %fs.1, s32[8,32]{1,0:T(8,128)} %bitcast.17, s32[8,32]{1,0:T(8,128)} %cs.1, bf16[256,128]{1,0:T(8,128)(2,1)} %bitcast.16), custom_call_target="tpu_custom_call" | custom-call | tf_op jit(solution)/shard_map/pack/pallas_call | solution.py:169
  2.3 4.0 %collective-permute-start.10 = (bf16[272,128]{1,0:T(8,128)(2,1)}, bf16[272,128]{1,0:T(8,128)(2,1)S(1)}, u32[]{:S(2)}, u32[]{:S(2)}) collective-permute-start(bf16[272,128]{1,0:T(8,128)(2,1)} %pack.1), channel_id=1, source_target_pairs={{0,16},{1,17},{2,18},{3,19},{4,20},{5,21},{6,22},{7,23},{8,24},{9,... | collective-permute-start | bytes 208904 | tf_op jit(solution)/shard_map/ppermute | solution.py:32
  6.3 1.6 %fusion.5 = (bf16[8,5120]{1,0:T(8,128)(2,1)S(1)}, bf16[128,5120]{1,0:T(8,128)(2,1)}, bf16[128,5120]{1,0:T(8,128)(2,1)}, bf16[8,5120]{1,0:T(8,128)(2,1)S(1)}) fusion(bf16[8,10240]{1,0:T(8,128)(2,1)} %param.9), kind=kLoop, calls=%fused_computation.43 | loop fusion | bytes 491520 | tf_op jit(solution)/shard_map/slice | solution.py:178
  8.0 2.9 %collective-permute-start = (bf16[8,5120]{1,0:T(8,128)(2,1)S(1)}, bf16[8,5120]{1,0:T(8,128)(2,1)S(1)}, u32[]{:S(2)}, u32[]{:S(2)}) collective-permute-start(bf16[8,5120]{1,0:T(8,128)(2,1)S(1)} %get-tuple-element.8), channel_id=1, source_target_pairs={{0,16},{1,17},{2,18},{3,19},{4,20},{5,21},{6,22},{7,23},{8,24},{9,... | collective-permute-start | bytes 245768 | tf_op jit(solution)/shard_map/ppermute | solution.py:32
  10.9 0.9 constant_dynamic-update-slice_fusion.14
  11.8 0.9 pad_maximum_fusion.9
  12.7 1.6 %collective-permute-start.11 = (bf16[544,128]{1,0:T(8,128)(2,1)S(1)}, bf16[544,128]{1,0:T(8,128)(2,1)S(1)}, u32[]{:S(2)}, u32[]{:S(2)}) collective-permute-start(bf16[544,128]{1,0:T(8,128)(2,1)S(1)} %pad_maximum_fusion.9), channel_id=1, source_target_pairs={{0,2},{1,3},{2,0},{3,1},{4,6},{5,7},{6,4},{7,5},{8,10},{9,11},{10,... | collective-permute-start | bytes 417800 | tf_op jit(solution)/shard_map/ppermute | solution.py:32
  14.3 2.9 %collective-permute-done.5 = bf16[8,5120]{1,0:T(8,128)(2,1)S(1)} collective-permute-done((bf16[8,5120]{1,0:T(8,128)(2,1)S(1)}, bf16[8,5120]{1,0:T(8,128)(2,1)S(1)}, u32[]{:S(2)}, u32[]{:S(2)}) %collective-permute-start.5) | collective-permute-done | bytes 81952 | tf_op jit(solution)/shard_map/ppermute | solution.py:32
  17.4 0.7 collective-permute-done
  18.2 1.6 %collective-permute-start.1 = (bf16[16,5120]{1,0:T(8,128)(2,1)S(1)}, bf16[16,5120]{1,0:T(8,128)(2,1)S(1)}, u32[]{:S(2)}, u32[]{:S(2)}) collective-permute-start(bf16[16,5120]{1,0:T(8,128)(2,1)S(1)} %pad_maximum_fusion.7), channel_id=1, source_target_pairs={{0,4},{1,5},{2,6},{3,7},{4,0},{5,1},{6,2},{7,3},{8,12},{9,13},{10,... | collective-permute-start | bytes 491528 | tf_op jit(solution)/shard_map/ppermute | solution.py:32
  21.6 1.0 collective-permute-done.6
  22.6 1.6 %collective-permute-start.7 = (bf16[32,5120]{1,0:T(8,128)(2,1)S(1)}, bf16[32,5120]{1,0:T(8,128)(2,1)S(1)}, u32[]{:S(2)}, u32[]{:S(2)}) collective-permute-start(bf16[32,5120]{1,0:T(8,128)(2,1)S(1)} %pad_maximum_fusion.5), channel_id=1, source_target_pairs={{0,2},{1,3},{2,0},{3,1},{4,6},{5,7},{6,4},{7,5},{8,10},{9,11},{10,... | collective-permute-start | bytes 983048 | tf_op jit(solution)/shard_map/ppermute | solution.py:32
  24.9 1.6 %collective-permute-start.2 = (bf16[32,5120]{1,0:T(8,128)(2,1)S(1)}, bf16[32,5120]{1,0:T(8,128)(2,1)S(1)}, u32[]{:S(2)}, u32[]{:S(2)}) collective-permute-start(bf16[32,5120]{1,0:T(8,128)(2,1)S(1)} %pad_maximum_fusion.4), channel_id=1, source_target_pairs={{0,8},{1,9},{2,10},{3,11},{4,12},{5,13},{6,14},{7,15},{8,0},{9,1},... | collective-permute-start | bytes 983048 | tf_op jit(solution)/shard_map/ppermute | solution.py:32
  27.9 1.6 %collective-permute-done.12 = bf16[1088,128]{1,0:T(8,128)(2,1)S(1)} collective-permute-done((bf16[1088,128]{1,0:T(8,128)(2,1)S(1)}, bf16[1088,128]{1,0:T(8,128)(2,1)S(1)}, u32[]{:S(2)}, u32[]{:S(2)}) %collective-permute-start.12) | collective-permute-done | bytes 278560 | tf_op jit(solution)/shard_map/ppermute | solution.py:32
  29.5 1.2 %collective-permute-start.13 = (bf16[2176,128]{1,0:T(8,128)(2,1)S(1)}, bf16[2176,128]{1,0:T(8,128)(2,1)S(1)}, u32[]{:S(2)}, u32[]{:S(2)}) collective-permute-start(bf16[2176,128]{1,0:T(8,128)(2,1)S(1)} %pad_maximum_fusion.3), channel_id=1, source_target_pairs={{0,8},{1,9},{2,10},{3,11},{4,12},{5,13},{6,14},{7,15},{8,0},{9,1},... | collective-permute-start | bytes 1671176 | tf_op jit(solution)/shard_map/ppermute | solution.py:32
  30.8 2.3 %collective-permute-done.2 = bf16[32,5120]{1,0:T(8,128)(2,1)S(1)} collective-permute-done((bf16[32,5120]{1,0:T(8,128)(2,1)S(1)}, bf16[32,5120]{1,0:T(8,128)(2,1)S(1)}, u32[]{:S(2)}, u32[]{:S(2)}) %collective-permute-start.2) | collective-permute-done | bytes 327712 | tf_op jit(solution)/shard_map/ppermute | solution.py:32
  33.2 1.6 %collective-permute-start.3 = (bf16[64,5120]{1,0:T(8,128)(2,1)S(1)}, bf16[64,5120]{1,0:T(8,128)(2,1)S(1)}, u32[]{:S(2)}, u32[]{:S(2)}) collective-permute-start(bf16[64,5120]{1,0:T(8,128)(2,1)S(1)} %pad_maximum_fusion.1), channel_id=1, source_target_pairs={{0,2},{1,3},{2,0},{3,1},{4,6},{5,7},{6,4},{7,5},{8,10},{9,11},{10,... | collective-permute-start | bytes 1966088 | tf_op jit(solution)/shard_map/ppermute | solution.py:32
  34.8 3.8 %collective-permute-start.8 = (bf16[64,5120]{1,0:T(8,128)(2,1)S(1)}, bf16[64,5120]{1,0:T(8,128)(2,1)S(1)}, u32[]{:S(2)}, u32[]{:S(2)}) collective-permute-start(bf16[64,5120]{1,0:T(8,128)(2,1)S(1)} %pad_maximum_fusion.2), channel_id=1, source_target_pairs={{0,4},{1,5},{2,6},{3,7},{4,0},{5,1},{6,2},{7,3},{8,12},{9,13},{10,... | collective-permute-start | bytes 1966088 | tf_op jit(solution)/shard_map/ppermute | solution.py:32
  38.6 0.8 constant_dynamic-update-slice_fusion.6
  39.3 0.8 constant_dynamic-update-slice_fusion.1
  40.1 3.9 %collective-permute-done.13 = bf16[2176,128]{1,0:T(8,128)(2,1)S(1)} collective-permute-done((bf16[2176,128]{1,0:T(8,128)(2,1)S(1)}, bf16[2176,128]{1,0:T(8,128)(2,1)S(1)}, u32[]{:S(2)}, u32[]{:S(2)}) %collective-permute-start.13) | collective-permute-done | bytes 557088 | tf_op jit(solution)/shard_map/ppermute | solution.py:32
  44.2 3.0 %collective-permute-done.8 = bf16[64,5120]{1,0:T(8,128)(2,1)S(1)} collective-permute-done((bf16[64,5120]{1,0:T(8,128)(2,1)S(1)}, bf16[64,5120]{1,0:T(8,128)(2,1)S(1)}, u32[]{:S(2)}, u32[]{:S(2)}) %collective-permute-start.8) | collective-permute-done | bytes 655392 | tf_op jit(solution)/shard_map/ppermute | solution.py:32
  47.1 0.9 constant_dynamic-update-slice_fusion.5.own
  48.0 0.9 constant_dynamic-update-slice_fusion.own
  49.6 0.8 copy-done
  53.2 1.2 %copy-done.1 = bf16[4352,128]{1,0:T(8,128)(2,1)S(1)} copy-done((bf16[4352,128]{1,0:T(8,128)(2,1)S(1)}, bf16[4352,128]{1,0:T(8,128)(2,1)}, u32[]{:S(2)}) %copy-start.1) | copy-done | bytes 1114136
  54.5 3.4 %copy-done.2 = bf16[256,128,128]{2,1,0:T(8,128)(2,1)S(1)} copy-done((bf16[256,128,128]{2,1,0:T(8,128)(2,1)S(1)}, bf16[256,128,128]{2,1,0:T(8,128)(2,1)}, u32[]{:S(2)}) %copy-start.2) | copy-done | bytes 8388632
  57.9 17.7 %maxsim.1 = f32[32,8,128]{2,1,0:T(8,128)S(1)} custom-call(s32[512]{0:T(512)S(1)} %reshape.74.lst, s32[32]{0:T(128)S(1)} %get-tuple-element.2.cnt, s32[256]{0:T(256)S(1)} %copy-done.3, bf16[4352,128]{1,0:T(8,128)(2,1)S(1)} %constant_dynamic-update-slice_fusion.10.own.codes_own, bf16[4352,128]{1,0:T(8,128)(2,1)S(1)} %copy-done.1, ...), custom_call_target="tpu_custom_call" | custom-call | flops 4294967296 | bytes 8388608 | tf_op jit(solution)/shard_map/maxsim/pallas_call | solution.py:197
  75.6 4.0 %beam.1.so_far = f32[256,512]{1,0:T(8,128)S(1)} custom-call(bf16[128,5120]{1,0:T(8,128)(2,1)} %constant_dynamic-update-slice_fusion.5.own, bf16[128,5120]{1,0:T(8,128)(2,1)} %collective-permute-done.9.other, bf16[512,10240]{1,0:T(8,128)(2,1)S(1)} %bitcast.12), custom_call_target="tpu_custom_call" | custom-call | flops 1342177280 | bytes 7864320 | tf_op jit(solution)/shard_map/beam/pallas_call | solution.py:220
  79.6 4.4 %beam_last.1 = f32[32,8,128]{2,1,0:T(8,128)S(1)} custom-call(s32[1]{0:T(128)} %bitcast.me_ref, bf16[128,5120]{1,0:T(8,128)(2,1)} %constant_dynamic-update-slice_fusion.own, bf16[128,5120]{1,0:T(8,128)(2,1)} %collective-permute-done.4.other, bf16[512,10240]{1,0:T(8,128)(2,1)S(1)} %bitcast.12, f32[256,512]{1,0:T(8,128)S(1)} %beam.1.so_far, ...), custom_call_target="tpu_custom_call" | custom-call | flops 1342177280 | bytes 7864320 | tf_op jit(solution)/shard_map/beam_last/pallas_call | solution.py:232
  84.0 35.4 %all_to_all.5.parts = f32[32,8,128]{2,1,0:T(8,128)} all-to-all(f32[32,8,128]{2,1,0:T(8,128)S(1)} %beam_last.1), channel_id=1, replica_groups=mesh['dom'=32,'rep'=1] {'dom'}, dimensions={0} | all-to-all | bytes 262144 | tf_op jit(solution)/shard_map/all_to_all | solution.py:248
  119.4 1.6 %collect.1 = (f32[3,8,16]{2,1,0:T(8,128)}, f32[8,32]{1,0:T(8,128)}) custom-call(f32[32,8,128]{2,1,0:T(8,128)} %all_to_all.5.parts), custom_call_target="tpu_custom_call" | custom-call | tf_op jit(solution)/shard_map/collect/pallas_call | solution.py:249
  (61 shorter events, 8.0 us)
Async XLA Ops:
  2.3 18.7 %copy-start.4 = (bf16[272,128]{1,0:T(8,128)(2,1)S(1)}, bf16[272,128]{1,0:T(8,128)(2,1)}, u32[]{:S(2)}) copy-start(bf16[272,128]{1,0:T(8,128)(2,1)} %pack.1) | copy-start | bytes 208900
  2.3 9.5 %collective-permute-start.10 = (bf16[272,128]{1,0:T(8,128)(2,1)}, bf16[272,128]{1,0:T(8,128)(2,1)S(1)}, u32[]{:S(2)}, u32[]{:S(2)}) collective-permute-start(bf16[272,128]{1,0:T(8,128)(2,1)} %pack.1), channel_id=1, source_target_pairs={{0,16},{1,17},{2,18},{3,19},{4,20},{5,21},{6,22},{7,23},{8,24},{9,... | collective-permute-start | bytes 208904 | tf_op jit(solution)/shard_map/ppermute | solution.py:32
  8.0 9.2 %collective-permute-start.5 = (bf16[8,5120]{1,0:T(8,128)(2,1)S(1)}, bf16[8,5120]{1,0:T(8,128)(2,1)S(1)}, u32[]{:S(2)}, u32[]{:S(2)}) collective-permute-start(bf16[8,5120]{1,0:T(8,128)(2,1)S(1)} %get-tuple-element.5), channel_id=1, source_target_pairs={{0,16},{1,17},{2,18},{3,19},{4,20},{5,21},{6,22},{7,23},{8,24},{9,... | collective-permute-start | bytes 245768 | tf_op jit(solution)/shard_map/ppermute | solution.py:32
  8.0 10.1 %collective-permute-start = (bf16[8,5120]{1,0:T(8,128)(2,1)S(1)}, bf16[8,5120]{1,0:T(8,128)(2,1)S(1)}, u32[]{:S(2)}, u32[]{:S(2)}) collective-permute-start(bf16[8,5120]{1,0:T(8,128)(2,1)S(1)} %get-tuple-element.8), channel_id=1, source_target_pairs={{0,16},{1,17},{2,18},{3,19},{4,20},{5,21},{6,22},{7,23},{8,24},{9,... | collective-permute-start | bytes 245768 | tf_op jit(solution)/shard_map/ppermute | solution.py:32
  12.7 8.3 %collective-permute-start.11 = (bf16[544,128]{1,0:T(8,128)(2,1)S(1)}, bf16[544,128]{1,0:T(8,128)(2,1)S(1)}, u32[]{:S(2)}, u32[]{:S(2)}) collective-permute-start(bf16[544,128]{1,0:T(8,128)(2,1)S(1)} %pad_maximum_fusion.9), channel_id=1, source_target_pairs={{0,2},{1,3},{2,0},{3,1},{4,6},{5,7},{6,4},{7,5},{8,10},{9,11},{10,... | collective-permute-start | bytes 417800 | tf_op jit(solution)/shard_map/ppermute | solution.py:32
  17.2 5.4 %collective-permute-start.6 = (bf16[16,5120]{1,0:T(8,128)(2,1)S(1)}, bf16[16,5120]{1,0:T(8,128)(2,1)S(1)}, u32[]{:S(2)}, u32[]{:S(2)}) collective-permute-start(bf16[16,5120]{1,0:T(8,128)(2,1)S(1)} %pad_maximum_fusion.8), channel_id=1, source_target_pairs={{0,8},{1,9},{2,10},{3,11},{4,12},{5,13},{6,14},{7,15},{8,0},{9,1},... | collective-permute-start | bytes 491528 | tf_op jit(solution)/shard_map/ppermute | solution.py:32
  18.2 6.7 %collective-permute-start.1 = (bf16[16,5120]{1,0:T(8,128)(2,1)S(1)}, bf16[16,5120]{1,0:T(8,128)(2,1)S(1)}, u32[]{:S(2)}, u32[]{:S(2)}) collective-permute-start(bf16[16,5120]{1,0:T(8,128)(2,1)S(1)} %pad_maximum_fusion.7), channel_id=1, source_target_pairs={{0,4},{1,5},{2,6},{3,7},{4,0},{5,1},{6,2},{7,3},{8,12},{9,13},{10,... | collective-permute-start | bytes 491528 | tf_op jit(solution)/shard_map/ppermute | solution.py:32
  21.0 8.5 %collective-permute-start.12 = (bf16[1088,128]{1,0:T(8,128)(2,1)S(1)}, bf16[1088,128]{1,0:T(8,128)(2,1)S(1)}, u32[]{:S(2)}, u32[]{:S(2)}) collective-permute-start(bf16[1088,128]{1,0:T(8,128)(2,1)S(1)} %pad_maximum_fusion.6), channel_id=1, source_target_pairs={{0,4},{1,5},{2,6},{3,7},{4,0},{5,1},{6,2},{7,3},{8,12},{9,13},{10,... | collective-permute-start | bytes 835592 | tf_op jit(solution)/shard_map/ppermute | solution.py:32
  22.6 12.1 %collective-permute-start.7 = (bf16[32,5120]{1,0:T(8,128)(2,1)S(1)}, bf16[32,5120]{1,0:T(8,128)(2,1)S(1)}, u32[]{:S(2)}, u32[]{:S(2)}) collective-permute-start(bf16[32,5120]{1,0:T(8,128)(2,1)S(1)} %pad_maximum_fusion.5), channel_id=1, source_target_pairs={{0,2},{1,3},{2,0},{3,1},{4,6},{5,7},{6,4},{7,5},{8,10},{9,11},{10,... | collective-permute-start | bytes 983048 | tf_op jit(solution)/shard_map/ppermute | solution.py:32
  24.9 8.2 %collective-permute-start.2 = (bf16[32,5120]{1,0:T(8,128)(2,1)S(1)}, bf16[32,5120]{1,0:T(8,128)(2,1)S(1)}, u32[]{:S(2)}, u32[]{:S(2)}) collective-permute-start(bf16[32,5120]{1,0:T(8,128)(2,1)S(1)} %pad_maximum_fusion.4), channel_id=1, source_target_pairs={{0,8},{1,9},{2,10},{3,11},{4,12},{5,13},{6,14},{7,15},{8,0},{9,1},... | collective-permute-start | bytes 983048 | tf_op jit(solution)/shard_map/ppermute | solution.py:32
  29.5 14.5 %collective-permute-start.13 = (bf16[2176,128]{1,0:T(8,128)(2,1)S(1)}, bf16[2176,128]{1,0:T(8,128)(2,1)S(1)}, u32[]{:S(2)}, u32[]{:S(2)}) collective-permute-start(bf16[2176,128]{1,0:T(8,128)(2,1)S(1)} %pad_maximum_fusion.3), channel_id=1, source_target_pairs={{0,8},{1,9},{2,10},{3,11},{4,12},{5,13},{6,14},{7,15},{8,0},{9,1},... | collective-permute-start | bytes 1671176 | tf_op jit(solution)/shard_map/ppermute | solution.py:32
  33.2 14.9 %collective-permute-start.3 = (bf16[64,5120]{1,0:T(8,128)(2,1)S(1)}, bf16[64,5120]{1,0:T(8,128)(2,1)S(1)}, u32[]{:S(2)}, u32[]{:S(2)}) collective-permute-start(bf16[64,5120]{1,0:T(8,128)(2,1)S(1)} %pad_maximum_fusion.1), channel_id=1, source_target_pairs={{0,2},{1,3},{2,0},{3,1},{4,6},{5,7},{6,4},{7,5},{8,10},{9,11},{10,... | collective-permute-start | bytes 1966088 | tf_op jit(solution)/shard_map/ppermute | solution.py:32
  34.8 12.4 %collective-permute-start.8 = (bf16[64,5120]{1,0:T(8,128)(2,1)S(1)}, bf16[64,5120]{1,0:T(8,128)(2,1)S(1)}, u32[]{:S(2)}, u32[]{:S(2)}) collective-permute-start(bf16[64,5120]{1,0:T(8,128)(2,1)S(1)} %pad_maximum_fusion.2), channel_id=1, source_target_pairs={{0,4},{1,5},{2,6},{3,7},{4,0},{5,1},{6,2},{7,3},{8,12},{9,13},{10,... | collective-permute-start | bytes 1966088 | tf_op jit(solution)/shard_map/ppermute | solution.py:32
  44.1 5.3 %collective-permute-start.14 = (bf16[4352,128]{1,0:T(8,128)(2,1)S(1)}, bf16[4352,128]{1,0:T(8,128)(2,1)S(1)}, u32[]{:S(2)}, u32[]{:S(2)}) collective-permute-start(bf16[4352,128]{1,0:T(8,128)(2,1)S(1)} %constant_dynamic-update-slice_fusion.10.own.codes_own), channel_id=1, source_target_pairs={{0,1},{1,0},{2,3},{3,2},{4,5},{5,4},{6,7},{7,6},{8,9},{9,8},{10,11... | collective-permute-start | bytes 3342344 | tf_op jit(solution)/shard_map/ppermute | solution.py:32
  48.0 27.6 %collective-permute-start.9 = (bf16[128,5120]{1,0:T(8,128)(2,1)}, bf16[128,5120]{1,0:T(8,128)(2,1)}, u32[]{:S(2)}, u32[]{:S(2)}) collective-permute-start(bf16[128,5120]{1,0:T(8,128)(2,1)} %constant_dynamic-update-slice_fusion.5.own), channel_id=1, source_target_pairs={{0,1},{1,0},{2,3},{3,2},{4,5},{5,4},{6,7},{7,6},{8,9},{9,8},{10,11... | collective-permute-start | bytes 3932168 | tf_op jit(solution)/shard_map/ppermute | solution.py:32
  48.9 30.7 %collective-permute-start.4 = (bf16[128,5120]{1,0:T(8,128)(2,1)}, bf16[128,5120]{1,0:T(8,128)(2,1)}, u32[]{:S(2)}, u32[]{:S(2)}) collective-permute-start(bf16[128,5120]{1,0:T(8,128)(2,1)} %constant_dynamic-update-slice_fusion.own), channel_id=1, source_target_pairs={{0,1},{1,0},{2,3},{3,2},{4,5},{5,4},{6,7},{7,6},{8,9},{9,8},{10,11... | collective-permute-start | bytes 3932168 | tf_op jit(solution)/shard_map/ppermute | solution.py:32
  49.4 1.0 copy-start
  49.4 26.2 %slice-start = ((s8[10485760]{0:T(1024)(128)(4,1)}), s8[2097152]{0:T(1024)(128)(4,1)S(1)}, s32[]{:S(2)}) async-start(s8[10485760]{0:T(1024)(128)(4,1)} %bitcast.11), calls=%async_computation.1 | async-start | bytes 4194304
  50.5 2.8 %copy-start.3 = (s32[256]{0:T(256)S(1)}, s32[256]{0:T(256)}, u32[]{:S(2)}) copy-start(s32[256]{0:T(256)} %lens.1) | copy-start | bytes 3076
  53.2 1.3 %copy-start.1 = (bf16[4352,128]{1,0:T(8,128)(2,1)S(1)}, bf16[4352,128]{1,0:T(8,128)(2,1)}, u32[]{:S(2)}) copy-start(bf16[4352,128]{1,0:T(8,128)(2,1)} %copy-done) | copy-start | bytes 3342340
  54.5 3.4 %copy-start.2 = (bf16[256,128,128]{2,1,0:T(8,128)(2,1)S(1)}, bf16[256,128,128]{2,1,0:T(8,128)(2,1)}, u32[]{:S(2)}) copy-start(bf16[256,128,128]{2,1,0:T(8,128)(2,1)} %tiles.1) | copy-start | bytes 25165828
  57.9 17.7 %slice-start.1 = ((s8[10485760]{0:T(1024)(128)(4,1)}), s8[4194304]{0:T(1024)(128)(4,1)S(1)}, s32[]{:S(2)}) async-start(s8[10485760]{0:T(1024)(128)(4,1)} %bitcast.11), calls=%async_computation.2 | async-start | bytes 8388608
  57.9 17.7 %slice-start.2 = ((s8[10485760]{0:T(1024)(128)(4,1)}), s8[4194304]{0:T(1024)(128)(4,1)S(1)}, s32[]{:S(2)}) async-start(s8[10485760]{0:T(1024)(128)(4,1)} %bitcast.11), calls=%async_computation.3 | async-start | bytes 8388608

commit v2 on v1

--- a/solution.py
+++ b/solution.py
@@ -10,7 +10,6 @@
 
 masked_value = -1e30
 LANES = 128
-GROUP = 4
 VMEM = pl.BlockSpec(memory_space=pltpu.VMEM)
 NT = (((1,), (1,)), ((), ()))
 
@@ -43,56 +42,94 @@
     )
 
 
-def prep_kernel(parts, fo, fs, co, cs, tok, out):
-    rounds, _, front = fo.shape
-    rows = tok.shape[0]
-    cand_at = rounds * front
-    first = place(co[...] * parts, cand_at)
-    second = place(cs[...], cand_at)
+def ids(shape, axis):
+    return lax.broadcasted_iota(jnp.int32, shape, axis)
+
+
+def exact(values):
+    return values.astype(jnp.float32).astype(jnp.bfloat16)
+
+
+def pick(a, b):
+    return jnp.dot(exact(a), exact(b), preferred_element_type=jnp.float32)
+
+
+def prep_kernel(parts, slots, cap, fo, fs, co, cs, tok, out):
+    rounds, queries, front = fo.shape
+    rows, cands = tok.shape[0], co.shape[1]
+    pairs = queries * cands
+    low_at = rounds * front
+    codes = jnp.zeros((queries, LANES), jnp.float32)
     for r in range(rounds):
-        first = first + place(fo[r] * parts + (fs[r] >> 8), r * front)
-        second = second + place(fs[r] & 255, r * front)
+        codes = codes + place(fo[r] * parts + (fs[r] >> 8), r * front)
+        codes = codes + place(fs[r] & 255, low_at + r * front)
+
+    across = (ids((cands, pairs), 1) % cands == ids((cands, pairs), 0))
+    mine = ids((queries, pairs), 1) // cands == ids((queries, pairs), 0)
+    line = lambda v: jnp.sum(jnp.where(mine, pick(v, across), 0.0), axis=0, keepdims=True)
+    owner_line, slot_line = line(co[...]), line(cs[...])
+    down = ids((pairs, queries), 0) // cands == ids((pairs, queries), 1)
+    here = ids((pairs, cands), 0) % cands == ids((pairs, cands), 1)
+    owner = jnp.sum(jnp.where(here, pick(down, co[...]), 0.0), axis=1, keepdims=True)
+    earlier = (owner == owner_line) & (ids((pairs, pairs), 1) < ids((pairs, pairs), 0))
+    position = jnp.sum(jnp.where(earlier, 1.0, 0.0), axis=1, keepdims=True)
+    target = (owner * cap + position).astype(jnp.int32)
+    number = (ids((1, pairs), 1) + 1).astype(jnp.float32)
+    table = jnp.zeros((8, LANES), jnp.float32)
+    for g in range(slots // LANES):
+        row = ids((8, pairs), 0)
+        values = jnp.where(row == 2 * g, number, jnp.where(row == 2 * g + 1, slot_line, 0.0))
+        table = table + pick(values, target == ids((pairs, LANES), 1) + g * LANES)
     out[:rows, :] = tok[...]
-    out[rows:, :] = jnp.concatenate([first, second], axis=0).astype(jnp.bfloat16)
-
-
-def maxsim_kernel(cand_at, cands, stride, lst, cnt, lens, own, other, tiles, out):
+    out[rows:, :] = jnp.concatenate([codes, table], axis=0).astype(jnp.bfloat16)
+
+
+def maxsim_kernel(cand_at, cands, cap, me_ref, lens, own, other, tiles, out, listed, lst, sem):
+    blocks = out.shape[0] // 2
+    stride = own.shape[0] // blocks
+    pt = tiles.shape[1]
     qt = (stride - 16) // 8
-    blocks = own.shape[0] // stride
-    pt = tiles.shape[1]
-    cap = lst.shape[0] // (2 * blocks)
-    width = stride - 16
-    token = lax.broadcasted_iota(jnp.int32, (pt, width), 0)
-    column = lax.broadcasted_iota(jnp.int32, (1, width), 1) // qt
-    row = lax.broadcasted_iota(jnp.int32, (8, LANES), 0)
-    lane = lax.broadcasted_iota(jnp.int32, (8, LANES), 1)
+    start = me_ref[0] * cap
+    row, lane = ids((8, LANES), 0), ids((8, LANES), 1)
+    group = start // LANES
     for side, ref in enumerate((own, other)):
-
-        def source(b, carry, side=side, ref=ref):
+        for b in range(blocks):
+            table = ref[(b + 1) * stride - 16 : (b + 1) * stride, :].astype(jnp.float32)[8:]
+            weight = jnp.where(row == 2 * group, 256.0, jnp.where(row == 2 * group + 1, 1.0, 0.0))
             at = side * blocks + b
-            weights = ref[pl.ds(pl.multiple_of(b * stride, 16), width), :]
-            held = cnt[at]
-
-            def group(g, acc):
-                entries = [lst[at * cap + g * GROUP + j] for j in range(GROUP)]
-                slots = [e & 255 for e in entries]
-                data = jnp.concatenate([tiles[s] for s in slots], axis=0)
-                sim = lax.dot_general(data, weights, NT, preferred_element_type=jnp.float32)
-                for j in range(GROUP):
-                    pair = entries[j] >> 8
-                    query, cand = pair // cands, pair % cands
-                    part = sim[j * pt : (j + 1) * pt, :]
-                    part = jnp.where(token < lens[slots[j]], part, masked_value)
-                    top = jnp.max(part, axis=0, keepdims=True)
-                    score = jnp.sum(jnp.where(column == query, top, 0.0), axis=1, keepdims=True) * (1.0 / qt)
-                    there = jnp.where(g * GROUP + j < held, cand_at + cand, -1)
-                    acc = acc + jnp.where((row == query) & (lane == there), score, 0.0)
-                return acc
-
-            out[at] = lax.fori_loop(0, (held + GROUP - 1) // GROUP, group, jnp.zeros((8, LANES), jnp.float32))
-            return carry
-
-        lax.fori_loop(0, blocks, source, 0)
+            listed[at : at + 1, :] = jnp.sum(table * weight, axis=0, keepdims=True).astype(jnp.int32)
+    listed[...] = pltpu.roll(listed[...], lax.rem(LANES - start % LANES, LANES), axis=1)
+    copy = pltpu.make_async_copy(listed, lst, sem)
+    copy.start()
+    copy.wait()
+
+    spot = jnp.where((lane >= cand_at) & (lane < cand_at + cands), row * cands + lane - cand_at, -1)
+    token = ids((pt, qt), 0)
+
+    def score(ref, b, at):
+        tops, pairs = [], []
+        for k in range(cap):
+            entry = lst[at, k]
+            slot, pair = entry & 255, (entry >> 8) - 1
+            query = jnp.maximum(pair, 0) // cands
+            tokens = ref[pl.ds(pl.multiple_of(b * stride + query * qt, 16), qt), :]
+            sim = lax.dot_general(tiles[slot], tokens, NT, preferred_element_type=jnp.float32)
+            sim = jnp.where(token < lens[slot], sim, masked_value)
+            tops.append(jnp.max(sim, axis=0, keepdims=True))
+            pairs.append(jnp.where(pair < 0, -2, pair))
+        means = jnp.sum(jnp.concatenate(tops, axis=0), axis=1, keepdims=True) * (1.0 / qt)
+        acc = jnp.zeros((8, LANES), jnp.float32)
+        for k in range(cap):
+            acc = acc + jnp.where(spot == pairs[k], means[k : k + 1, :], 0.0)
+        out[at] = acc
+
+    def step(i, carry):
+        for u in range(2):
+            score(own, 2 * i + u, 2 * i + u)
+            score(other, 2 * i + u, blocks + 2 * i + u)
+        return carry
+
+    lax.fori_loop(0, blocks // 2, step, 0)
 
 
 def beam_kernel(own, other, doc, total):
@@ -129,8 +166,10 @@
         for side, ref in enumerate((codes_own, codes_other)):
             for p in range(blocks):
                 t = code_order.index(order[p])
-                codes = ref[t * stride + stride - 16 : (t + 1) * stride, :].astype(jnp.float32).astype(jnp.int32)
-                owner, high, low = codes[:8] // parts, codes[:8] % parts, codes[8:]
+                codes = ref[(t + 1) * stride - 16 : (t + 1) * stride, :].astype(jnp.float32)[:8]
+                low = pltpu.roll(codes, LANES - cand_at, axis=1).astype(jnp.int32)
+                codes = codes.astype(jnp.int32)
+                owner, high = codes // parts, codes % parts
                 slot = high * 256 + low
                 within, page = slot % LANES, slot // LANES
                 rows = total[side * half + p * 8 : side * half + p * 8 + 8, :]
@@ -159,21 +198,24 @@
     parts = nodes // 256
     cand_at = rounds * front
     assert n & (n - 1) == 0 and queries == 8 and dim == LANES and nodes % 256 == 0
-    assert cand_at + cands <= LANES and n * parts <= 256 and passage_tiles.shape[0] <= 256
+    assert cand_at + max(cand_at, cands) <= LANES and n * parts <= 256 and passage_tiles.shape[0] <= 256
     me = lax.axis_index("dom").astype(jnp.int32)
     stride = queries * qt + 16
     blocks = n // 2
     orders = orders_of(n)
     masks = [sources_of(o) for o in orders]
 
+    pairs_count = queries * cands
+    cap = max(2, min(pairs_count, 2 * pairs_count // n))
+    slots = n * cap
+    assert slots % LANES == 0 and slots <= 4 * LANES and LANES % cap == 0 and pairs_count <= 256
     packed = pl.pallas_call(
-        functools.partial(prep_kernel, parts),
+        functools.partial(prep_kernel, parts, slots, cap),
         out_shape=jax.ShapeDtypeStruct((stride, dim), jnp.bfloat16),
         in_specs=[VMEM] * 5,
         out_specs=VMEM,
         name="pack",
     )(frontier_owner, frontier_slot, cand_owner.reshape(queries, cands), cand_slot, query_tokens.reshape(queries * qt, dim))
-
     half = fde // 2
     chunks = [packed, query_fde[:, :half], query_fde[:, half:]]
     for step in range(len(orders[0])):
@@ -182,30 +224,23 @@
     pairs = [(c, exchange(c, 1, n)) for c in chunks]
     (tok_own, tok_other), (a_own, a_other), (b_own, b_other) = pairs
 
-    codes = jnp.stack(pairs[0]).reshape(n, stride, dim)[:, queries * qt :, cand_at : cand_at + cands]
-    codes = codes.astype(jnp.int32)
-    mine = (codes[:, :queries] // parts == me).reshape(n, queries * cands)
-    slots = codes[:, queries:].reshape(n, queries * cands)
-    cap = max(2, min(queries * cands, 2 * queries * cands // n))
-    position = jnp.cumsum(mine.astype(jnp.int32), axis=1) - 1
-    payload = jnp.arange(queries * cands, dtype=jnp.int32)[None] * 256 + slots
-    chosen = mine[:, None, :] & (position[:, None, :] == jnp.arange(cap, dtype=jnp.int32)[None, :, None])
-    entries = jnp.sum(jnp.where(chosen, payload[:, None, :], 0), axis=2)
-    counts = jnp.sum(mine.astype(jnp.int32), axis=1)
-
-    pairs_bound = n * cap
+    pt = passage_tiles.shape[1]
     maxsim = pl.pallas_call(
-        functools.partial(maxsim_kernel, cand_at, cands, stride),
+        functools.partial(maxsim_kernel, cand_at, cands, cap),
         out_shape=jax.ShapeDtypeStruct((n, 8, LANES), jnp.float32),
         grid_spec=pltpu.PrefetchScalarGridSpec(
-            num_scalar_prefetch=3, grid=(), in_specs=[VMEM] * 3, out_specs=VMEM
+            num_scalar_prefetch=2,
+            grid=(),
+            in_specs=[VMEM] * 3,
+            out_specs=VMEM,
+            scratch_shapes=[pltpu.VMEM((n, LANES), jnp.int32), pltpu.SMEM((n, LANES), jnp.int32), pltpu.SemaphoreType.DMA],
         ),
-        compiler_params=pltpu.CompilerParams(vmem_limit_bytes=24 << 20),
+        compiler_params=pltpu.CompilerParams(vmem_limit_bytes=16 << 20),
         cost_estimate=pl.CostEstimate(
-            flops=2 * pairs_bound * 128 * 256 * 128, bytes_accessed=8 << 20, transcendentals=0
+            flops=16 * slots * pt * qt * dim, bytes_accessed=8 << 20, transcendentals=0
         ),
         name="maxsim",
-    )(entries.reshape(-1), counts, passage_len, tok_own, tok_other, passage_tiles)
+    )(me.reshape(1), passage_len, tok_own, tok_other, passage_tiles)
 
     block = math.gcd(half, 1280)
     steps = half // block

time: 122 us -> 89.8 us (0.74)
  blocking collectives: 35.4 us -> 13.9 us
  Pallas kernels: 29.3 us -> 23.9 us
  waiting for transfers between devices: 16.2 us -> 21.2 us
  local copies, waits for them, and re-layouts: 14.6 us -> 10.9 us
  starting transfers between devices: 21.2 us -> 17.5 us
  other arithmetic: 3.45 us -> 1.1 us
    all_to_all x1, blocking collectives: 35.4 us -> 13.9 us  [local(): lax.all_to_all(scored, 'dom', split_axis=0, concat_axis=0, tiled=True)]
    pallas_call x2, Pallas kernels: 19.4 us -> 13 us  [the longest x1 11 us: local(): pl.pallas_call(functools.partial(maxsim_kernel, cand_at, cands, cap), out...]
    ppermute x15, waiting for transfers between devices: 16.2 us -> 21.2 us  [exchange(): return lax.ppermute(x, 'dom', [(i, i ^ bit) for i in range(n)])]
    ppermute x15, starting transfers between devices: 21.2 us -> 17.5 us  [exchange(): return lax.ppermute(x, 'dom', [(i, i ^ bit) for i in range(n)])]
    unnamed x26, local copies, waits for them, and re-layouts: 10.6 us -> 8.14 us
    reduce_sum x2 -> x0, other arithmetic: 1.29 us -> none  [the longest x1 0.67 us: local(): counts = jnp.sum(mine.astype(jnp.int32), axis=1)]
  transfers between devices with their start and end apart: 15 -> 15, of which waited for: 8 -> 8; matrix products, arithmetic and copies ran while one was open for 10% -> 7% of each run, Pallas kernels for 18% -> 19%
where the time goes in v2:
time: 89.8 us; the launch traced here: 89.3 us
  Pallas kernels  23.9 us (27%)
  waiting for transfers between devices  21.2 us (24%)
  starting transfers between devices  17.5 us (19%)
  blocking collectives  13.9 us (15%)
  local copies, waits for them, and re-layouts  10.9 us (12%)
  other arithmetic  1.1 us (1%)
    ppermute x15, waiting for transfers between devices, exchange(): return lax.ppermute(x, 'dom', [(i, i ^ bit) for i in range(n)])  21.2 us
    ppermute x15, starting transfers between devices, exchange(): return lax.ppermute(x, 'dom', [(i, i ^ bit) for i in range(n)])  17.5 us
    all_to_all x1, blocking collectives, local(): lax.all_to_all(scored, 'dom', split_axis=0, concat_axis=0, tiled=True)  13.9 us
    pallas_call x1, Pallas kernels, local(): pl.pallas_call(functools.partial(maxsim_kernel, cand_at, cands, cap), out...  11 us
    unnamed x26, local copies, waits for them, and re-layouts  8.14 us
    pallas_call x1, Pallas kernels, local(): pl.pallas_call(functools.partial(last_kernel, cfg), out_shape=jax.ShapeDt...  5.37 us
    pallas_call x1, Pallas kernels, local(): pl.pallas_call(beam_kernel, out_shape=jax.ShapeDtypeStruct((rows, nodes),...  3.83 us
    pallas_call x1, Pallas kernels, local(): pl.pallas_call(functools.partial(prep_kernel, parts, slots, cap), out_sha...  2.02 us
  transfers between devices with their start and end apart: 15, of which 8 were waited for; matrix products, arithmetic and copies ran while one was open for 7% of the time, Pallas kernels for 19%

profile of v2, /device:TPU:0, one launch (start us, length us, event | category | flops | bytes accessed | tf_op | source)
XLA Modules:
  0.0 89.3 jit_solution(2318024423368801029)
XLA Ops:
  0.6 1.0 %fusion = (bf16[8,5120]{1,0:T(8,128)(2,1)S(1)}, bf16[128,5120]{1,0:T(8,128)(2,1)S(1)}, bf16[128,5120]{1,0:T(8,128)(2,1)S(1)}, bf16[8,5120]{1,0:T(8,128)(2,1)S(1)}) fusion(bf16[8,10240]{1,0:T(8,128)(2,1)} %param.9), kind=kLoop, calls=%fused_computation.24 | loop fusion | bytes 491520 | tf_op jit(solution)/shard_map/slice | solution.py:220
  1.6 4.1 %collective-permute-start = (bf16[8,5120]{1,0:T(8,128)(2,1)S(1)}, bf16[8,5120]{1,0:T(8,128)(2,1)S(1)}, u32[]{:S(2)}, u32[]{:S(2)}) collective-permute-start(bf16[8,5120]{1,0:T(8,128)(2,1)S(1)} %get-tuple-element.5), channel_id=1, source_target_pairs={{0,16},{1,17},{2,18},{3,19},{4,20},{5,21},{6,22},{7,23},{8,24},{9,... | collective-permute-start | bytes 245768 | tf_op jit(solution)/shard_map/ppermute | solution.py:31
  5.8 2.0 %pack.1 = bf16[272,128]{1,0:T(8,128)(2,1)} custom-call(s32[3,8,16]{2,1,0:T(8,128)} %fo.1, s32[3,8,16]{2,1,0:T(8,128)} %fs.1, s32[8,32]{1,0:T(8,128)} %bitcast.6, s32[8,32]{1,0:T(8,128)} %cs.1, bf16[256,128]{1,0:T(8,128)(2,1)} %bitcast.5), custom_call_target="tpu_custom_call" | custom-call | tf_op jit(solution)/shard_map/pack/pallas_call | solution.py:212
  7.8 2.8 %collective-permute-start.10 = (bf16[272,128]{1,0:T(8,128)(2,1)}, bf16[272,128]{1,0:T(8,128)(2,1)S(1)}, u32[]{:S(2)}, u32[]{:S(2)}) collective-permute-start(bf16[272,128]{1,0:T(8,128)(2,1)} %pack.1), channel_id=1, source_target_pairs={{0,16},{1,17},{2,18},{3,19},{4,20},{5,21},{6,22},{7,23},{8,24},{9,... | collective-permute-start | bytes 208904 | tf_op jit(solution)/shard_map/ppermute | solution.py:31
  10.6 1.5 %constant_dynamic-update-slice_fusion.14 = bf16[4352,128]{1,0:T(8,128)(2,1)} fusion(bf16[272,128]{1,0:T(8,128)(2,1)} %pack.1), kind=kLoop, calls=%fused_computation.23 | loop fusion | bytes 139264
  12.2 4.2 %collective-permute-done.10 = bf16[272,128]{1,0:T(8,128)(2,1)S(1)} collective-permute-done((bf16[272,128]{1,0:T(8,128)(2,1)}, bf16[272,128]{1,0:T(8,128)(2,1)S(1)}, u32[]{:S(2)}, u32[]{:S(2)}) %collective-permute-start.10) | collective-permute-done | bytes 69664 | tf_op jit(solution)/shard_map/ppermute | solution.py:31
  16.4 0.9 pad_maximum_fusion.8
  17.3 1.7 %collective-permute-start.11 = (bf16[544,128]{1,0:T(8,128)(2,1)S(1)}, bf16[544,128]{1,0:T(8,128)(2,1)S(1)}, u32[]{:S(2)}, u32[]{:S(2)}) collective-permute-start(bf16[544,128]{1,0:T(8,128)(2,1)S(1)} %pad_maximum_fusion.8), channel_id=1, source_target_pairs={{0,2},{1,3},{2,0},{3,1},{4,6},{5,7},{6,4},{7,5},{8,10},{9,11},{10,... | collective-permute-start | bytes 417800 | tf_op jit(solution)/shard_map/ppermute | solution.py:31
  19.0 0.7 constant_dynamic-update-slice_fusion.13
  19.7 1.6 %collective-permute-start.1 = (bf16[16,5120]{1,0:T(8,128)(2,1)S(1)}, bf16[16,5120]{1,0:T(8,128)(2,1)S(1)}, u32[]{:S(2)}, u32[]{:S(2)}) collective-permute-start(bf16[16,5120]{1,0:T(8,128)(2,1)S(1)} %pad_maximum_fusion.6), channel_id=1, source_target_pairs={{0,4},{1,5},{2,6},{3,7},{4,0},{5,1},{6,2},{7,3},{8,12},{9,13},{10,... | collective-permute-start | bytes 491528 | tf_op jit(solution)/shard_map/ppermute | solution.py:31
  21.3 0.7 collective-permute-start.6
  22.0 0.6 collective-permute-done.11
  22.7 1.5 %collective-permute-start.12 = (bf16[1088,128]{1,0:T(8,128)(2,1)S(1)}, bf16[1088,128]{1,0:T(8,128)(2,1)S(1)}, u32[]{:S(2)}, u32[]{:S(2)}) collective-permute-start(bf16[1088,128]{1,0:T(8,128)(2,1)S(1)} %pad_maximum_fusion.5), channel_id=1, source_target_pairs={{0,4},{1,5},{2,6},{3,7},{4,0},{5,1},{6,2},{7,3},{8,12},{9,13},{10,... | collective-permute-start | bytes 835592 | tf_op jit(solution)/shard_map/ppermute | solution.py:31
  24.2 0.7 constant_dynamic-update-slice_fusion.12
  24.9 1.1 %collective-permute-done.1 = bf16[16,5120]{1,0:T(8,128)(2,1)S(1)} collective-permute-done((bf16[16,5120]{1,0:T(8,128)(2,1)S(1)}, bf16[16,5120]{1,0:T(8,128)(2,1)S(1)}, u32[]{:S(2)}, u32[]{:S(2)}) %collective-permute-start.1) | collective-permute-done | bytes 163872 | tf_op jit(solution)/shard_map/ppermute | solution.py:31
  26.0 0.9 %collective-permute-start.2 = (bf16[32,5120]{1,0:T(8,128)(2,1)S(1)}, bf16[32,5120]{1,0:T(8,128)(2,1)S(1)}, u32[]{:S(2)}, u32[]{:S(2)}) collective-permute-start(bf16[32,5120]{1,0:T(8,128)(2,1)S(1)} %pad_maximum_fusion.3), channel_id=1, source_target_pairs={{0,8},{1,9},{2,10},{3,11},{4,12},{5,13},{6,14},{7,15},{8,0},{9,1},... | collective-permute-start | bytes 983048 | tf_op jit(solution)/shard_map/ppermute | solution.py:31
  27.8 3.3 %collective-permute-done.12 = bf16[1088,128]{1,0:T(8,128)(2,1)S(1)} collective-permute-done((bf16[1088,128]{1,0:T(8,128)(2,1)S(1)}, bf16[1088,128]{1,0:T(8,128)(2,1)S(1)}, u32[]{:S(2)}, u32[]{:S(2)}) %collective-permute-start.12) | collective-permute-done | bytes 278560 | tf_op jit(solution)/shard_map/ppermute | solution.py:31
  31.1 1.2 %collective-permute-start.13 = (bf16[2176,128]{1,0:T(8,128)(2,1)S(1)}, bf16[2176,128]{1,0:T(8,128)(2,1)S(1)}, u32[]{:S(2)}, u32[]{:S(2)}) collective-permute-start(bf16[2176,128]{1,0:T(8,128)(2,1)S(1)} %pad_maximum_fusion.2), channel_id=1, source_target_pairs={{0,8},{1,9},{2,10},{3,11},{4,12},{5,13},{6,14},{7,15},{8,0},{9,1},... | collective-permute-start | bytes 1671176 | tf_op jit(solution)/shard_map/ppermute | solution.py:31
  32.3 0.7 constant_dynamic-update-slice_fusion.11
  33.1 1.7 %collective-permute-done.2 = bf16[32,5120]{1,0:T(8,128)(2,1)S(1)} collective-permute-done((bf16[32,5120]{1,0:T(8,128)(2,1)S(1)}, bf16[32,5120]{1,0:T(8,128)(2,1)S(1)}, u32[]{:S(2)}, u32[]{:S(2)}) %collective-permute-start.2) | collective-permute-done | bytes 327712 | tf_op jit(solution)/shard_map/ppermute | solution.py:31
  34.8 1.7 %collective-permute-start.3 = (bf16[64,5120]{1,0:T(8,128)(2,1)S(1)}, bf16[64,5120]{1,0:T(8,128)(2,1)S(1)}, u32[]{:S(2)}, u32[]{:S(2)}) collective-permute-start(bf16[64,5120]{1,0:T(8,128)(2,1)S(1)} %pad_maximum_fusion), channel_id=1, source_target_pairs={{0,2},{1,3},{2,0},{3,1},{4,6},{5,7},{6,4},{7,5},{8,10},{9,11},{10,... | collective-permute-start | bytes 1966088 | tf_op jit(solution)/shard_map/ppermute | solution.py:31
  36.8 1.0 %copy-done = bf16[128,5120]{1,0:T(8,128)(2,1)} copy-done((bf16[128,5120]{1,0:T(8,128)(2,1)}, bf16[128,5120]{1,0:T(8,128)(2,1)S(1)}, u32[]{:S(2)}) %copy-start) | copy-done | bytes 1310744
  37.8 7.8 %collective-permute-done.13 = bf16[2176,128]{1,0:T(8,128)(2,1)S(1)} collective-permute-done((bf16[2176,128]{1,0:T(8,128)(2,1)S(1)}, bf16[2176,128]{1,0:T(8,128)(2,1)S(1)}, u32[]{:S(2)}, u32[]{:S(2)}) %collective-permute-start.13) | collective-permute-done | bytes 557088 | tf_op jit(solution)/shard_map/ppermute | solution.py:31
  45.6 0.9 constant_dynamic-update-slice_fusion.10.own.codes_own
  46.5 2.0 %collective-permute-done.8 = bf16[64,5120]{1,0:T(8,128)(2,1)S(1)} collective-permute-done((bf16[64,5120]{1,0:T(8,128)(2,1)S(1)}, bf16[64,5120]{1,0:T(8,128)(2,1)S(1)}, u32[]{:S(2)}, u32[]{:S(2)}) %collective-permute-start.8) | collective-permute-done | bytes 655392 | tf_op jit(solution)/shard_map/ppermute | solution.py:31
  48.5 0.9 constant_dynamic-update-slice_fusion.5.own
  50.1 3.4 %copy-done.2 = bf16[256,128,128]{2,1,0:T(8,128)(2,1)S(1)} copy-done((bf16[256,128,128]{2,1,0:T(8,128)(2,1)S(1)}, bf16[256,128,128]{2,1,0:T(8,128)(2,1)}, u32[]{:S(2)}) %copy-start.2) | copy-done | bytes 8388632
  53.5 11.0 %maxsim.1 = f32[32,8,128]{2,1,0:T(8,128)S(1)} custom-call(s32[1]{0:T(128)} %bitcast.me_ref, s32[256]{0:T(256)S(1)} %copy-done.3, bf16[4352,128]{1,0:T(8,128)(2,1)} %constant_dynamic-update-slice_fusion.10.own.codes_own, bf16[4352,128]{1,0:T(8,128)(2,1)} %collective-permute-done.14.other.codes_other, bf16[256,128,128]{2,1,0:T(8,128)(2,1)S(1)} %copy-done.2), custom_call_target="tpu_custom_call" | custom-call | flops 4294967296 | bytes 8388608 | tf_op jit(solution)/shard_map/maxsim/pallas_call | solution.py:228
  64.6 3.8 %beam.1.so_far = f32[256,512]{1,0:T(8,128)S(1)} custom-call(bf16[128,5120]{1,0:T(8,128)(2,1)S(1)} %copy-done.1, bf16[128,5120]{1,0:T(8,128)(2,1)} %collective-permute-done.9.other, bf16[512,10240]{1,0:T(8,128)(2,1)S(1)} %bitcast.4), custom_call_target="tpu_custom_call" | custom-call | flops 1342177280 | bytes 7864320 | tf_op jit(solution)/shard_map/beam/pallas_call | solution.py:255
  68.4 5.4 %beam_last.1 = f32[32,8,128]{2,1,0:T(8,128)S(1)} custom-call(s32[1]{0:T(128)} %bitcast.me_ref, bf16[128,5120]{1,0:T(8,128)(2,1)S(1)} %constant_dynamic-update-slice_fusion.own, bf16[128,5120]{1,0:T(8,128)(2,1)} %collective-permute-done.4.other, bf16[512,10240]{1,0:T(8,128)(2,1)S(1)} %bitcast.4, f32[256,512]{1,0:T(8,128)S(1)} %beam.1.so_far, ...), custom_call_target="tpu_custom_call" | custom-call | flops 1342177280 | bytes 7864320 | tf_op jit(solution)/shard_map/beam_last/pallas_call | solution.py:267
  73.8 13.9 %all_to_all.5.parts = f32[32,8,128]{2,1,0:T(8,128)} all-to-all(f32[32,8,128]{2,1,0:T(8,128)S(1)} %beam_last.1), channel_id=1, replica_groups=mesh['dom'=32,'rep'=1] {'dom'}, dimensions={0} | all-to-all | bytes 262144 | tf_op jit(solution)/shard_map/all_to_all | solution.py:283
  87.7 1.6 %collect.1 = (f32[3,8,16]{2,1,0:T(8,128)}, f32[8,32]{1,0:T(8,128)}) custom-call(f32[32,8,128]{2,1,0:T(8,128)} %all_to_all.5.parts), custom_call_target="tpu_custom_call" | custom-call | tf_op jit(solution)/shard_map/collect/pallas_call | solution.py:284
  (44 shorter events, 2.0 us)
Async XLA Ops:
  1.6 18.1 %collective-permute-start = (bf16[8,5120]{1,0:T(8,128)(2,1)S(1)}, bf16[8,5120]{1,0:T(8,128)(2,1)S(1)}, u32[]{:S(2)}, u32[]{:S(2)}) collective-permute-start(bf16[8,5120]{1,0:T(8,128)(2,1)S(1)} %get-tuple-element.5), channel_id=1, source_target_pairs={{0,16},{1,17},{2,18},{3,19},{4,20},{5,21},{6,22},{7,23},{8,24},{9,... | collective-permute-start | bytes 245768 | tf_op jit(solution)/shard_map/ppermute | solution.py:31
  5.7 15.6 %collective-permute-start.5 = (bf16[8,5120]{1,0:T(8,128)(2,1)S(1)}, bf16[8,5120]{1,0:T(8,128)(2,1)S(1)}, u32[]{:S(2)}, u32[]{:S(2)}) collective-permute-start(bf16[8,5120]{1,0:T(8,128)(2,1)S(1)} %get-tuple-element.2), channel_id=1, source_target_pairs={{0,16},{1,17},{2,18},{3,19},{4,20},{5,21},{6,22},{7,23},{8,24},{9,... | collective-permute-start | bytes 245768 | tf_op jit(solution)/shard_map/ppermute | solution.py:31
  7.8 14.9 %copy-start.4 = (bf16[272,128]{1,0:T(8,128)(2,1)S(1)}, bf16[272,128]{1,0:T(8,128)(2,1)}, u32[]{:S(2)}) copy-start(bf16[272,128]{1,0:T(8,128)(2,1)} %pack.1) | copy-start | bytes 208900
  7.8 8.6 %collective-permute-start.10 = (bf16[272,128]{1,0:T(8,128)(2,1)}, bf16[272,128]{1,0:T(8,128)(2,1)S(1)}, u32[]{:S(2)}, u32[]{:S(2)}) collective-permute-start(bf16[272,128]{1,0:T(8,128)(2,1)} %pack.1), channel_id=1, source_target_pairs={{0,16},{1,17},{2,18},{3,19},{4,20},{5,21},{6,22},{7,23},{8,24},{9,... | collective-permute-start | bytes 208904 | tf_op jit(solution)/shard_map/ppermute | solution.py:31
  17.3 5.4 %collective-permute-start.11 = (bf16[544,128]{1,0:T(8,128)(2,1)S(1)}, bf16[544,128]{1,0:T(8,128)(2,1)S(1)}, u32[]{:S(2)}, u32[]{:S(2)}) collective-permute-start(bf16[544,128]{1,0:T(8,128)(2,1)S(1)} %pad_maximum_fusion.8), channel_id=1, source_target_pairs={{0,2},{1,3},{2,0},{3,1},{4,6},{5,7},{6,4},{7,5},{8,10},{9,11},{10,... | collective-permute-start | bytes 417800 | tf_op jit(solution)/shard_map/ppermute | solution.py:31
  19.7 6.3 %collective-permute-start.1 = (bf16[16,5120]{1,0:T(8,128)(2,1)S(1)}, bf16[16,5120]{1,0:T(8,128)(2,1)S(1)}, u32[]{:S(2)}, u32[]{:S(2)}) collective-permute-start(bf16[16,5120]{1,0:T(8,128)(2,1)S(1)} %pad_maximum_fusion.6), channel_id=1, source_target_pairs={{0,4},{1,5},{2,6},{3,7},{4,0},{5,1},{6,2},{7,3},{8,12},{9,13},{10,... | collective-permute-start | bytes 491528 | tf_op jit(solution)/shard_map/ppermute | solution.py:31
  21.3 6.0 %collective-permute-start.6 = (bf16[16,5120]{1,0:T(8,128)(2,1)S(1)}, bf16[16,5120]{1,0:T(8,128)(2,1)S(1)}, u32[]{:S(2)}, u32[]{:S(2)}) collective-permute-start(bf16[16,5120]{1,0:T(8,128)(2,1)S(1)} %pad_maximum_fusion.7), channel_id=1, source_target_pairs={{0,8},{1,9},{2,10},{3,11},{4,12},{5,13},{6,14},{7,15},{8,0},{9,1},... | collective-permute-start | bytes 491528 | tf_op jit(solution)/shard_map/ppermute | solution.py:31
  22.7 8.4 %collective-permute-start.12 = (bf16[1088,128]{1,0:T(8,128)(2,1)S(1)}, bf16[1088,128]{1,0:T(8,128)(2,1)S(1)}, u32[]{:S(2)}, u32[]{:S(2)}) collective-permute-start(bf16[1088,128]{1,0:T(8,128)(2,1)S(1)} %pad_maximum_fusion.5), channel_id=1, source_target_pairs={{0,4},{1,5},{2,6},{3,7},{4,0},{5,1},{6,2},{7,3},{8,12},{9,13},{10,... | collective-permute-start | bytes 835592 | tf_op jit(solution)/shard_map/ppermute | solution.py:31
  26.0 8.8 %collective-permute-start.2 = (bf16[32,5120]{1,0:T(8,128)(2,1)S(1)}, bf16[32,5120]{1,0:T(8,128)(2,1)S(1)}, u32[]{:S(2)}, u32[]{:S(2)}) collective-permute-start(bf16[32,5120]{1,0:T(8,128)(2,1)S(1)} %pad_maximum_fusion.3), channel_id=1, source_target_pairs={{0,8},{1,9},{2,10},{3,11},{4,12},{5,13},{6,14},{7,15},{8,0},{9,1},... | collective-permute-start | bytes 983048 | tf_op jit(solution)/shard_map/ppermute | solution.py:31
  27.3 9.2 %collective-permute-start.7 = (bf16[32,5120]{1,0:T(8,128)(2,1)S(1)}, bf16[32,5120]{1,0:T(8,128)(2,1)S(1)}, u32[]{:S(2)}, u32[]{:S(2)}) collective-permute-start(bf16[32,5120]{1,0:T(8,128)(2,1)S(1)} %pad_maximum_fusion.4), channel_id=1, source_target_pairs={{0,2},{1,3},{2,0},{3,1},{4,6},{5,7},{6,4},{7,5},{8,10},{9,11},{10,... | collective-permute-start | bytes 983048 | tf_op jit(solution)/shard_map/ppermute | solution.py:31
  31.1 14.6 %collective-permute-start.13 = (bf16[2176,128]{1,0:T(8,128)(2,1)S(1)}, bf16[2176,128]{1,0:T(8,128)(2,1)S(1)}, u32[]{:S(2)}, u32[]{:S(2)}) collective-permute-start(bf16[2176,128]{1,0:T(8,128)(2,1)S(1)} %pad_maximum_fusion.2), channel_id=1, source_target_pairs={{0,8},{1,9},{2,10},{3,11},{4,12},{5,13},{6,14},{7,15},{8,0},{9,1},... | collective-permute-start | bytes 1671176 | tf_op jit(solution)/shard_map/ppermute | solution.py:31
  34.8 14.6 %collective-permute-start.3 = (bf16[64,5120]{1,0:T(8,128)(2,1)S(1)}, bf16[64,5120]{1,0:T(8,128)(2,1)S(1)}, u32[]{:S(2)}, u32[]{:S(2)}) collective-permute-start(bf16[64,5120]{1,0:T(8,128)(2,1)S(1)} %pad_maximum_fusion), channel_id=1, source_target_pairs={{0,2},{1,3},{2,0},{3,1},{4,6},{5,7},{6,4},{7,5},{8,10},{9,11},{10,... | collective-permute-start | bytes 1966088 | tf_op jit(solution)/shard_map/ppermute | solution.py:31
  36.6 12.0 %collective-permute-start.8 = (bf16[64,5120]{1,0:T(8,128)(2,1)S(1)}, bf16[64,5120]{1,0:T(8,128)(2,1)S(1)}, u32[]{:S(2)}, u32[]{:S(2)}) collective-permute-start(bf16[64,5120]{1,0:T(8,128)(2,1)S(1)} %pad_maximum_fusion.1), channel_id=1, source_target_pairs={{0,4},{1,5},{2,6},{3,7},{4,0},{5,1},{6,2},{7,3},{8,12},{9,13},{10,... | collective-permute-start | bytes 1966088 | tf_op jit(solution)/shard_map/ppermute | solution.py:31
  36.8 1.1 %copy-start = (bf16[128,5120]{1,0:T(8,128)(2,1)}, bf16[128,5120]{1,0:T(8,128)(2,1)S(1)}, u32[]{:S(2)}) copy-start(bf16[128,5120]{1,0:T(8,128)(2,1)S(1)} %constant_dynamic-update-slice_fusion.6) | copy-start | bytes 3932164
  45.6 18.9 %slice-start = ((s8[10485760]{0:T(1024)(128)(4,1)}), s8[2097152]{0:T(1024)(128)(4,1)S(1)}, s32[]{:S(2)}) async-start(s8[10485760]{0:T(1024)(128)(4,1)} %bitcast.3), calls=%async_computation.1 | async-start | bytes 4194304
  46.5 3.6 %copy-start.3 = (s32[256]{0:T(256)S(1)}, s32[256]{0:T(256)}, u32[]{:S(2)}) copy-start(s32[256]{0:T(256)} %lens.1) | copy-start | bytes 3076
  46.5 3.6 %collective-permute-start.14 = (bf16[4352,128]{1,0:T(8,128)(2,1)}, bf16[4352,128]{1,0:T(8,128)(2,1)}, u32[]{:S(2)}, u32[]{:S(2)}) collective-permute-start(bf16[4352,128]{1,0:T(8,128)(2,1)} %constant_dynamic-update-slice_fusion.10.own.codes_own), channel_id=1, source_target_pairs={{0,1},{1,0},{2,3},{3,2},{4,5},{5,4},{6,7},{7,6},{8,9},{9,8},{10,11... | collective-permute-start | bytes 3342344 | tf_op jit(solution)/shard_map/ppermute | solution.py:31
  49.4 15.1 %collective-permute-start.9 = (bf16[128,5120]{1,0:T(8,128)(2,1)}, bf16[128,5120]{1,0:T(8,128)(2,1)}, u32[]{:S(2)}, u32[]{:S(2)}) collective-permute-start(bf16[128,5120]{1,0:T(8,128)(2,1)} %constant_dynamic-update-slice_fusion.5.own), channel_id=1, source_target_pairs={{0,1},{1,0},{2,3},{3,2},{4,5},{5,4},{6,7},{7,6},{8,9},{9,8},{10,11... | collective-permute-start | bytes 3932168 | tf_op jit(solution)/shard_map/ppermute | solution.py:31
  49.5 18.9 %collective-permute-start.4 = (bf16[128,5120]{1,0:T(8,128)(2,1)S(1)}, bf16[128,5120]{1,0:T(8,128)(2,1)}, u32[]{:S(2)}, u32[]{:S(2)}) collective-permute-start(bf16[128,5120]{1,0:T(8,128)(2,1)S(1)} %constant_dynamic-update-slice_fusion.own), channel_id=1, source_target_pairs={{0,1},{1,0},{2,3},{3,2},{4,5},{5,4},{6,7},{7,6},{8,9},{9,8},{10,11... | collective-permute-start | bytes 3932168 | tf_op jit(solution)/shard_map/ppermute | solution.py:31
  50.1 3.4 %copy-start.2 = (bf16[256,128,128]{2,1,0:T(8,128)(2,1)S(1)}, bf16[256,128,128]{2,1,0:T(8,128)(2,1)}, u32[]{:S(2)}) copy-start(bf16[256,128,128]{2,1,0:T(8,128)(2,1)} %tiles.1) | copy-start | bytes 25165828
  53.5 11.1 %slice-start.1 = ((s8[10485760]{0:T(1024)(128)(4,1)}), s8[4194304]{0:T(1024)(128)(4,1)S(1)}, s32[]{:S(2)}) async-start(s8[10485760]{0:T(1024)(128)(4,1)} %bitcast.3), calls=%async_computation.2 | async-start | bytes 8388608
  53.5 11.1 %slice-start.2 = ((s8[10485760]{0:T(1024)(128)(4,1)}), s8[4194304]{0:T(1024)(128)(4,1)S(1)}, s32[]{:S(2)}) async-start(s8[10485760]{0:T(1024)(128)(4,1)} %bitcast.3), calls=%async_computation.3 | async-start | bytes 8388608
  53.5 11.1 %copy-start.1 = (bf16[128,5120]{1,0:T(8,128)(2,1)S(1)}, bf16[128,5120]{1,0:T(8,128)(2,1)}, u32[]{:S(2)}) copy-start(bf16[128,5120]{1,0:T(8,128)(2,1)} %constant_dynamic-update-slice_fusion.5.own) | copy-start | bytes 3932164

commit v3 on v2

--- a/solution.py
+++ b/solution.py
@@ -23,8 +23,11 @@
 
 def orders_of(n):
     bits = [1 << i for i in range(1, n.bit_length() - 1)]
-    far, rest = bits[-1], bits[:-1]
-    return [[far] + rest[i:] + rest[:i] for i in (0, len(rest) - 1, 1)]
+    far, rest = bits[-1:], bits[:-1]
+    return [[16, 2, 4, 8], [16, 8, 2, 4], [16, 4, 8, 2]]
+
+
+TIES = {}
 
 
 def exchange(x, bit, n):
@@ -141,44 +144,35 @@
     total[...] += lax.dot_general(left, doc[...], NT, preferred_element_type=jnp.float32)
 
 
-def last_kernel(cfg, me_ref, own, other, doc, so_far, codes_own, codes_other, maxsim, out, total):
-    order, first_order, code_order, parts, cand_at, stride = cfg
-    blocks = len(order)
-    half = blocks * 8
-
-    @pl.when(pl.program_id(0) == 0)
-    def _():
-        for side in range(2):
-            for p in range(blocks):
-                q = first_order.index(order[p])
-                total[side * half + p * 8 : side * half + p * 8 + 8, :] = so_far[
-                    side * half + q * 8 : side * half + q * 8 + 8, :
-                ]
-
-    left = jnp.concatenate([own[...], other[...]], axis=0)
-    total[...] += lax.dot_general(left, doc[...], NT, preferred_element_type=jnp.float32)
+def last_kernel(cfg, me_ref, own, other, doc, first, *refs):
+    masks, parts, cand_at, blocks = cfg
+    codes, scores, out, last = refs[:4], refs[4:6], refs[6], refs[7]
+    stride = codes[0].shape[0] // blocks
+    beam_kernel(own, other, doc, last)
 
     @pl.when(pl.program_id(0) == pl.num_programs(0) - 1)
     def _():
         me = me_ref[0]
-        lane = lax.broadcasted_iota(jnp.int32, (8, LANES), 1)
-        nodes = total.shape[1]
-        for side, ref in enumerate((codes_own, codes_other)):
-            for p in range(blocks):
-                t = code_order.index(order[p])
-                codes = ref[(t + 1) * stride - 16 : (t + 1) * stride, :].astype(jnp.float32)[:8]
-                low = pltpu.roll(codes, LANES - cand_at, axis=1).astype(jnp.int32)
-                codes = codes.astype(jnp.int32)
-                owner, high = codes // parts, codes % parts
+        lane = ids((8, LANES), 1)
+        nodes = last.shape[1]
+
+        for m in masks[0]:
+            for side in range(2):
+                half, t = divmod(masks[0].index(m), blocks)
+                table = codes[2 * half + side][(t + 1) * stride - 16 : (t + 1) * stride, :].astype(jnp.float32)[:8]
+                low = pltpu.roll(table, LANES - cand_at, axis=1).astype(jnp.int32)
+                table = table.astype(jnp.int32)
+                owner, high = table // parts, table % parts
                 slot = high * 256 + low
                 within, page = slot % LANES, slot // LANES
-                rows = total[side * half + p * 8 : side * half + p * 8 + 8, :]
+                ats = [(side * 2 * blocks + masks[k].index(m)) * 8 for k in (1, 2)]
+                rows = first[ats[0] : ats[0] + 8, :] + last[ats[1] : ats[1] + 8, :]
                 found = jnp.zeros((8, LANES), jnp.float32)
                 for g in range(nodes // LANES):
                     here = jnp.take_along_axis(rows[:, g * LANES : (g + 1) * LANES], within, axis=1)
                     found = jnp.where(page == g, here, found)
                 found = jnp.where(owner == me, found, 0.0)
-                out[me ^ (order[p] + side)] = jnp.where(lane < cand_at, found, maxsim[side * blocks + t])
+                out[me ^ (m + side)] = jnp.where(lane < cand_at, found, scores[half][side * blocks + t])
 
 
 def sum_kernel(rounds, front, cands, parts, beam, maxsim):
@@ -201,7 +195,7 @@
     assert cand_at + max(cand_at, cands) <= LANES and n * parts <= 256 and passage_tiles.shape[0] <= 256
     me = lax.axis_index("dom").astype(jnp.int32)
     stride = queries * qt + 16
-    blocks = n // 2
+    blocks = n // 4
     orders = orders_of(n)
     masks = [sources_of(o) for o in orders]
 
@@ -217,68 +211,86 @@
         name="pack",
     )(frontier_owner, frontier_slot, cand_owner.reshape(queries, cands), cand_slot, query_tokens.reshape(queries * qt, dim))
     half = fde // 2
-    chunks = [packed, query_fde[:, :half], query_fde[:, half:]]
-    for step in range(len(orders[0])):
-        for k in range(3):
-            chunks[k] = jnp.concatenate([chunks[k], exchange(chunks[k], orders[k][step], n)], axis=0)
-    pairs = [(c, exchange(c, 1, n)) for c in chunks]
-    (tok_own, tok_other), (a_own, a_other), (b_own, b_other) = pairs
+    starts = [packed, query_fde[:, :half], query_fde[:, half:]]
+    stages = len(orders[0])
+
+    @functools.cache
+    def gathered(k, step):
+        if step == 0:
+            return starts[k]
+        return jnp.concatenate([gathered(k, step - 1), arrived(k, step - 1)], axis=0)
+
+    @functools.cache
+    def arrived(k, step):
+        mine = gathered(k, step)
+        if (k, step) in TIES:
+            mine = lax.optimization_barrier((mine, arrived(*TIES[k, step])))[0]
+        return exchange(mine, orders[k][step], n)
+
+    tok = [gathered(0, stages - 1), arrived(0, stages - 1)]
+    tok = [(tok[0], exchange(tok[0], 1, n)), tok[1]]
 
     pt = passage_tiles.shape[1]
-    maxsim = pl.pallas_call(
-        functools.partial(maxsim_kernel, cand_at, cands, cap),
-        out_shape=jax.ShapeDtypeStruct((n, 8, LANES), jnp.float32),
-        grid_spec=pltpu.PrefetchScalarGridSpec(
-            num_scalar_prefetch=2,
-            grid=(),
-            in_specs=[VMEM] * 3,
-            out_specs=VMEM,
-            scratch_shapes=[pltpu.VMEM((n, LANES), jnp.int32), pltpu.SMEM((n, LANES), jnp.int32), pltpu.SemaphoreType.DMA],
-        ),
-        compiler_params=pltpu.CompilerParams(vmem_limit_bytes=16 << 20),
-        cost_estimate=pl.CostEstimate(
-            flops=16 * slots * pt * qt * dim, bytes_accessed=8 << 20, transcendentals=0
-        ),
-        name="maxsim",
-    )(me.reshape(1), passage_len, tok_own, tok_other, passage_tiles)
+    score = lambda own, other: pl.pallas_call(
+            functools.partial(maxsim_kernel, cand_at, cands, cap),
+            out_shape=jax.ShapeDtypeStruct((n // 2, 8, LANES), jnp.float32),
+            grid_spec=pltpu.PrefetchScalarGridSpec(
+                num_scalar_prefetch=2,
+                grid=(),
+                in_specs=[VMEM] * 3,
+                out_specs=VMEM,
+                scratch_shapes=[
+                    pltpu.VMEM((n // 2, LANES), jnp.int32),
+                    pltpu.SMEM((n // 2, LANES), jnp.int32),
+                    pltpu.SemaphoreType.DMA,
+                ],
+            ),
+            compiler_params=pltpu.CompilerParams(vmem_limit_bytes=16 << 20),
+            cost_estimate=pl.CostEstimate(flops=8 * slots * pt * qt * dim, bytes_accessed=8 << 20, transcendentals=0),
+            name="maxsim",
+        )(me.reshape(1), passage_len, own, other, passage_tiles)
+
+    early = score(*tok[0])
+    late, early = lax.optimization_barrier((tok[1], early))
+    late_other = exchange(late, 1, n)
+    a_own, b_own, late_other = lax.optimization_barrier((gathered(1, stages), gathered(2, stages), late_other))
+    tok = [tok[0], (late, late_other)]
+    maxsim = [early, score(*tok[1])]
+    a_other, b_other = exchange(a_own, 1, n), exchange(b_own, 1, n)
 
     block = math.gcd(half, 1280)
     steps = half // block
     rows = n * 8
-
-    def beam_specs(first, prefetch):
-        left = pl.BlockSpec((rows // 2, block), lambda i, *_: (0, i))
-        return [left, left, pl.BlockSpec((nodes, block), lambda i, *_: (0, first + i))]
-
-    whole = pl.BlockSpec((rows, nodes), lambda i, *_: (0, 0))
+    full = lambda shape: pl.BlockSpec(shape, lambda i, *_: (0,) * len(shape))
+    left = pl.BlockSpec((rows // 2, block), lambda i, *_: (0, i))
+    doc = lambda first: pl.BlockSpec((nodes, block), lambda i, *_: (0, first + i))
+    partial = jax.ShapeDtypeStruct((rows, nodes), jnp.float32)
     cost = pl.CostEstimate(flops=2 * rows * nodes * half, bytes_accessed=2 * (rows + nodes) * half, transcendentals=0)
-    so_far = pl.pallas_call(
+    first = pl.pallas_call(
         beam_kernel,
-        out_shape=jax.ShapeDtypeStruct((rows, nodes), jnp.float32),
+        out_shape=partial,
         grid=(steps,),
-        in_specs=beam_specs(0, 0),
-        out_specs=whole,
+        in_specs=[left, left, doc(0)],
+        out_specs=full(partial.shape),
         compiler_params=pltpu.CompilerParams(vmem_limit_bytes=16 << 20),
         cost_estimate=cost,
         name="beam",
     )(a_own, a_other, doc_fde)
-    cfg = (masks[2], masks[1], masks[0], parts, cand_at, stride)
-    full = lambda shape: pl.BlockSpec(shape, lambda i, *_: (0,) * len(shape))
+    codes = [*tok[0], *tok[1]]
     scored = pl.pallas_call(
-        functools.partial(last_kernel, cfg),
+        functools.partial(last_kernel, (masks, parts, cand_at, blocks)),
         out_shape=jax.ShapeDtypeStruct((n, 8, LANES), jnp.float32),
         grid_spec=pltpu.PrefetchScalarGridSpec(
             num_scalar_prefetch=1,
             grid=(steps,),
-            in_specs=beam_specs(steps, 1)
-            + [whole, full(tok_own.shape), full(tok_own.shape), full((n, 8, LANES))],
+            in_specs=[left, left, doc(steps)] + [full(x.shape) for x in (first, *codes, *maxsim)],
             out_specs=full((n, 8, LANES)),
-            scratch_shapes=[pltpu.VMEM((rows, nodes), jnp.float32)],
+            scratch_shapes=[pltpu.VMEM(partial.shape, jnp.float32)],
         ),
         compiler_params=pltpu.CompilerParams(vmem_limit_bytes=24 << 20),
         cost_estimate=cost,
         name="beam_last",
-    )(me.reshape(1), b_own, b_other, doc_fde, so_far, tok_own, tok_other, maxsim)
+    )(me.reshape(1), b_own, b_other, doc_fde, first, *codes, *maxsim)
 
     returned = lax.all_to_all(scored, "dom", split_axis=0, concat_axis=0, tiled=True)
     return pl.pallas_call(

time: 89.8 us -> 75.7 us (0.84)
  local copies, waits for them, and re-layouts: 10.9 us -> 1.15 us
  Pallas kernels: 23.9 us -> 20.4 us
  waiting for transfers between devices: 21.2 us -> 19.5 us
    unnamed x26 -> x18, local copies, waits for them, and re-layouts: 8.14 us -> 0.12 us
    pallas_call x2, Pallas kernels: 9.2 us -> 6.38 us  [the longest x1 3.58 us: local(): pl.pallas_call(functools.partial(last_kernel, (masks, parts, cand_at, blo...]
    concatenate x3 -> x2, local copies, waits for them, and re-layouts: 1.79 us -> 0.09 us  [gathered(): jnp.concatenate([gathered(k, step - 1), arrived(k, step - 1)], axis=0)]
    ppermute x15 -> x16, waiting for transfers between devices: 21.2 us -> 19.5 us  [exchange(): return lax.ppermute(x, 'dom', [(i, i ^ bit) for i in range(n)])]
    pallas_call x1 -> x2, Pallas kernels: 11 us -> 10.4 us  [local(): pl.pallas_call(functools.partial(maxsim_kernel, cand_at, cands, cap), out...]
    ppermute x15 -> x16, starting transfers between devices: 17.5 us -> 18.1 us  [exchange(): return lax.ppermute(x, 'dom', [(i, i ^ bit) for i in range(n)])]
  transfers between devices with their start and end apart: 15 -> 16, of which waited for: 8 -> 10; matrix products, arithmetic and copies ran while one was open for 7% -> 3% of each run, Pallas kernels for 19% -> 17%
where the time goes in v3:
time: 75.7 us; the launch traced here: 75.5 us
  Pallas kernels  20.4 us (27%)
  waiting for transfers between devices  19.5 us (26%)
  starting transfers between devices  18.1 us (24%)
  blocking collectives  14.3 us (19%)
  local copies, waits for them, and re-layouts  1.15 us (2%)
  other arithmetic  1.11 us (1%)
  between operations  0.9 us (1%)
    ppermute x16, waiting for transfers between devices, exchange(): return lax.ppermute(x, 'dom', [(i, i ^ bit) for i in range(n)])  19.5 us
    ppermute x16, starting transfers between devices, exchange(): return lax.ppermute(x, 'dom', [(i, i ^ bit) for i in range(n)])  18.1 us
    all_to_all x1, blocking collectives, local(): lax.all_to_all(scored, 'dom', split_axis=0, concat_axis=0, tiled=True)  14.3 us
    pallas_call x2, Pallas kernels, local(): pl.pallas_call(functools.partial(maxsim_kernel, cand_at, cands, cap), out...  10.4 us
    pallas_call x1, Pallas kernels, local(): pl.pallas_call(functools.partial(last_kernel, (masks, parts, cand_at, blo...  3.58 us
    pallas_call x1, Pallas kernels, local(): pl.pallas_call(beam_kernel, out_shape=partial, grid=(steps,), in_specs=[l...  2.8 us
    pallas_call x1, Pallas kernels, local(): pl.pallas_call(functools.partial(prep_kernel, parts, slots, cap), out_sha...  2.01 us
    pallas_call x1, Pallas kernels, local(): pl.pallas_call(functools.partial(sum_kernel, rounds, front, cands), out_s...  1.61 us
  transfers between devices with their start and end apart: 16, of which 10 were waited for; matrix products, arithmetic and copies ran while one was open for 3% of the time, Pallas kernels for 17%

profile of v3, /device:TPU:0, one launch (start us, length us, event | category | flops | bytes accessed | tf_op | source)
XLA Modules:
  0.0 75.5 jit_solution(14828677352703446384)
XLA Ops:
  0.6 2.0 %pack.1 = bf16[272,128]{1,0:T(8,128)(2,1)} custom-call(s32[3,8,16]{2,1,0:T(8,128)} %fo.1, s32[3,8,16]{2,1,0:T(8,128)} %fs.1, s32[8,32]{1,0:T(8,128)} %bitcast.6, s32[8,32]{1,0:T(8,128)} %cs.1, bf16[256,128]{1,0:T(8,128)(2,1)} %bitcast.5), custom_call_target="tpu_custom_call" | custom-call | tf_op jit(solution)/shard_map/pack/pallas_call | solution.py:206
  2.6 4.0 %collective-permute-start.8 = (bf16[272,128]{1,0:T(8,128)(2,1)}, bf16[272,128]{1,0:T(8,128)(2,1)S(1)}, u32[]{:S(2)}, u32[]{:S(2)}) collective-permute-start(bf16[272,128]{1,0:T(8,128)(2,1)} %pack.1), channel_id=1, source_target_pairs={{0,16},{1,17},{2,18},{3,19},{4,20},{5,21},{6,22},{7,23},{8,24},{9,... | collective-permute-start | bytes 208904 | tf_op jit(solution)/shard_map/ppermute | solution.py:34
  6.7 0.9 %fusion = (bf16[8,5120]{1,0:T(8,128)(2,1)S(1)}, bf16[128,5120]{1,0:T(8,128)(2,1)S(1)}, bf16[128,5120]{1,0:T(8,128)(2,1)S(1)}, bf16[8,5120]{1,0:T(8,128)(2,1)S(1)}) fusion(bf16[8,10240]{1,0:T(8,128)(2,1)} %param.9), kind=kLoop, calls=%fused_computation.19 | loop fusion | bytes 491520 | tf_op jit(solution)/shard_map/slice | solution.py:214
  7.6 0.1 collective-permute-start.4
  7.7 2.9 %collective-permute-start = (bf16[8,5120]{1,0:T(8,128)(2,1)S(1)}, bf16[8,5120]{1,0:T(8,128)(2,1)S(1)}, u32[]{:S(2)}, u32[]{:S(2)}) collective-permute-start(bf16[8,5120]{1,0:T(8,128)(2,1)S(1)} %get-tuple-element.15), channel_id=1, source_target_pairs={{0,16},{1,17},{2,18},{3,19},{4,20},{5,21},{6,22},{7,23},{8,24},{9,... | collective-permute-start | bytes 245768 | tf_op jit(solution)/shard_map/ppermute | solution.py:34
  10.6 0.1 collective-permute-done.8
  10.7 0.9 %pad_maximum_fusion.8 = bf16[544,128]{1,0:T(8,128)(2,1)S(1)} fusion(bf16[272,128]{1,0:T(8,128)(2,1)S(1)} %collective-permute-done.8, bf16[272,128]{1,0:T(8,128)(2,1)} %pack.1), kind=kLoop, calls=%fused_computation.8 | loop fusion | flops 278528 | bytes 278528 | tf_op jit(solution)/shard_map/concatenate | solution.py:221
  11.6 1.8 %collective-permute-start.9 = (bf16[544,128]{1,0:T(8,128)(2,1)S(1)}, bf16[544,128]{1,0:T(8,128)(2,1)S(1)}, u32[]{:S(2)}, u32[]{:S(2)}) collective-permute-start(bf16[544,128]{1,0:T(8,128)(2,1)S(1)} %pad_maximum_fusion.8), channel_id=1, source_target_pairs={{0,2},{1,3},{2,0},{3,1},{4,6},{5,7},{6,4},{7,5},{8,10},{9,11},{10,... | collective-permute-start | bytes 417800 | tf_op jit(solution)/shard_map/ppermute | solution.py:34
  13.4 3.5 %collective-permute-done.4 = bf16[8,5120]{1,0:T(8,128)(2,1)S(1)} collective-permute-done((bf16[8,5120]{1,0:T(8,128)(2,1)S(1)}, bf16[8,5120]{1,0:T(8,128)(2,1)S(1)}, u32[]{:S(2)}, u32[]{:S(2)}) %collective-permute-start.4) | collective-permute-done | bytes 81952 | tf_op jit(solution)/shard_map/ppermute | solution.py:34
  16.9 1.7 %collective-permute-start.5 = (bf16[16,5120]{1,0:T(8,128)(2,1)S(1)}, bf16[16,5120]{1,0:T(8,128)(2,1)S(1)}, u32[]{:S(2)}, u32[]{:S(2)}) collective-permute-start(bf16[16,5120]{1,0:T(8,128)(2,1)S(1)} %pad_maximum_fusion.7), channel_id=1, source_target_pairs={{0,4},{1,5},{2,6},{3,7},{4,0},{5,1},{6,2},{7,3},{8,12},{9,13},{10,... | collective-permute-start | bytes 491528 | tf_op jit(solution)/shard_map/ppermute | solution.py:34
  18.7 0.5 collective-permute-start.1
  19.2 0.8 %collective-permute-start.10 = (bf16[1088,128]{1,0:T(8,128)(2,1)S(1)}, bf16[1088,128]{1,0:T(8,128)(2,1)S(1)}, u32[]{:S(2)}, u32[]{:S(2)}) collective-permute-start(bf16[1088,128]{1,0:T(8,128)(2,1)S(1)} %pad_maximum_fusion.5), channel_id=1, source_target_pairs={{0,4},{1,5},{2,6},{3,7},{4,0},{5,1},{6,2},{7,3},{8,12},{9,13},{10,... | collective-permute-start | bytes 835592 | tf_op jit(solution)/shard_map/ppermute | solution.py:34
  20.0 3.7 %collective-permute-done.5 = bf16[16,5120]{1,0:T(8,128)(2,1)S(1)} collective-permute-done((bf16[16,5120]{1,0:T(8,128)(2,1)S(1)}, bf16[16,5120]{1,0:T(8,128)(2,1)S(1)}, u32[]{:S(2)}, u32[]{:S(2)}) %collective-permute-start.5) | collective-permute-done | bytes 163872 | tf_op jit(solution)/shard_map/ppermute | solution.py:34
  23.8 1.7 %collective-permute-done.1 = bf16[16,5120]{1,0:T(8,128)(2,1)S(1)} collective-permute-done((bf16[16,5120]{1,0:T(8,128)(2,1)S(1)}, bf16[16,5120]{1,0:T(8,128)(2,1)S(1)}, u32[]{:S(2)}, u32[]{:S(2)}) %collective-permute-start.1) | collective-permute-done | bytes 163872 | tf_op jit(solution)/shard_map/ppermute | solution.py:34
  25.5 1.6 %collective-permute-start.2 = (bf16[32,5120]{1,0:T(8,128)(2,1)S(1)}, bf16[32,5120]{1,0:T(8,128)(2,1)S(1)}, u32[]{:S(2)}, u32[]{:S(2)}) collective-permute-start(bf16[32,5120]{1,0:T(8,128)(2,1)S(1)} %pad_maximum_fusion.3), channel_id=1, source_target_pairs={{0,2},{1,3},{2,0},{3,1},{4,6},{5,7},{6,4},{7,5},{8,10},{9,11},{10,... | collective-permute-start | bytes 983048 | tf_op jit(solution)/shard_map/ppermute | solution.py:34
  27.1 1.1 %collective-permute-done.10 = bf16[1088,128]{1,0:T(8,128)(2,1)S(1)} collective-permute-done((bf16[1088,128]{1,0:T(8,128)(2,1)S(1)}, bf16[1088,128]{1,0:T(8,128)(2,1)S(1)}, u32[]{:S(2)}, u32[]{:S(2)}) %collective-permute-start.10) | collective-permute-done | bytes 278560 | tf_op jit(solution)/shard_map/ppermute | solution.py:34
  28.3 0.1 collective-permute-start.12
  28.4 0.9 %collective-permute-start.11 = (bf16[2176,128]{1,0:T(8,128)(2,1)S(1)}, bf16[2176,128]{1,0:T(8,128)(2,1)S(1)}, u32[]{:S(2)}, u32[]{:S(2)}) collective-permute-start(bf16[2176,128]{1,0:T(8,128)(2,1)S(1)} %pad_maximum_fusion.2.own.refs_0_), channel_id=1, source_target_pairs={{0,8},{1,9},{2,10},{3,11},{4,12},{5,13},{6,14},{7,15},{8,0},{9,1},... | collective-permute-start | bytes 1671176 | tf_op jit(solution)/shard_map/ppermute | solution.py:34
  29.3 1.8 %collective-permute-done.6 = bf16[32,5120]{1,0:T(8,128)(2,1)S(1)} collective-permute-done((bf16[32,5120]{1,0:T(8,128)(2,1)S(1)}, bf16[32,5120]{1,0:T(8,128)(2,1)S(1)}, u32[]{:S(2)}, u32[]{:S(2)}) %collective-permute-start.6) | collective-permute-done | bytes 327712 | tf_op jit(solution)/shard_map/ppermute | solution.py:34
  31.1 1.7 %collective-permute-start.7 = (bf16[64,5120]{1,0:T(8,128)(2,1)S(1)}, bf16[64,5120]{1,0:T(8,128)(2,1)S(1)}, u32[]{:S(2)}, u32[]{:S(2)}) collective-permute-start(bf16[64,5120]{1,0:T(8,128)(2,1)S(1)} %pad_maximum_fusion.1), channel_id=1, source_target_pairs={{0,2},{1,3},{2,0},{3,1},{4,6},{5,7},{6,4},{7,5},{8,10},{9,11},{10,... | collective-permute-start | bytes 1966088 | tf_op jit(solution)/shard_map/ppermute | solution.py:34
  32.8 0.3 collective-permute-done.2
  33.2 1.3 %collective-permute-start.3 = (bf16[64,5120]{1,0:T(8,128)(2,1)S(1)}, bf16[64,5120]{1,0:T(8,128)(2,1)S(1)}, u32[]{:S(2)}, u32[]{:S(2)}) collective-permute-start(bf16[64,5120]{1,0:T(8,128)(2,1)S(1)} %pad_maximum_fusion), channel_id=1, source_target_pairs={{0,4},{1,5},{2,6},{3,7},{4,0},{5,1},{6,2},{7,3},{8,12},{9,13},{10,... | collective-permute-start | bytes 1966088 | tf_op jit(solution)/shard_map/ppermute | solution.py:34
  34.6 5.2 %maxsim.2.refs_4_ = f32[16,8,128]{2,1,0:T(8,128)S(1)} custom-call(s32[1]{0:T(128)} %bitcast.me_ref, s32[256]{0:T(256)S(1)} %copy-done.1, bf16[2176,128]{1,0:T(8,128)(2,1)S(1)} %pad_maximum_fusion.2.own.refs_0_, bf16[2176,128]{1,0:T(8,128)(2,1)S(1)} %collective-permute-done.12.other.refs_1_, bf16[256,128,128]{2,1,0:T(8,128)(2,1)S(1)} %copy-done), custom_call_target="tpu_custom_call" | custom-call | flops 2147483648 | bytes 8388608 | tf_op jit(solution)/shard_map/maxsim/pallas_call | solution.py:234
  39.8 3.6 %collective-permute-done.11.own.refs_2_ = bf16[2176,128]{1,0:T(8,128)(2,1)S(1)} collective-permute-done((bf16[2176,128]{1,0:T(8,128)(2,1)S(1)}, bf16[2176,128]{1,0:T(8,128)(2,1)S(1)}, u32[]{:S(2)}, u32[]{:S(2)}) %collective-permute-start.11) | collective-permute-done | bytes 557088 | tf_op jit(solution)/shard_map/ppermute | solution.py:34
  43.4 3.3 %collective-permute-done.7 = bf16[64,5120]{1,0:T(8,128)(2,1)S(1)} collective-permute-done((bf16[64,5120]{1,0:T(8,128)(2,1)S(1)}, bf16[64,5120]{1,0:T(8,128)(2,1)S(1)}, u32[]{:S(2)}, u32[]{:S(2)}) %collective-permute-start.7) | collective-permute-done | bytes 655392 | tf_op jit(solution)/shard_map/ppermute | solution.py:34
  46.8 0.5 collective-permute-done.3
  47.4 0.5 collective-permute-start.14
  47.9 5.2 %maxsim.3.refs_5_ = f32[16,8,128]{2,1,0:T(8,128)S(1)} custom-call(s32[1]{0:T(128)} %bitcast.me_ref, s32[256]{0:T(256)S(1)} %copy-done.1, bf16[2176,128]{1,0:T(8,128)(2,1)S(1)} %collective-permute-done.11.own.refs_2_, bf16[2176,128]{1,0:T(8,128)(2,1)S(1)} %collective-permute-done.13.other.refs_3_, bf16[256,128,128]{2,1,0:T(8,128)(2,1)S(1)} %copy-done), custom_call_target="tpu_custom_call" | custom-call | flops 2147483648 | bytes 8388608 | tf_op jit(solution)/shard_map/maxsim/pallas_call | solution.py:234
  53.2 2.8 %beam.1.first = f32[256,512]{1,0:T(8,128)S(1)} custom-call(bf16[128,5120]{1,0:T(8,128)(2,1)S(1)} %constant_dynamic-update-slice_fusion.own, bf16[128,5120]{1,0:T(8,128)(2,1)S(1)} %collective-permute-done.15.other, bf16[512,10240]{1,0:T(8,128)(2,1)S(1)} %bitcast.4), custom_call_target="tpu_custom_call" | custom-call | flops 1342177280 | bytes 7864320 | tf_op jit(solution)/shard_map/beam/pallas_call | solution.py:269
  56.0 3.6 %beam_last.1 = f32[32,8,128]{2,1,0:T(8,128)S(1)} custom-call(s32[1]{0:T(128)} %bitcast.me_ref, bf16[128,5120]{1,0:T(8,128)(2,1)S(1)} %constant_dynamic-update-slice_fusion.5.own, bf16[128,5120]{1,0:T(8,128)(2,1)S(1)} %collective-permute-done.14.other, bf16[512,10240]{1,0:T(8,128)(2,1)S(1)} %bitcast.4, f32[256,512]{1,0:T(8,128)S(1)} %beam.1.first, ...), custom_call_target="tpu_custom_call" | custom-call | flops 1342177280 | bytes 7864320 | tf_op jit(solution)/shard_map/beam_last/pallas_call | solution.py:280
  59.6 14.3 %all_to_all.5.parts = f32[32,8,128]{2,1,0:T(8,128)} all-to-all(f32[32,8,128]{2,1,0:T(8,128)S(1)} %beam_last.1), channel_id=1, replica_groups=mesh['dom'=32,'rep'=1] {'dom'}, dimensions={0} | all-to-all | bytes 262144 | tf_op jit(solution)/shard_map/all_to_all | solution.py:295
  73.8 1.6 %collect.1 = (f32[3,8,16]{2,1,0:T(8,128)}, f32[8,32]{1,0:T(8,128)}) custom-call(f32[32,8,128]{2,1,0:T(8,128)} %all_to_all.5.parts), custom_call_target="tpu_custom_call" | custom-call | tf_op jit(solution)/shard_map/collect/pallas_call | solution.py:296
  (38 shorter events, 0.6 us)
Async XLA Ops:
  2.6 16.5 %copy-start.2 = (bf16[272,128]{1,0:T(8,128)(2,1)S(1)}, bf16[272,128]{1,0:T(8,128)(2,1)}, u32[]{:S(2)}) copy-start(bf16[272,128]{1,0:T(8,128)(2,1)} %pack.1) | copy-start | bytes 208900
  2.6 8.1 %collective-permute-start.8 = (bf16[272,128]{1,0:T(8,128)(2,1)}, bf16[272,128]{1,0:T(8,128)(2,1)S(1)}, u32[]{:S(2)}, u32[]{:S(2)}) collective-permute-start(bf16[272,128]{1,0:T(8,128)(2,1)} %pack.1), channel_id=1, source_target_pairs={{0,16},{1,17},{2,18},{3,19},{4,20},{5,21},{6,22},{7,23},{8,24},{9,... | collective-permute-start | bytes 208904 | tf_op jit(solution)/shard_map/ppermute | solution.py:34
  7.6 9.3 %collective-permute-start.4 = (bf16[8,5120]{1,0:T(8,128)(2,1)S(1)}, bf16[8,5120]{1,0:T(8,128)(2,1)S(1)}, u32[]{:S(2)}, u32[]{:S(2)}) collective-permute-start(bf16[8,5120]{1,0:T(8,128)(2,1)S(1)} %get-tuple-element.12), channel_id=1, source_target_pairs={{0,16},{1,17},{2,18},{3,19},{4,20},{5,21},{6,22},{7,23},{8,24},{9,... | collective-permute-start | bytes 245768 | tf_op jit(solution)/shard_map/ppermute | solution.py:34
  7.7 10.9 %collective-permute-start = (bf16[8,5120]{1,0:T(8,128)(2,1)S(1)}, bf16[8,5120]{1,0:T(8,128)(2,1)S(1)}, u32[]{:S(2)}, u32[]{:S(2)}) collective-permute-start(bf16[8,5120]{1,0:T(8,128)(2,1)S(1)} %get-tuple-element.15), channel_id=1, source_target_pairs={{0,16},{1,17},{2,18},{3,19},{4,20},{5,21},{6,22},{7,23},{8,24},{9,... | collective-permute-start | bytes 245768 | tf_op jit(solution)/shard_map/ppermute | solution.py:34
  11.6 7.5 %collective-permute-start.9 = (bf16[544,128]{1,0:T(8,128)(2,1)S(1)}, bf16[544,128]{1,0:T(8,128)(2,1)S(1)}, u32[]{:S(2)}, u32[]{:S(2)}) collective-permute-start(bf16[544,128]{1,0:T(8,128)(2,1)S(1)} %pad_maximum_fusion.8), channel_id=1, source_target_pairs={{0,2},{1,3},{2,0},{3,1},{4,6},{5,7},{6,4},{7,5},{8,10},{9,11},{10,... | collective-permute-start | bytes 417800 | tf_op jit(solution)/shard_map/ppermute | solution.py:34
  16.9 17.7 %copy-start = (bf16[256,128,128]{2,1,0:T(8,128)(2,1)S(1)}, bf16[256,128,128]{2,1,0:T(8,128)(2,1)}, u32[]{:S(2)}) copy-start(bf16[256,128,128]{2,1,0:T(8,128)(2,1)} %tiles.3) | copy-start | bytes 25165828
  16.9 6.8 %collective-permute-start.5 = (bf16[16,5120]{1,0:T(8,128)(2,1)S(1)}, bf16[16,5120]{1,0:T(8,128)(2,1)S(1)}, u32[]{:S(2)}, u32[]{:S(2)}) collective-permute-start(bf16[16,5120]{1,0:T(8,128)(2,1)S(1)} %pad_maximum_fusion.7), channel_id=1, source_target_pairs={{0,4},{1,5},{2,6},{3,7},{4,0},{5,1},{6,2},{7,3},{8,12},{9,13},{10,... | collective-permute-start | bytes 491528 | tf_op jit(solution)/shard_map/ppermute | solution.py:34
  18.7 6.8 %collective-permute-start.1 = (bf16[16,5120]{1,0:T(8,128)(2,1)S(1)}, bf16[16,5120]{1,0:T(8,128)(2,1)S(1)}, u32[]{:S(2)}, u32[]{:S(2)}) collective-permute-start(bf16[16,5120]{1,0:T(8,128)(2,1)S(1)} %pad_maximum_fusion.6), channel_id=1, source_target_pairs={{0,8},{1,9},{2,10},{3,11},{4,12},{5,13},{6,14},{7,15},{8,0},{9,1},... | collective-permute-start | bytes 491528 | tf_op jit(solution)/shard_map/ppermute | solution.py:34
  19.2 9.0 %collective-permute-start.10 = (bf16[1088,128]{1,0:T(8,128)(2,1)S(1)}, bf16[1088,128]{1,0:T(8,128)(2,1)S(1)}, u32[]{:S(2)}, u32[]{:S(2)}) collective-permute-start(bf16[1088,128]{1,0:T(8,128)(2,1)S(1)} %pad_maximum_fusion.5), channel_id=1, source_target_pairs={{0,4},{1,5},{2,6},{3,7},{4,0},{5,1},{6,2},{7,3},{8,12},{9,13},{10,... | collective-permute-start | bytes 835592 | tf_op jit(solution)/shard_map/ppermute | solution.py:34
  23.8 7.3 %collective-permute-start.6 = (bf16[32,5120]{1,0:T(8,128)(2,1)S(1)}, bf16[32,5120]{1,0:T(8,128)(2,1)S(1)}, u32[]{:S(2)}, u32[]{:S(2)}) collective-permute-start(bf16[32,5120]{1,0:T(8,128)(2,1)S(1)} %pad_maximum_fusion.4), channel_id=1, source_target_pairs={{0,8},{1,9},{2,10},{3,11},{4,12},{5,13},{6,14},{7,15},{8,0},{9,1},... | collective-permute-start | bytes 983048 | tf_op jit(solution)/shard_map/ppermute | solution.py:34
  25.5 7.6 %collective-permute-start.2 = (bf16[32,5120]{1,0:T(8,128)(2,1)S(1)}, bf16[32,5120]{1,0:T(8,128)(2,1)S(1)}, u32[]{:S(2)}, u32[]{:S(2)}) collective-permute-start(bf16[32,5120]{1,0:T(8,128)(2,1)S(1)} %pad_maximum_fusion.3), channel_id=1, source_target_pairs={{0,2},{1,3},{2,0},{3,1},{4,6},{5,7},{6,4},{7,5},{8,10},{9,11},{10,... | collective-permute-start | bytes 983048 | tf_op jit(solution)/shard_map/ppermute | solution.py:34
  28.3 6.2 %collective-permute-start.12 = (bf16[2176,128]{1,0:T(8,128)(2,1)S(1)}, bf16[2176,128]{1,0:T(8,128)(2,1)S(1)}, u32[]{:S(2)}, u32[]{:S(2)}) collective-permute-start(bf16[2176,128]{1,0:T(8,128)(2,1)S(1)} %pad_maximum_fusion.2.own.refs_0_), channel_id=1, source_target_pairs={{0,1},{1,0},{2,3},{3,2},{4,5},{5,4},{6,7},{7,6},{8,9},{9,8},{10,11... | collective-permute-start | bytes 1671176 | tf_op jit(solution)/shard_map/ppermute | solution.py:34
  28.4 15.0 %collective-permute-start.11 = (bf16[2176,128]{1,0:T(8,128)(2,1)S(1)}, bf16[2176,128]{1,0:T(8,128)(2,1)S(1)}, u32[]{:S(2)}, u32[]{:S(2)}) collective-permute-start(bf16[2176,128]{1,0:T(8,128)(2,1)S(1)} %pad_maximum_fusion.2.own.refs_0_), channel_id=1, source_target_pairs={{0,8},{1,9},{2,10},{3,11},{4,12},{5,13},{6,14},{7,15},{8,0},{9,1},... | collective-permute-start | bytes 1671176 | tf_op jit(solution)/shard_map/ppermute | solution.py:34
  31.1 3.4 %copy-start.1 = (s32[256]{0:T(256)S(1)}, s32[256]{0:T(256)}, u32[]{:S(2)}) copy-start(s32[256]{0:T(256)} %lens.3) | copy-start | bytes 3076
  31.1 15.6 %collective-permute-start.7 = (bf16[64,5120]{1,0:T(8,128)(2,1)S(1)}, bf16[64,5120]{1,0:T(8,128)(2,1)S(1)}, u32[]{:S(2)}, u32[]{:S(2)}) collective-permute-start(bf16[64,5120]{1,0:T(8,128)(2,1)S(1)} %pad_maximum_fusion.1), channel_id=1, source_target_pairs={{0,2},{1,3},{2,0},{3,1},{4,6},{5,7},{6,4},{7,5},{8,10},{9,11},{10,... | collective-permute-start | bytes 1966088 | tf_op jit(solution)/shard_map/ppermute | solution.py:34
  33.2 14.1 %collective-permute-start.3 = (bf16[64,5120]{1,0:T(8,128)(2,1)S(1)}, bf16[64,5120]{1,0:T(8,128)(2,1)S(1)}, u32[]{:S(2)}, u32[]{:S(2)}) collective-permute-start(bf16[64,5120]{1,0:T(8,128)(2,1)S(1)} %pad_maximum_fusion), channel_id=1, source_target_pairs={{0,4},{1,5},{2,6},{3,7},{4,0},{5,1},{6,2},{7,3},{8,12},{9,13},{10,... | collective-permute-start | bytes 1966088 | tf_op jit(solution)/shard_map/ppermute | solution.py:34
  34.6 18.5 %slice-start = ((s8[10485760]{0:T(1024)(128)(4,1)}), s8[4194304]{0:T(1024)(128)(4,1)S(1)}, s32[]{:S(2)}) async-start(s8[10485760]{0:T(1024)(128)(4,1)} %bitcast.3), calls=%async_computation.1 | async-start | bytes 8388608
  34.6 18.5 %slice-start.1 = ((s8[10485760]{0:T(1024)(128)(4,1)}), s8[4194304]{0:T(1024)(128)(4,1)S(1)}, s32[]{:S(2)}) async-start(s8[10485760]{0:T(1024)(128)(4,1)} %bitcast.3), calls=%async_computation.2 | async-start | bytes 8388608
  43.4 3.9 %collective-permute-start.13 = (bf16[2176,128]{1,0:T(8,128)(2,1)S(1)}, bf16[2176,128]{1,0:T(8,128)(2,1)S(1)}, u32[]{:S(2)}, u32[]{:S(2)}) collective-permute-start(bf16[2176,128]{1,0:T(8,128)(2,1)S(1)} %collective-permute-done.11.own.refs_2_), channel_id=1, source_target_pairs={{0,1},{1,0},{2,3},{3,2},{4,5},{5,4},{6,7},{7,6},{8,9},{9,8},{10,11... | collective-permute-start | bytes 1671176 | tf_op jit(solution)/shard_map/ppermute | solution.py:34
  47.3 5.8 %slice-start.2 = ((s8[10485760]{0:T(1024)(128)(4,1)}), s8[2097152]{0:T(1024)(128)(4,1)S(1)}, s32[]{:S(2)}) async-start(s8[10485760]{0:T(1024)(128)(4,1)} %bitcast.3), calls=%async_computation.3 | async-start | bytes 4194304
  47.3 5.8 %collective-permute-start.15 = (bf16[128,5120]{1,0:T(8,128)(2,1)S(1)}, bf16[128,5120]{1,0:T(8,128)(2,1)S(1)}, u32[]{:S(2)}, u32[]{:S(2)}) collective-permute-start(bf16[128,5120]{1,0:T(8,128)(2,1)S(1)} %constant_dynamic-update-slice_fusion.own), channel_id=1, source_target_pairs={{0,1},{1,0},{2,3},{3,2},{4,5},{5,4},{6,7},{7,6},{8,9},{9,8},{10,11... | collective-permute-start | bytes 3932168 | tf_op jit(solution)/shard_map/ppermute | solution.py:34
  47.4 8.6 %collective-permute-start.14 = (bf16[128,5120]{1,0:T(8,128)(2,1)S(1)}, bf16[128,5120]{1,0:T(8,128)(2,1)S(1)}, u32[]{:S(2)}, u32[]{:S(2)}) collective-permute-start(bf16[128,5120]{1,0:T(8,128)(2,1)S(1)} %constant_dynamic-update-slice_fusion.5.own), channel_id=1, source_target_pairs={{0,1},{1,0},{2,3},{3,2},{4,5},{5,4},{6,7},{7,6},{8,9},{9,8},{10,11... | collective-permute-start | bytes 3932168 | tf_op jit(solution)/shard_map/ppermute | solution.py:34

commit v4 on v3

--- a/solution.py
+++ b/solution.py
@@ -107,32 +107,44 @@
     copy.wait()
 
     spot = jnp.where((lane >= cand_at) & (lane < cand_at + cands), row * cands + lane - cand_at, -1)
-    token = ids((pt, qt), 0)
+    token = ids((pt, 2 * qt), 0)
+    right = ids((1, 2 * qt), 1) >= qt
+    empty = jnp.zeros((qt, LANES), own.dtype)
 
     def score(ref, b, at):
         tops, pairs = [], []
-        for k in range(cap):
-            entry = lst[at, k]
-            slot, pair = entry & 255, (entry >> 8) - 1
-            query = jnp.maximum(pair, 0) // cands
-            tokens = ref[pl.ds(pl.multiple_of(b * stride + query * qt, 16), qt), :]
-            sim = lax.dot_general(tiles[slot], tokens, NT, preferred_element_type=jnp.float32)
-            sim = jnp.where(token < lens[slot], sim, masked_value)
+        for k in range(0, cap, 2):
+            slots, tokens = [], []
+            for entry in (lst[at, k], lst[at, k + 1]):
+                pair = (entry >> 8) - 1
+                query = jnp.maximum(pair, 0) // cands
+                slots.append(entry & 255)
+                tokens.append(ref[pl.ds(pl.multiple_of(b * stride + query * qt, 16), qt), :])
+                pairs.append(jnp.where(pair < 0, -2, pair))
+            data = jnp.concatenate([tiles[slots[0]], tiles[slots[1]]], axis=1)
+            weights = jnp.concatenate(
+                [jnp.concatenate([tokens[0], empty], axis=1), jnp.concatenate([empty, tokens[1]], axis=1)], axis=0
+            )
+            sim = lax.dot_general(data, weights, NT, preferred_element_type=jnp.float32)
+            length = jnp.where(right, lens[slots[1]], lens[slots[0]])
+            sim = jnp.where(token < length, sim, masked_value)
             tops.append(jnp.max(sim, axis=0, keepdims=True))
-            pairs.append(jnp.where(pair < 0, -2, pair))
-        means = jnp.sum(jnp.concatenate(tops, axis=0), axis=1, keepdims=True) * (1.0 / qt)
+        tops = jnp.concatenate(tops, axis=0)
+        first = jnp.sum(jnp.where(right, 0.0, tops), axis=1, keepdims=True) * (1.0 / qt)
+        second = jnp.sum(jnp.where(right, tops, 0.0), axis=1, keepdims=True) * (1.0 / qt)
         acc = jnp.zeros((8, LANES), jnp.float32)
         for k in range(cap):
-            acc = acc + jnp.where(spot == pairs[k], means[k : k + 1, :], 0.0)
+            means = second if k % 2 else first
+            acc = acc + jnp.where(spot == pairs[k], means[k // 2 : k // 2 + 1, :], 0.0)
         out[at] = acc
 
     def step(i, carry):
-        for u in range(2):
-            score(own, 2 * i + u, 2 * i + u)
-            score(other, 2 * i + u, blocks + 2 * i + u)
+        for u in range(4):
+            score(own, 4 * i + u, 4 * i + u)
+            score(other, 4 * i + u, blocks + 4 * i + u)
         return carry
 
-    lax.fori_loop(0, blocks // 2, step, 0)
+    lax.fori_loop(0, blocks // 4, step, 0)
 
 
 def beam_kernel(own, other, doc, total):
@@ -258,7 +270,7 @@
     maxsim = [early, score(*tok[1])]
     a_other, b_other = exchange(a_own, 1, n), exchange(b_own, 1, n)
 
-    block = math.gcd(half, 1280)
+    block = half
     steps = half // block
     rows = n * 8
     full = lambda shape: pl.BlockSpec(shape, lambda i, *_: (0,) * len(shape))

time: 75.7 us -> 71.6 us (0.946)
  Pallas kernels: 20.4 us -> 15.2 us
  waiting for transfers between devices: 19.5 us -> 20.6 us
    pallas_call x2, Pallas kernels: 10.4 us -> 8.24 us  [local(): pl.pallas_call(functools.partial(maxsim_kernel, cand_at, cands, cap), out...]
    pallas_call x1, Pallas kernels: 3.58 us -> 1.8 us  [local(): pl.pallas_call(functools.partial(last_kernel, (masks, parts, cand_at, blo...]
    pallas_call x1, Pallas kernels: 2.8 us -> 1.54 us  [local(): pl.pallas_call(beam_kernel, out_shape=partial, grid=(steps,), in_specs=[l...]
    ppermute x16, waiting for transfers between devices: 19.5 us -> 20.6 us  [exchange(): return lax.ppermute(x, 'dom', [(i, i ^ bit) for i in range(n)])]
  transfers between devices with their start and end apart: 16 -> 16, of which waited for: 10 -> 10; matrix products, arithmetic and copies ran while one was open for 3% -> 3% of each run, Pallas kernels for 17% -> 14%
where the time goes in v4:
time: 71.6 us; the launch traced here: 71.3 us
  waiting for transfers between devices  20.6 us (29%)
  starting transfers between devices  18.1 us (25%)
  Pallas kernels  15.2 us (21%)
  blocking collectives  14.3 us (20%)
  local copies, waits for them, and re-layouts  1.15 us (2%)
  other arithmetic  1.11 us (2%)
  between operations  0.9 us (1%)
    ppermute x16, waiting for transfers between devices, exchange(): return lax.ppermute(x, 'dom', [(i, i ^ bit) for i in range(n)])  20.6 us
    ppermute x16, starting transfers between devices, exchange(): return lax.ppermute(x, 'dom', [(i, i ^ bit) for i in range(n)])  18.1 us
    all_to_all x1, blocking collectives, local(): lax.all_to_all(scored, 'dom', split_axis=0, concat_axis=0, tiled=True)  14.3 us
    pallas_call x2, Pallas kernels, local(): pl.pallas_call(functools.partial(maxsim_kernel, cand_at, cands, cap), out...  8.24 us
    pallas_call x1, Pallas kernels, local(): pl.pallas_call(functools.partial(prep_kernel, parts, slots, cap), out_sha...  2.01 us
    pallas_call x1, Pallas kernels, local(): pl.pallas_call(functools.partial(last_kernel, (masks, parts, cand_at, blo...  1.8 us
    pallas_call x1, Pallas kernels, local(): pl.pallas_call(functools.partial(sum_kernel, rounds, front, cands), out_s...  1.61 us
    pallas_call x1, Pallas kernels, local(): pl.pallas_call(beam_kernel, out_shape=partial, grid=(steps,), in_specs=[l...  1.54 us
  transfers between devices with their start and end apart: 16, of which 10 were waited for; matrix products, arithmetic and copies ran while one was open for 3% of the time, Pallas kernels for 14%

profile of v4, /device:TPU:0, one launch (start us, length us, event | category | flops | bytes accessed | tf_op | source)
XLA Modules:
  0.0 71.3 jit_solution(14216698099885633254)
XLA Ops:
  0.6 2.0 %pack.1 = bf16[272,128]{1,0:T(8,128)(2,1)} custom-call(s32[3,8,16]{2,1,0:T(8,128)} %fo.1, s32[3,8,16]{2,1,0:T(8,128)} %fs.1, s32[8,32]{1,0:T(8,128)} %bitcast.6, s32[8,32]{1,0:T(8,128)} %cs.1, bf16[256,128]{1,0:T(8,128)(2,1)} %bitcast.5), custom_call_target="tpu_custom_call" | custom-call | tf_op jit(solution)/shard_map/pack/pallas_call | solution.py:218
  2.6 4.0 %collective-permute-start.8 = (bf16[272,128]{1,0:T(8,128)(2,1)}, bf16[272,128]{1,0:T(8,128)(2,1)S(1)}, u32[]{:S(2)}, u32[]{:S(2)}) collective-permute-start(bf16[272,128]{1,0:T(8,128)(2,1)} %pack.1), channel_id=1, source_target_pairs={{0,16},{1,17},{2,18},{3,19},{4,20},{5,21},{6,22},{7,23},{8,24},{9,... | collective-permute-start | bytes 208904 | tf_op jit(solution)/shard_map/ppermute | solution.py:34
  6.7 0.9 %fusion = (bf16[8,5120]{1,0:T(8,128)(2,1)S(1)}, bf16[128,5120]{1,0:T(8,128)(2,1)S(1)}, bf16[128,5120]{1,0:T(8,128)(2,1)S(1)}, bf16[8,5120]{1,0:T(8,128)(2,1)S(1)}) fusion(bf16[8,10240]{1,0:T(8,128)(2,1)} %param.9), kind=kLoop, calls=%fused_computation.19 | loop fusion | bytes 491520 | tf_op jit(solution)/shard_map/slice | solution.py:226
  7.6 0.1 collective-permute-start.4
  7.7 2.9 %collective-permute-start = (bf16[8,5120]{1,0:T(8,128)(2,1)S(1)}, bf16[8,5120]{1,0:T(8,128)(2,1)S(1)}, u32[]{:S(2)}, u32[]{:S(2)}) collective-permute-start(bf16[8,5120]{1,0:T(8,128)(2,1)S(1)} %get-tuple-element.15), channel_id=1, source_target_pairs={{0,16},{1,17},{2,18},{3,19},{4,20},{5,21},{6,22},{7,23},{8,24},{9,... | collective-permute-start | bytes 245768 | tf_op jit(solution)/shard_map/ppermute | solution.py:34
  10.6 0.1 collective-permute-done.8
  10.7 0.9 %pad_maximum_fusion.8 = bf16[544,128]{1,0:T(8,128)(2,1)S(1)} fusion(bf16[272,128]{1,0:T(8,128)(2,1)S(1)} %collective-permute-done.8, bf16[272,128]{1,0:T(8,128)(2,1)} %pack.1), kind=kLoop, calls=%fused_computation.8 | loop fusion | flops 278528 | bytes 278528 | tf_op jit(solution)/shard_map/concatenate | solution.py:233
  11.6 1.8 %collective-permute-start.9 = (bf16[544,128]{1,0:T(8,128)(2,1)S(1)}, bf16[544,128]{1,0:T(8,128)(2,1)S(1)}, u32[]{:S(2)}, u32[]{:S(2)}) collective-permute-start(bf16[544,128]{1,0:T(8,128)(2,1)S(1)} %pad_maximum_fusion.8), channel_id=1, source_target_pairs={{0,2},{1,3},{2,0},{3,1},{4,6},{5,7},{6,4},{7,5},{8,10},{9,11},{10,... | collective-permute-start | bytes 417800 | tf_op jit(solution)/shard_map/ppermute | solution.py:34
  13.4 3.5 %collective-permute-done.4 = bf16[8,5120]{1,0:T(8,128)(2,1)S(1)} collective-permute-done((bf16[8,5120]{1,0:T(8,128)(2,1)S(1)}, bf16[8,5120]{1,0:T(8,128)(2,1)S(1)}, u32[]{:S(2)}, u32[]{:S(2)}) %collective-permute-start.4) | collective-permute-done | bytes 81952 | tf_op jit(solution)/shard_map/ppermute | solution.py:34
  16.9 1.7 %collective-permute-start.5 = (bf16[16,5120]{1,0:T(8,128)(2,1)S(1)}, bf16[16,5120]{1,0:T(8,128)(2,1)S(1)}, u32[]{:S(2)}, u32[]{:S(2)}) collective-permute-start(bf16[16,5120]{1,0:T(8,128)(2,1)S(1)} %pad_maximum_fusion.7), channel_id=1, source_target_pairs={{0,4},{1,5},{2,6},{3,7},{4,0},{5,1},{6,2},{7,3},{8,12},{9,13},{10,... | collective-permute-start | bytes 491528 | tf_op jit(solution)/shard_map/ppermute | solution.py:34
  18.7 0.5 collective-permute-start.1
  19.2 0.8 %collective-permute-start.10 = (bf16[1088,128]{1,0:T(8,128)(2,1)S(1)}, bf16[1088,128]{1,0:T(8,128)(2,1)S(1)}, u32[]{:S(2)}, u32[]{:S(2)}) collective-permute-start(bf16[1088,128]{1,0:T(8,128)(2,1)S(1)} %pad_maximum_fusion.5), channel_id=1, source_target_pairs={{0,4},{1,5},{2,6},{3,7},{4,0},{5,1},{6,2},{7,3},{8,12},{9,13},{10,... | collective-permute-start | bytes 835592 | tf_op jit(solution)/shard_map/ppermute | solution.py:34
  20.0 3.7 %collective-permute-done.5 = bf16[16,5120]{1,0:T(8,128)(2,1)S(1)} collective-permute-done((bf16[16,5120]{1,0:T(8,128)(2,1)S(1)}, bf16[16,5120]{1,0:T(8,128)(2,1)S(1)}, u32[]{:S(2)}, u32[]{:S(2)}) %collective-permute-start.5) | collective-permute-done | bytes 163872 | tf_op jit(solution)/shard_map/ppermute | solution.py:34
  23.8 1.7 %collective-permute-done.1 = bf16[16,5120]{1,0:T(8,128)(2,1)S(1)} collective-permute-done((bf16[16,5120]{1,0:T(8,128)(2,1)S(1)}, bf16[16,5120]{1,0:T(8,128)(2,1)S(1)}, u32[]{:S(2)}, u32[]{:S(2)}) %collective-permute-start.1) | collective-permute-done | bytes 163872 | tf_op jit(solution)/shard_map/ppermute | solution.py:34
  25.5 1.6 %collective-permute-start.2 = (bf16[32,5120]{1,0:T(8,128)(2,1)S(1)}, bf16[32,5120]{1,0:T(8,128)(2,1)S(1)}, u32[]{:S(2)}, u32[]{:S(2)}) collective-permute-start(bf16[32,5120]{1,0:T(8,128)(2,1)S(1)} %pad_maximum_fusion.3), channel_id=1, source_target_pairs={{0,2},{1,3},{2,0},{3,1},{4,6},{5,7},{6,4},{7,5},{8,10},{9,11},{10,... | collective-permute-start | bytes 983048 | tf_op jit(solution)/shard_map/ppermute | solution.py:34
  27.1 1.1 %collective-permute-done.10 = bf16[1088,128]{1,0:T(8,128)(2,1)S(1)} collective-permute-done((bf16[1088,128]{1,0:T(8,128)(2,1)S(1)}, bf16[1088,128]{1,0:T(8,128)(2,1)S(1)}, u32[]{:S(2)}, u32[]{:S(2)}) %collective-permute-start.10) | collective-permute-done | bytes 278560 | tf_op jit(solution)/shard_map/ppermute | solution.py:34
  28.3 0.1 collective-permute-start.12
  28.4 0.9 %collective-permute-start.11 = (bf16[2176,128]{1,0:T(8,128)(2,1)S(1)}, bf16[2176,128]{1,0:T(8,128)(2,1)S(1)}, u32[]{:S(2)}, u32[]{:S(2)}) collective-permute-start(bf16[2176,128]{1,0:T(8,128)(2,1)S(1)} %pad_maximum_fusion.2.own.refs_0_), channel_id=1, source_target_pairs={{0,8},{1,9},{2,10},{3,11},{4,12},{5,13},{6,14},{7,15},{8,0},{9,1},... | collective-permute-start | bytes 1671176 | tf_op jit(solution)/shard_map/ppermute | solution.py:34
  29.3 1.8 %collective-permute-done.6 = bf16[32,5120]{1,0:T(8,128)(2,1)S(1)} collective-permute-done((bf16[32,5120]{1,0:T(8,128)(2,1)S(1)}, bf16[32,5120]{1,0:T(8,128)(2,1)S(1)}, u32[]{:S(2)}, u32[]{:S(2)}) %collective-permute-start.6) | collective-permute-done | bytes 327712 | tf_op jit(solution)/shard_map/ppermute | solution.py:34
  31.1 1.7 %collective-permute-start.7 = (bf16[64,5120]{1,0:T(8,128)(2,1)S(1)}, bf16[64,5120]{1,0:T(8,128)(2,1)S(1)}, u32[]{:S(2)}, u32[]{:S(2)}) collective-permute-start(bf16[64,5120]{1,0:T(8,128)(2,1)S(1)} %pad_maximum_fusion.1), channel_id=1, source_target_pairs={{0,2},{1,3},{2,0},{3,1},{4,6},{5,7},{6,4},{7,5},{8,10},{9,11},{10,... | collective-permute-start | bytes 1966088 | tf_op jit(solution)/shard_map/ppermute | solution.py:34
  32.8 0.3 collective-permute-done.2
  33.2 1.3 %collective-permute-start.3 = (bf16[64,5120]{1,0:T(8,128)(2,1)S(1)}, bf16[64,5120]{1,0:T(8,128)(2,1)S(1)}, u32[]{:S(2)}, u32[]{:S(2)}) collective-permute-start(bf16[64,5120]{1,0:T(8,128)(2,1)S(1)} %pad_maximum_fusion), channel_id=1, source_target_pairs={{0,4},{1,5},{2,6},{3,7},{4,0},{5,1},{6,2},{7,3},{8,12},{9,13},{10,... | collective-permute-start | bytes 1966088 | tf_op jit(solution)/shard_map/ppermute | solution.py:34
  34.6 4.1 %maxsim.2.refs_4_ = f32[16,8,128]{2,1,0:T(8,128)S(1)} custom-call(s32[1]{0:T(128)} %bitcast.me_ref, s32[256]{0:T(256)S(1)} %copy-done.1, bf16[2176,128]{1,0:T(8,128)(2,1)S(1)} %pad_maximum_fusion.2.own.refs_0_, bf16[2176,128]{1,0:T(8,128)(2,1)S(1)} %collective-permute-done.12.other.refs_1_, bf16[256,128,128]{2,1,0:T(8,128)(2,1)S(1)} %copy-done), custom_call_target="tpu_custom_call" | custom-call | flops 2147483648 | bytes 8388608 | tf_op jit(solution)/shard_map/maxsim/pallas_call | solution.py:246
  38.7 4.7 %collective-permute-done.11.own.refs_2_ = bf16[2176,128]{1,0:T(8,128)(2,1)S(1)} collective-permute-done((bf16[2176,128]{1,0:T(8,128)(2,1)S(1)}, bf16[2176,128]{1,0:T(8,128)(2,1)S(1)}, u32[]{:S(2)}, u32[]{:S(2)}) %collective-permute-start.11) | collective-permute-done | bytes 557088 | tf_op jit(solution)/shard_map/ppermute | solution.py:34
  43.4 3.3 %collective-permute-done.7 = bf16[64,5120]{1,0:T(8,128)(2,1)S(1)} collective-permute-done((bf16[64,5120]{1,0:T(8,128)(2,1)S(1)}, bf16[64,5120]{1,0:T(8,128)(2,1)S(1)}, u32[]{:S(2)}, u32[]{:S(2)}) %collective-permute-start.7) | collective-permute-done | bytes 655392 | tf_op jit(solution)/shard_map/ppermute | solution.py:34
  46.8 0.5 collective-permute-done.3
  47.4 0.5 collective-permute-start.14
  47.9 4.1 %maxsim.3.refs_5_ = f32[16,8,128]{2,1,0:T(8,128)S(1)} custom-call(s32[1]{0:T(128)} %bitcast.me_ref, s32[256]{0:T(256)S(1)} %copy-done.1, bf16[2176,128]{1,0:T(8,128)(2,1)S(1)} %collective-permute-done.11.own.refs_2_, bf16[2176,128]{1,0:T(8,128)(2,1)S(1)} %collective-permute-done.13.other.refs_3_, bf16[256,128,128]{2,1,0:T(8,128)(2,1)S(1)} %copy-done), custom_call_target="tpu_custom_call" | custom-call | flops 2147483648 | bytes 8388608 | tf_op jit(solution)/shard_map/maxsim/pallas_call | solution.py:246
  52.1 1.5 %beam.1.first = f32[256,512]{1,0:T(8,128)S(1)} custom-call(bf16[128,5120]{1,0:T(8,128)(2,1)S(1)} %constant_dynamic-update-slice_fusion.own, bf16[128,5120]{1,0:T(8,128)(2,1)S(1)} %collective-permute-done.15.other, bf16[512,10240]{1,0:T(8,128)(2,1)S(1)} %bitcast.4), custom_call_target="tpu_custom_call" | custom-call | flops 1342177280 | bytes 7864320 | tf_op jit(solution)/shard_map/beam/pallas_call | solution.py:281
  53.6 1.8 %beam_last.1 = f32[32,8,128]{2,1,0:T(8,128)S(1)} custom-call(s32[1]{0:T(128)} %bitcast.me_ref, bf16[128,5120]{1,0:T(8,128)(2,1)S(1)} %constant_dynamic-update-slice_fusion.5.own, bf16[128,5120]{1,0:T(8,128)(2,1)S(1)} %collective-permute-done.14.other, bf16[512,10240]{1,0:T(8,128)(2,1)S(1)} %bitcast.4, f32[256,512]{1,0:T(8,128)S(1)} %beam.1.first, ...), custom_call_target="tpu_custom_call" | custom-call | flops 1342177280 | bytes 7864320 | tf_op jit(solution)/shard_map/beam_last/pallas_call | solution.py:292
  55.4 14.3 %all_to_all.5.parts = f32[32,8,128]{2,1,0:T(8,128)} all-to-all(f32[32,8,128]{2,1,0:T(8,128)S(1)} %beam_last.1), channel_id=1, replica_groups=mesh['dom'=32,'rep'=1] {'dom'}, dimensions={0} | all-to-all | bytes 262144 | tf_op jit(solution)/shard_map/all_to_all | solution.py:307
  69.7 1.6 %collect.1 = (f32[3,8,16]{2,1,0:T(8,128)}, f32[8,32]{1,0:T(8,128)}) custom-call(f32[32,8,128]{2,1,0:T(8,128)} %all_to_all.5.parts), custom_call_target="tpu_custom_call" | custom-call | tf_op jit(solution)/shard_map/collect/pallas_call | solution.py:308
  (38 shorter events, 0.6 us)
Async XLA Ops:
  2.6 16.5 %copy-start.2 = (bf16[272,128]{1,0:T(8,128)(2,1)S(1)}, bf16[272,128]{1,0:T(8,128)(2,1)}, u32[]{:S(2)}) copy-start(bf16[272,128]{1,0:T(8,128)(2,1)} %pack.1) | copy-start | bytes 208900
  2.6 8.1 %collective-permute-start.8 = (bf16[272,128]{1,0:T(8,128)(2,1)}, bf16[272,128]{1,0:T(8,128)(2,1)S(1)}, u32[]{:S(2)}, u32[]{:S(2)}) collective-permute-start(bf16[272,128]{1,0:T(8,128)(2,1)} %pack.1), channel_id=1, source_target_pairs={{0,16},{1,17},{2,18},{3,19},{4,20},{5,21},{6,22},{7,23},{8,24},{9,... | collective-permute-start | bytes 208904 | tf_op jit(solution)/shard_map/ppermute | solution.py:34
  7.6 9.3 %collective-permute-start.4 = (bf16[8,5120]{1,0:T(8,128)(2,1)S(1)}, bf16[8,5120]{1,0:T(8,128)(2,1)S(1)}, u32[]{:S(2)}, u32[]{:S(2)}) collective-permute-start(bf16[8,5120]{1,0:T(8,128)(2,1)S(1)} %get-tuple-element.12), channel_id=1, source_target_pairs={{0,16},{1,17},{2,18},{3,19},{4,20},{5,21},{6,22},{7,23},{8,24},{9,... | collective-permute-start | bytes 245768 | tf_op jit(solution)/shard_map/ppermute | solution.py:34
  7.7 10.9 %collective-permute-start = (bf16[8,5120]{1,0:T(8,128)(2,1)S(1)}, bf16[8,5120]{1,0:T(8,128)(2,1)S(1)}, u32[]{:S(2)}, u32[]{:S(2)}) collective-permute-start(bf16[8,5120]{1,0:T(8,128)(2,1)S(1)} %get-tuple-element.15), channel_id=1, source_target_pairs={{0,16},{1,17},{2,18},{3,19},{4,20},{5,21},{6,22},{7,23},{8,24},{9,... | collective-permute-start | bytes 245768 | tf_op jit(solution)/shard_map/ppermute | solution.py:34
  11.6 7.5 %collective-permute-start.9 = (bf16[544,128]{1,0:T(8,128)(2,1)S(1)}, bf16[544,128]{1,0:T(8,128)(2,1)S(1)}, u32[]{:S(2)}, u32[]{:S(2)}) collective-permute-start(bf16[544,128]{1,0:T(8,128)(2,1)S(1)} %pad_maximum_fusion.8), channel_id=1, source_target_pairs={{0,2},{1,3},{2,0},{3,1},{4,6},{5,7},{6,4},{7,5},{8,10},{9,11},{10,... | collective-permute-start | bytes 417800 | tf_op jit(solution)/shard_map/ppermute | solution.py:34
  16.9 17.7 %copy-start = (bf16[256,128,128]{2,1,0:T(8,128)(2,1)S(1)}, bf16[256,128,128]{2,1,0:T(8,128)(2,1)}, u32[]{:S(2)}) copy-start(bf16[256,128,128]{2,1,0:T(8,128)(2,1)} %tiles.3) | copy-start | bytes 25165828
  16.9 6.8 %collective-permute-start.5 = (bf16[16,5120]{1,0:T(8,128)(2,1)S(1)}, bf16[16,5120]{1,0:T(8,128)(2,1)S(1)}, u32[]{:S(2)}, u32[]{:S(2)}) collective-permute-start(bf16[16,5120]{1,0:T(8,128)(2,1)S(1)} %pad_maximum_fusion.7), channel_id=1, source_target_pairs={{0,4},{1,5},{2,6},{3,7},{4,0},{5,1},{6,2},{7,3},{8,12},{9,13},{10,... | collective-permute-start | bytes 491528 | tf_op jit(solution)/shard_map/ppermute | solution.py:34
  18.7 6.8 %collective-permute-start.1 = (bf16[16,5120]{1,0:T(8,128)(2,1)S(1)}, bf16[16,5120]{1,0:T(8,128)(2,1)S(1)}, u32[]{:S(2)}, u32[]{:S(2)}) collective-permute-start(bf16[16,5120]{1,0:T(8,128)(2,1)S(1)} %pad_maximum_fusion.6), channel_id=1, source_target_pairs={{0,8},{1,9},{2,10},{3,11},{4,12},{5,13},{6,14},{7,15},{8,0},{9,1},... | collective-permute-start | bytes 491528 | tf_op jit(solution)/shard_map/ppermute | solution.py:34
  19.2 9.0 %collective-permute-start.10 = (bf16[1088,128]{1,0:T(8,128)(2,1)S(1)}, bf16[1088,128]{1,0:T(8,128)(2,1)S(1)}, u32[]{:S(2)}, u32[]{:S(2)}) collective-permute-start(bf16[1088,128]{1,0:T(8,128)(2,1)S(1)} %pad_maximum_fusion.5), channel_id=1, source_target_pairs={{0,4},{1,5},{2,6},{3,7},{4,0},{5,1},{6,2},{7,3},{8,12},{9,13},{10,... | collective-permute-start | bytes 835592 | tf_op jit(solution)/shard_map/ppermute | solution.py:34
  23.8 7.3 %collective-permute-start.6 = (bf16[32,5120]{1,0:T(8,128)(2,1)S(1)}, bf16[32,5120]{1,0:T(8,128)(2,1)S(1)}, u32[]{:S(2)}, u32[]{:S(2)}) collective-permute-start(bf16[32,5120]{1,0:T(8,128)(2,1)S(1)} %pad_maximum_fusion.4), channel_id=1, source_target_pairs={{0,8},{1,9},{2,10},{3,11},{4,12},{5,13},{6,14},{7,15},{8,0},{9,1},... | collective-permute-start | bytes 983048 | tf_op jit(solution)/shard_map/ppermute | solution.py:34
  25.5 7.6 %collective-permute-start.2 = (bf16[32,5120]{1,0:T(8,128)(2,1)S(1)}, bf16[32,5120]{1,0:T(8,128)(2,1)S(1)}, u32[]{:S(2)}, u32[]{:S(2)}) collective-permute-start(bf16[32,5120]{1,0:T(8,128)(2,1)S(1)} %pad_maximum_fusion.3), channel_id=1, source_target_pairs={{0,2},{1,3},{2,0},{3,1},{4,6},{5,7},{6,4},{7,5},{8,10},{9,11},{10,... | collective-permute-start | bytes 983048 | tf_op jit(solution)/shard_map/ppermute | solution.py:34
  28.3 6.2 %collective-permute-start.12 = (bf16[2176,128]{1,0:T(8,128)(2,1)S(1)}, bf16[2176,128]{1,0:T(8,128)(2,1)S(1)}, u32[]{:S(2)}, u32[]{:S(2)}) collective-permute-start(bf16[2176,128]{1,0:T(8,128)(2,1)S(1)} %pad_maximum_fusion.2.own.refs_0_), channel_id=1, source_target_pairs={{0,1},{1,0},{2,3},{3,2},{4,5},{5,4},{6,7},{7,6},{8,9},{9,8},{10,11... | collective-permute-start | bytes 1671176 | tf_op jit(solution)/shard_map/ppermute | solution.py:34
  28.4 15.0 %collective-permute-start.11 = (bf16[2176,128]{1,0:T(8,128)(2,1)S(1)}, bf16[2176,128]{1,0:T(8,128)(2,1)S(1)}, u32[]{:S(2)}, u32[]{:S(2)}) collective-permute-start(bf16[2176,128]{1,0:T(8,128)(2,1)S(1)} %pad_maximum_fusion.2.own.refs_0_), channel_id=1, source_target_pairs={{0,8},{1,9},{2,10},{3,11},{4,12},{5,13},{6,14},{7,15},{8,0},{9,1},... | collective-permute-start | bytes 1671176 | tf_op jit(solution)/shard_map/ppermute | solution.py:34
  31.1 3.4 %copy-start.1 = (s32[256]{0:T(256)S(1)}, s32[256]{0:T(256)}, u32[]{:S(2)}) copy-start(s32[256]{0:T(256)} %lens.3) | copy-start | bytes 3076
  31.1 15.6 %collective-permute-start.7 = (bf16[64,5120]{1,0:T(8,128)(2,1)S(1)}, bf16[64,5120]{1,0:T(8,128)(2,1)S(1)}, u32[]{:S(2)}, u32[]{:S(2)}) collective-permute-start(bf16[64,5120]{1,0:T(8,128)(2,1)S(1)} %pad_maximum_fusion.1), channel_id=1, source_target_pairs={{0,2},{1,3},{2,0},{3,1},{4,6},{5,7},{6,4},{7,5},{8,10},{9,11},{10,... | collective-permute-start | bytes 1966088 | tf_op jit(solution)/shard_map/ppermute | solution.py:34
  33.2 14.1 %collective-permute-start.3 = (bf16[64,5120]{1,0:T(8,128)(2,1)S(1)}, bf16[64,5120]{1,0:T(8,128)(2,1)S(1)}, u32[]{:S(2)}, u32[]{:S(2)}) collective-permute-start(bf16[64,5120]{1,0:T(8,128)(2,1)S(1)} %pad_maximum_fusion), channel_id=1, source_target_pairs={{0,4},{1,5},{2,6},{3,7},{4,0},{5,1},{6,2},{7,3},{8,12},{9,13},{10,... | collective-permute-start | bytes 1966088 | tf_op jit(solution)/shard_map/ppermute | solution.py:34
  34.6 17.5 %slice-start = ((s8[10485760]{0:T(1024)(128)(4,1)}), s8[4194304]{0:T(1024)(128)(4,1)S(1)}, s32[]{:S(2)}) async-start(s8[10485760]{0:T(1024)(128)(4,1)} %bitcast.3), calls=%async_computation.1 | async-start | bytes 8388608
  34.6 17.5 %slice-start.1 = ((s8[10485760]{0:T(1024)(128)(4,1)}), s8[4194304]{0:T(1024)(128)(4,1)S(1)}, s32[]{:S(2)}) async-start(s8[10485760]{0:T(1024)(128)(4,1)} %bitcast.3), calls=%async_computation.2 | async-start | bytes 8388608
  43.4 3.9 %collective-permute-start.13 = (bf16[2176,128]{1,0:T(8,128)(2,1)S(1)}, bf16[2176,128]{1,0:T(8,128)(2,1)S(1)}, u32[]{:S(2)}, u32[]{:S(2)}) collective-permute-start(bf16[2176,128]{1,0:T(8,128)(2,1)S(1)} %collective-permute-done.11.own.refs_2_), channel_id=1, source_target_pairs={{0,1},{1,0},{2,3},{3,2},{4,5},{5,4},{6,7},{7,6},{8,9},{9,8},{10,11... | collective-permute-start | bytes 1671176 | tf_op jit(solution)/shard_map/ppermute | solution.py:34
  47.3 4.8 %slice-start.2 = ((s8[10485760]{0:T(1024)(128)(4,1)}), s8[2097152]{0:T(1024)(128)(4,1)S(1)}, s32[]{:S(2)}) async-start(s8[10485760]{0:T(1024)(128)(4,1)} %bitcast.3), calls=%async_computation.3 | async-start | bytes 4194304
  47.3 4.7 %collective-permute-start.15 = (bf16[128,5120]{1,0:T(8,128)(2,1)S(1)}, bf16[128,5120]{1,0:T(8,128)(2,1)S(1)}, u32[]{:S(2)}, u32[]{:S(2)}) collective-permute-start(bf16[128,5120]{1,0:T(8,128)(2,1)S(1)} %constant_dynamic-update-slice_fusion.own), channel_id=1, source_target_pairs={{0,1},{1,0},{2,3},{3,2},{4,5},{5,4},{6,7},{7,6},{8,9},{9,8},{10,11... | collective-permute-start | bytes 3932168 | tf_op jit(solution)/shard_map/ppermute | solution.py:34
  47.4 6.2 %collective-permute-start.14 = (bf16[128,5120]{1,0:T(8,128)(2,1)S(1)}, bf16[128,5120]{1,0:T(8,128)(2,1)S(1)}, u32[]{:S(2)}, u32[]{:S(2)}) collective-permute-start(bf16[128,5120]{1,0:T(8,128)(2,1)S(1)} %constant_dynamic-update-slice_fusion.5.own), channel_id=1, source_target_pairs={{0,1},{1,0},{2,3},{3,2},{4,5},{5,4},{6,7},{7,6},{8,9},{9,8},{10,11... | collective-permute-start | bytes 3932168 | tf_op jit(solution)/shard_map/ppermute | solution.py:34

commit v5 on v4

--- a/solution.py
+++ b/solution.py
@@ -87,15 +87,16 @@
     out[rows:, :] = jnp.concatenate([codes, table], axis=0).astype(jnp.bfloat16)
 
 
-def maxsim_kernel(cand_at, cands, cap, me_ref, lens, own, other, tiles, out, listed, lst, sem):
-    blocks = out.shape[0] // 2
-    stride = own.shape[0] // blocks
+def maxsim_kernel(cand_at, cands, cap, me_ref, lens, *refs):
+    *sides, tiles, out, listed, lst, sem = refs
+    blocks = out.shape[0] // len(sides)
+    stride = sides[0].shape[0] // blocks
     pt = tiles.shape[1]
     qt = (stride - 16) // 8
     start = me_ref[0] * cap
     row, lane = ids((8, LANES), 0), ids((8, LANES), 1)
     group = start // LANES
-    for side, ref in enumerate((own, other)):
+    for side, ref in enumerate(sides):
         for b in range(blocks):
             table = ref[(b + 1) * stride - 16 : (b + 1) * stride, :].astype(jnp.float32)[8:]
             weight = jnp.where(row == 2 * group, 256.0, jnp.where(row == 2 * group + 1, 1.0, 0.0))
@@ -109,7 +110,7 @@
     spot = jnp.where((lane >= cand_at) & (lane < cand_at + cands), row * cands + lane - cand_at, -1)
     token = ids((pt, 2 * qt), 0)
     right = ids((1, 2 * qt), 1) >= qt
-    empty = jnp.zeros((qt, LANES), own.dtype)
+    empty = jnp.zeros((qt, LANES), sides[0].dtype)
 
     def score(ref, b, at):
         tops, pairs = [], []
@@ -138,13 +139,15 @@
             acc = acc + jnp.where(spot == pairs[k], means[k // 2 : k // 2 + 1, :], 0.0)
         out[at] = acc
 
+    together = 8 // len(sides)
+
     def step(i, carry):
-        for u in range(4):
-            score(own, 4 * i + u, 4 * i + u)
-            score(other, 4 * i + u, blocks + 4 * i + u)
+        for u in range(together):
+            for side, ref in enumerate(sides):
+                score(ref, together * i + u, side * blocks + together * i + u)
         return carry
 
-    lax.fori_loop(0, blocks // 4, step, 0)
+    lax.fori_loop(0, blocks // together, step, 0)
 
 
 def beam_kernel(own, other, doc, total):
@@ -158,7 +161,7 @@
 
 def last_kernel(cfg, me_ref, own, other, doc, first, *refs):
     masks, parts, cand_at, blocks = cfg
-    codes, scores, out, last = refs[:4], refs[4:6], refs[6], refs[7]
+    codes, scores, out, last = refs[:4], refs[4:7], refs[7], refs[8]
     stride = codes[0].shape[0] // blocks
     beam_kernel(own, other, doc, last)
 
@@ -184,7 +187,7 @@
                     here = jnp.take_along_axis(rows[:, g * LANES : (g + 1) * LANES], within, axis=1)
                     found = jnp.where(page == g, here, found)
                 found = jnp.where(owner == me, found, 0.0)
-                out[me ^ (m + side)] = jnp.where(lane < cand_at, found, scores[half][side * blocks + t])
+                out[me ^ (m + side)] = jnp.where(lane < cand_at, found, (scores[0][side * blocks + t] if half == 0 else scores[1 + side][t]))
 
 
 def sum_kernel(rounds, front, cands, parts, beam, maxsim):
@@ -215,6 +218,10 @@
     cap = max(2, min(pairs_count, 2 * pairs_count // n))
     slots = n * cap
     assert slots % LANES == 0 and slots <= 4 * LANES and LANES % cap == 0 and pairs_count <= 256
+    half = fde // 2
+    query_tokens, left_part, right_part = lax.optimization_barrier(
+        (query_tokens, query_fde[:, :half], query_fde[:, half:])
+    )
     packed = pl.pallas_call(
         functools.partial(prep_kernel, parts, slots, cap),
         out_shape=jax.ShapeDtypeStruct((stride, dim), jnp.bfloat16),
@@ -222,8 +229,7 @@
         out_specs=VMEM,
         name="pack",
     )(frontier_owner, frontier_slot, cand_owner.reshape(queries, cands), cand_slot, query_tokens.reshape(queries * qt, dim))
-    half = fde // 2
-    starts = [packed, query_fde[:, :half], query_fde[:, half:]]
+    starts = [packed, left_part, right_part]
     stages = len(orders[0])
 
     @functools.cache
@@ -243,31 +249,32 @@
     tok = [(tok[0], exchange(tok[0], 1, n)), tok[1]]
 
     pt = passage_tiles.shape[1]
-    score = lambda own, other: pl.pallas_call(
+    score = lambda *sides: pl.pallas_call(
             functools.partial(maxsim_kernel, cand_at, cands, cap),
-            out_shape=jax.ShapeDtypeStruct((n // 2, 8, LANES), jnp.float32),
+            out_shape=jax.ShapeDtypeStruct((n // 4 * len(sides), 8, LANES), jnp.float32),
             grid_spec=pltpu.PrefetchScalarGridSpec(
                 num_scalar_prefetch=2,
                 grid=(),
-                in_specs=[VMEM] * 3,
+                in_specs=[VMEM] * (len(sides) + 1),
                 out_specs=VMEM,
                 scratch_shapes=[
-                    pltpu.VMEM((n // 2, LANES), jnp.int32),
-                    pltpu.SMEM((n // 2, LANES), jnp.int32),
+                    pltpu.VMEM((n // 4 * len(sides), LANES), jnp.int32),
+                    pltpu.SMEM((n // 4 * len(sides), LANES), jnp.int32),
                     pltpu.SemaphoreType.DMA,
                 ],
             ),
             compiler_params=pltpu.CompilerParams(vmem_limit_bytes=16 << 20),
-            cost_estimate=pl.CostEstimate(flops=8 * slots * pt * qt * dim, bytes_accessed=8 << 20, transcendentals=0),
+            cost_estimate=pl.CostEstimate(flops=4 * len(sides) * slots * pt * qt * dim, bytes_accessed=8 << 20, transcendentals=0),
             name="maxsim",
-        )(me.reshape(1), passage_len, own, other, passage_tiles)
+        )(me.reshape(1), passage_len, *sides, passage_tiles)
 
     early = score(*tok[0])
     late, early = lax.optimization_barrier((tok[1], early))
     late_other = exchange(late, 1, n)
-    a_own, b_own, late_other = lax.optimization_barrier((gathered(1, stages), gathered(2, stages), late_other))
+    maxsim = [early, score(late)]
+    a_own, b_own, late_other, _ = lax.optimization_barrier((gathered(1, stages), gathered(2, stages), late_other, maxsim[1]))
     tok = [tok[0], (late, late_other)]
-    maxsim = [early, score(*tok[1])]
+    maxsim.append(score(late_other))
     a_other, b_other = exchange(a_own, 1, n), exchange(b_own, 1, n)
 
     block = half

time: 71.6 us -> 69.5 us (0.971)
  starting transfers between devices: 18.1 us -> 13.6 us
  waiting for transfers between devices: 20.6 us -> 24.3 us
  blocking collectives: 14.3 us -> 11.7 us
  Pallas kernels: 15.2 us -> 16.4 us
    ppermute x16, starting transfers between devices: 18.1 us -> 13.6 us  [exchange(): return lax.ppermute(x, 'dom', [(i, i ^ bit) for i in range(n)])]
    ppermute x16, waiting for transfers between devices: 20.6 us -> 24.3 us  [exchange(): return lax.ppermute(x, 'dom', [(i, i ^ bit) for i in range(n)])]
    all_to_all x1, blocking collectives: 14.3 us -> 11.7 us  [local(): lax.all_to_all(scored, 'dom', split_axis=0, concat_axis=0, tiled=True)]
    pallas_call x2 -> x3, Pallas kernels: 8.24 us -> 9.46 us  [local(): pl.pallas_call(functools.partial(maxsim_kernel, cand_at, cands, cap), out...]
  transfers between devices with their start and end apart: 16 -> 16, of which waited for: 10 -> 10; matrix products, arithmetic and copies ran while one was open for 3% -> 2% of each run, Pallas kernels for 14% -> 19%
where the time goes in v5:
time: 69.5 us; the launch traced here: 69.2 us
  waiting for transfers between devices  24.3 us (35%)
  Pallas kernels  16.4 us (24%)
  starting transfers between devices  13.6 us (20%)
  blocking collectives  11.7 us (17%)
  local copies, waits for them, and re-layouts  1.16 us (2%)
  other arithmetic  1.11 us (2%)
  between operations  0.92 us (1%)
    ppermute x16, waiting for transfers between devices, exchange(): return lax.ppermute(x, 'dom', [(i, i ^ bit) for i in range(n)])  24.3 us
    ppermute x16, starting transfers between devices, exchange(): return lax.ppermute(x, 'dom', [(i, i ^ bit) for i in range(n)])  13.6 us
    all_to_all x1, blocking collectives, local(): lax.all_to_all(scored, 'dom', split_axis=0, concat_axis=0, tiled=True)  11.7 us
    pallas_call x3, Pallas kernels, local(): pl.pallas_call(functools.partial(maxsim_kernel, cand_at, cands, cap), out...  9.46 us
    pallas_call x1, Pallas kernels, local(): pl.pallas_call(functools.partial(prep_kernel, parts, slots, cap), out_sha...  2.02 us
    pallas_call x1, Pallas kernels, local(): pl.pallas_call(functools.partial(last_kernel, (masks, parts, cand_at, blo...  1.8 us
    pallas_call x1, Pallas kernels, local(): pl.pallas_call(functools.partial(sum_kernel, rounds, front, cands), out_s...  1.61 us
    pallas_call x1, Pallas kernels, local(): pl.pallas_call(beam_kernel, out_shape=partial, grid=(steps,), in_specs=[l...  1.54 us
  transfers between devices with their start and end apart: 16, of which 10 were waited for; matrix products, arithmetic and copies ran while one was open for 2% of the time, Pallas kernels for 19%

profile of v5, /device:TPU:0, one launch (start us, length us, event | category | flops | bytes accessed | tf_op | source)
XLA Modules:
  0.0 69.2 jit_solution(8622792635427570802)
XLA Ops:
  0.6 0.9 %fusion = (bf16[8,5120]{1,0:T(8,128)(2,1)S(1)}, bf16[8,5120]{1,0:T(8,128)(2,1)S(1)}) fusion(bf16[8,10240]{1,0:T(8,128)(2,1)} %param.9), kind=kLoop, calls=%fused_computation.19 | loop fusion | bytes 327680 | tf_op jit(solution)/shard_map/slice | solution.py:223
  1.6 4.1 %collective-permute-start.4 = (bf16[8,5120]{1,0:T(8,128)(2,1)S(1)}, bf16[8,5120]{1,0:T(8,128)(2,1)S(1)}, u32[]{:S(2)}, u32[]{:S(2)}) collective-permute-start(bf16[8,5120]{1,0:T(8,128)(2,1)S(1)} %get-tuple-element.11), channel_id=1, source_target_pairs={{0,16},{1,17},{2,18},{3,19},{4,20},{5,21},{6,22},{7,23},{8,24},{9,... | collective-permute-start | bytes 245768 | tf_op jit(solution)/shard_map/ppermute | solution.py:34
  5.7 2.0 %pack.1 = bf16[272,128]{1,0:T(8,128)(2,1)} custom-call(s32[3,8,16]{2,1,0:T(8,128)} %fo.1, s32[3,8,16]{2,1,0:T(8,128)} %fs.1, s32[8,32]{1,0:T(8,128)} %bitcast.6, s32[8,32]{1,0:T(8,128)} %cs.1, bf16[256,128]{1,0:T(8,128)(2,1)} %bitcast.5), custom_call_target="tpu_custom_call" | custom-call | tf_op jit(solution)/shard_map/pack/pallas_call | solution.py:225
  7.7 2.9 %collective-permute-start = (bf16[8,5120]{1,0:T(8,128)(2,1)S(1)}, bf16[8,5120]{1,0:T(8,128)(2,1)S(1)}, u32[]{:S(2)}, u32[]{:S(2)}) collective-permute-start(bf16[8,5120]{1,0:T(8,128)(2,1)S(1)} %get-tuple-element.10), channel_id=1, source_target_pairs={{0,16},{1,17},{2,18},{3,19},{4,20},{5,21},{6,22},{7,23},{8,24},{9,... | collective-permute-start | bytes 245768 | tf_op jit(solution)/shard_map/ppermute | solution.py:34
  10.6 5.9 %collective-permute-done.8 = bf16[272,128]{1,0:T(8,128)(2,1)S(1)} collective-permute-done((bf16[272,128]{1,0:T(8,128)(2,1)}, bf16[272,128]{1,0:T(8,128)(2,1)S(1)}, u32[]{:S(2)}, u32[]{:S(2)}) %collective-permute-start.8) | collective-permute-done | bytes 69664 | tf_op jit(solution)/shard_map/ppermute | solution.py:34
  16.6 0.9 %pad_maximum_fusion.8 = bf16[544,128]{1,0:T(8,128)(2,1)S(1)} fusion(bf16[272,128]{1,0:T(8,128)(2,1)S(1)} %collective-permute-done.8, bf16[272,128]{1,0:T(8,128)(2,1)} %pack.1), kind=kLoop, calls=%fused_computation.8 | loop fusion | flops 278528 | bytes 278528 | tf_op jit(solution)/shard_map/concatenate | solution.py:239
  17.5 1.6 %collective-permute-start.9 = (bf16[544,128]{1,0:T(8,128)(2,1)S(1)}, bf16[544,128]{1,0:T(8,128)(2,1)S(1)}, u32[]{:S(2)}, u32[]{:S(2)}) collective-permute-start(bf16[544,128]{1,0:T(8,128)(2,1)S(1)} %pad_maximum_fusion.8), channel_id=1, source_target_pairs={{0,2},{1,3},{2,0},{3,1},{4,6},{5,7},{6,4},{7,5},{8,10},{9,11},{10,... | collective-permute-start | bytes 417800 | tf_op jit(solution)/shard_map/ppermute | solution.py:34
  19.0 1.6 %collective-permute-start.5 = (bf16[16,5120]{1,0:T(8,128)(2,1)S(1)}, bf16[16,5120]{1,0:T(8,128)(2,1)S(1)}, u32[]{:S(2)}, u32[]{:S(2)}) collective-permute-start(bf16[16,5120]{1,0:T(8,128)(2,1)S(1)} %pad_maximum_fusion.7), channel_id=1, source_target_pairs={{0,4},{1,5},{2,6},{3,7},{4,0},{5,1},{6,2},{7,3},{8,12},{9,13},{10,... | collective-permute-start | bytes 491528 | tf_op jit(solution)/shard_map/ppermute | solution.py:34
  20.7 0.1 collective-permute-start.1
  20.8 1.8 %collective-permute-done.9 = bf16[544,128]{1,0:T(8,128)(2,1)S(1)} collective-permute-done((bf16[544,128]{1,0:T(8,128)(2,1)S(1)}, bf16[544,128]{1,0:T(8,128)(2,1)S(1)}, u32[]{:S(2)}, u32[]{:S(2)}) %collective-permute-start.9) | collective-permute-done | bytes 139296 | tf_op jit(solution)/shard_map/ppermute | solution.py:34
  22.6 1.6 %collective-permute-start.10 = (bf16[1088,128]{1,0:T(8,128)(2,1)S(1)}, bf16[1088,128]{1,0:T(8,128)(2,1)S(1)}, u32[]{:S(2)}, u32[]{:S(2)}) collective-permute-start(bf16[1088,128]{1,0:T(8,128)(2,1)S(1)} %pad_maximum_fusion.5), channel_id=1, source_target_pairs={{0,4},{1,5},{2,6},{3,7},{4,0},{5,1},{6,2},{7,3},{8,12},{9,13},{10,... | collective-permute-start | bytes 835592 | tf_op jit(solution)/shard_map/ppermute | solution.py:34
  24.2 1.9 %collective-permute-done.5 = bf16[16,5120]{1,0:T(8,128)(2,1)S(1)} collective-permute-done((bf16[16,5120]{1,0:T(8,128)(2,1)S(1)}, bf16[16,5120]{1,0:T(8,128)(2,1)S(1)}, u32[]{:S(2)}, u32[]{:S(2)}) %collective-permute-start.5) | collective-permute-done | bytes 163872 | tf_op jit(solution)/shard_map/ppermute | solution.py:34
  26.1 0.1 collective-permute-start.6
  26.2 1.7 %collective-permute-done.1 = bf16[16,5120]{1,0:T(8,128)(2,1)S(1)} collective-permute-done((bf16[16,5120]{1,0:T(8,128)(2,1)S(1)}, bf16[16,5120]{1,0:T(8,128)(2,1)S(1)}, u32[]{:S(2)}, u32[]{:S(2)}) %collective-permute-start.1) | collective-permute-done | bytes 163872 | tf_op jit(solution)/shard_map/ppermute | solution.py:34
  27.9 0.5 collective-permute-start.2
  28.4 0.9 %collective-permute-done.10 = bf16[1088,128]{1,0:T(8,128)(2,1)S(1)} collective-permute-done((bf16[1088,128]{1,0:T(8,128)(2,1)S(1)}, bf16[1088,128]{1,0:T(8,128)(2,1)S(1)}, u32[]{:S(2)}, u32[]{:S(2)}) %collective-permute-start.10) | collective-permute-done | bytes 278560 | tf_op jit(solution)/shard_map/ppermute | solution.py:34
  29.3 0.1 collective-permute-start.12
  29.4 0.5 collective-permute-start.11
  29.8 4.1 %collective-permute-done.6 = bf16[32,5120]{1,0:T(8,128)(2,1)S(1)} collective-permute-done((bf16[32,5120]{1,0:T(8,128)(2,1)S(1)}, bf16[32,5120]{1,0:T(8,128)(2,1)S(1)}, u32[]{:S(2)}, u32[]{:S(2)}) %collective-permute-start.6) | collective-permute-done | bytes 327712 | tf_op jit(solution)/shard_map/ppermute | solution.py:34
  34.1 3.2 %collective-permute-done.2 = bf16[32,5120]{1,0:T(8,128)(2,1)S(1)} collective-permute-done((bf16[32,5120]{1,0:T(8,128)(2,1)S(1)}, bf16[32,5120]{1,0:T(8,128)(2,1)S(1)}, u32[]{:S(2)}, u32[]{:S(2)}) %collective-permute-start.2) | collective-permute-done | bytes 327712 | tf_op jit(solution)/shard_map/ppermute | solution.py:34
  37.3 0.1 collective-permute-start.3
  37.5 4.1 %maxsim.3.refs_4_ = f32[16,8,128]{2,1,0:T(8,128)S(1)} custom-call(s32[1]{0:T(128)} %bitcast.me_ref, s32[256]{0:T(256)S(1)} %copy-done.1, bf16[2176,128]{1,0:T(8,128)(2,1)S(1)} %pad_maximum_fusion.2.refs_0_, bf16[2176,128]{1,0:T(8,128)(2,1)S(1)} %collective-permute-done.12.refs_1_, bf16[256,128,128]{2,1,0:T(8,128)(2,1)S(1)} %copy-done), custom_call_target="tpu_custom_call" | custom-call | flops 2147483648 | bytes 8388608 | tf_op jit(solution)/shard_map/maxsim/pallas_call | solution.py:252
  41.6 3.6 %collective-permute-done.11.refs_0_.refs_2_ = bf16[2176,128]{1,0:T(8,128)(2,1)S(1)} collective-permute-done((bf16[2176,128]{1,0:T(8,128)(2,1)S(1)}, bf16[2176,128]{1,0:T(8,128)(2,1)S(1)}, u32[]{:S(2)}, u32[]{:S(2)}) %collective-permute-start.11) | collective-permute-done | bytes 557088 | tf_op jit(solution)/shard_map/ppermute | solution.py:34
  45.2 2.7 %maxsim.4.refs_5_ = f32[8,8,128]{2,1,0:T(8,128)S(1)} custom-call(s32[1]{0:T(128)} %bitcast.me_ref, s32[256]{0:T(256)S(1)} %copy-done.1, bf16[2176,128]{1,0:T(8,128)(2,1)S(1)} %collective-permute-done.11.refs_0_.refs_2_, bf16[256,128,128]{2,1,0:T(8,128)(2,1)S(1)} %copy-done), custom_call_target="tpu_custom_call" | custom-call | flops 1073741824 | bytes 8388608 | tf_op jit(solution)/shard_map/maxsim/pallas_call | solution.py:252
  47.9 1.2 %collective-permute-done.7 = bf16[64,5120]{1,0:T(8,128)(2,1)S(1)} collective-permute-done((bf16[64,5120]{1,0:T(8,128)(2,1)S(1)}, bf16[64,5120]{1,0:T(8,128)(2,1)S(1)}, u32[]{:S(2)}, u32[]{:S(2)}) %collective-permute-start.7) | collective-permute-done | bytes 655392 | tf_op jit(solution)/shard_map/ppermute | solution.py:34
  49.2 0.5 collective-permute-start.14
  49.7 2.7 %maxsim.5.refs_6_ = f32[8,8,128]{2,1,0:T(8,128)S(1)} custom-call(s32[1]{0:T(128)} %bitcast.me_ref, s32[256]{0:T(256)S(1)} %copy-done.1, bf16[2176,128]{1,0:T(8,128)(2,1)S(1)} %collective-permute-done.13.refs_0_.refs_3_, bf16[256,128,128]{2,1,0:T(8,128)(2,1)S(1)} %copy-done), custom_call_target="tpu_custom_call" | custom-call | flops 1073741824 | bytes 8388608 | tf_op jit(solution)/shard_map/maxsim/pallas_call | solution.py:252
  52.5 1.5 %beam.1.first = f32[256,512]{1,0:T(8,128)S(1)} custom-call(bf16[128,5120]{1,0:T(8,128)(2,1)S(1)} %constant_dynamic-update-slice_fusion.own, bf16[128,5120]{1,0:T(8,128)(2,1)S(1)} %collective-permute-done.15.other, bf16[512,10240]{1,0:T(8,128)(2,1)S(1)} %bitcast.4), custom_call_target="tpu_custom_call" | custom-call | flops 1342177280 | bytes 7864320 | tf_op jit(solution)/shard_map/beam/pallas_call | solution.py:288
  54.0 0.1 collective-permute-done.14.other
  54.1 1.8 %beam_last.1 = f32[32,8,128]{2,1,0:T(8,128)S(1)} custom-call(s32[1]{0:T(128)} %bitcast.me_ref, bf16[128,5120]{1,0:T(8,128)(2,1)S(1)} %constant_dynamic-update-slice_fusion.5.own, bf16[128,5120]{1,0:T(8,128)(2,1)S(1)} %collective-permute-done.14.other, bf16[512,10240]{1,0:T(8,128)(2,1)S(1)} %bitcast.4, f32[256,512]{1,0:T(8,128)S(1)} %beam.1.first, ...), custom_call_target="tpu_custom_call" | custom-call | flops 1342177280 | bytes 7864320 | tf_op jit(solution)/shard_map/beam_last/pallas_call | solution.py:299
  56.0 11.7 %all_to_all.5.parts = f32[32,8,128]{2,1,0:T(8,128)} all-to-all(f32[32,8,128]{2,1,0:T(8,128)S(1)} %beam_last.1), channel_id=1, replica_groups=mesh['dom'=32,'rep'=1] {'dom'}, dimensions={0} | all-to-all | bytes 262144 | tf_op jit(solution)/shard_map/all_to_all | solution.py:314
  67.6 1.6 %collect.1 = (f32[3,8,16]{2,1,0:T(8,128)}, f32[8,32]{1,0:T(8,128)}) custom-call(f32[32,8,128]{2,1,0:T(8,128)} %all_to_all.5.parts), custom_call_target="tpu_custom_call" | custom-call | tf_op jit(solution)/shard_map/collect/pallas_call | solution.py:315
  (40 shorter events, 0.6 us)
Async XLA Ops:
  1.6 17.5 %collective-permute-start.4 = (bf16[8,5120]{1,0:T(8,128)(2,1)S(1)}, bf16[8,5120]{1,0:T(8,128)(2,1)S(1)}, u32[]{:S(2)}, u32[]{:S(2)}) collective-permute-start(bf16[8,5120]{1,0:T(8,128)(2,1)S(1)} %get-tuple-element.11), channel_id=1, source_target_pairs={{0,16},{1,17},{2,18},{3,19},{4,20},{5,21},{6,22},{7,23},{8,24},{9,... | collective-permute-start | bytes 245768 | tf_op jit(solution)/shard_map/ppermute | solution.py:34
  7.7 14.9 %copy-start.2 = (bf16[272,128]{1,0:T(8,128)(2,1)S(1)}, bf16[272,128]{1,0:T(8,128)(2,1)}, u32[]{:S(2)}) copy-start(bf16[272,128]{1,0:T(8,128)(2,1)} %pack.1) | copy-start | bytes 208900
  7.7 8.9 %collective-permute-start.8 = (bf16[272,128]{1,0:T(8,128)(2,1)}, bf16[272,128]{1,0:T(8,128)(2,1)S(1)}, u32[]{:S(2)}, u32[]{:S(2)}) collective-permute-start(bf16[272,128]{1,0:T(8,128)(2,1)} %pack.1), channel_id=1, source_target_pairs={{0,16},{1,17},{2,18},{3,19},{4,20},{5,21},{6,22},{7,23},{8,24},{9,... | collective-permute-start | bytes 208904 | tf_op jit(solution)/shard_map/ppermute | solution.py:34
  7.7 12.9 %collective-permute-start = (bf16[8,5120]{1,0:T(8,128)(2,1)S(1)}, bf16[8,5120]{1,0:T(8,128)(2,1)S(1)}, u32[]{:S(2)}, u32[]{:S(2)}) collective-permute-start(bf16[8,5120]{1,0:T(8,128)(2,1)S(1)} %get-tuple-element.10), channel_id=1, source_target_pairs={{0,16},{1,17},{2,18},{3,19},{4,20},{5,21},{6,22},{7,23},{8,24},{9,... | collective-permute-start | bytes 245768 | tf_op jit(solution)/shard_map/ppermute | solution.py:34
  17.5 5.1 %collective-permute-start.9 = (bf16[544,128]{1,0:T(8,128)(2,1)S(1)}, bf16[544,128]{1,0:T(8,128)(2,1)S(1)}, u32[]{:S(2)}, u32[]{:S(2)}) collective-permute-start(bf16[544,128]{1,0:T(8,128)(2,1)S(1)} %pad_maximum_fusion.8), channel_id=1, source_target_pairs={{0,2},{1,3},{2,0},{3,1},{4,6},{5,7},{6,4},{7,5},{8,10},{9,11},{10,... | collective-permute-start | bytes 417800 | tf_op jit(solution)/shard_map/ppermute | solution.py:34
  19.0 18.4 %copy-start = (bf16[256,128,128]{2,1,0:T(8,128)(2,1)S(1)}, bf16[256,128,128]{2,1,0:T(8,128)(2,1)}, u32[]{:S(2)}) copy-start(bf16[256,128,128]{2,1,0:T(8,128)(2,1)} %refs_1_.3) | copy-start | bytes 25165828
  19.0 7.0 %collective-permute-start.5 = (bf16[16,5120]{1,0:T(8,128)(2,1)S(1)}, bf16[16,5120]{1,0:T(8,128)(2,1)S(1)}, u32[]{:S(2)}, u32[]{:S(2)}) collective-permute-start(bf16[16,5120]{1,0:T(8,128)(2,1)S(1)} %pad_maximum_fusion.7), channel_id=1, source_target_pairs={{0,4},{1,5},{2,6},{3,7},{4,0},{5,1},{6,2},{7,3},{8,12},{9,13},{10,... | collective-permute-start | bytes 491528 | tf_op jit(solution)/shard_map/ppermute | solution.py:34
  20.7 7.2 %collective-permute-start.1 = (bf16[16,5120]{1,0:T(8,128)(2,1)S(1)}, bf16[16,5120]{1,0:T(8,128)(2,1)S(1)}, u32[]{:S(2)}, u32[]{:S(2)}) collective-permute-start(bf16[16,5120]{1,0:T(8,128)(2,1)S(1)} %pad_maximum_fusion.6), channel_id=1, source_target_pairs={{0,8},{1,9},{2,10},{3,11},{4,12},{5,13},{6,14},{7,15},{8,0},{9,1},... | collective-permute-start | bytes 491528 | tf_op jit(solution)/shard_map/ppermute | solution.py:34
  22.6 6.6 %collective-permute-start.10 = (bf16[1088,128]{1,0:T(8,128)(2,1)S(1)}, bf16[1088,128]{1,0:T(8,128)(2,1)S(1)}, u32[]{:S(2)}, u32[]{:S(2)}) collective-permute-start(bf16[1088,128]{1,0:T(8,128)(2,1)S(1)} %pad_maximum_fusion.5), channel_id=1, source_target_pairs={{0,4},{1,5},{2,6},{3,7},{4,0},{5,1},{6,2},{7,3},{8,12},{9,13},{10,... | collective-permute-start | bytes 835592 | tf_op jit(solution)/shard_map/ppermute | solution.py:34
  26.1 7.8 %collective-permute-start.6 = (bf16[32,5120]{1,0:T(8,128)(2,1)S(1)}, bf16[32,5120]{1,0:T(8,128)(2,1)S(1)}, u32[]{:S(2)}, u32[]{:S(2)}) collective-permute-start(bf16[32,5120]{1,0:T(8,128)(2,1)S(1)} %pad_maximum_fusion.4), channel_id=1, source_target_pairs={{0,8},{1,9},{2,10},{3,11},{4,12},{5,13},{6,14},{7,15},{8,0},{9,1},... | collective-permute-start | bytes 983048 | tf_op jit(solution)/shard_map/ppermute | solution.py:34
  27.9 9.4 %collective-permute-start.2 = (bf16[32,5120]{1,0:T(8,128)(2,1)S(1)}, bf16[32,5120]{1,0:T(8,128)(2,1)S(1)}, u32[]{:S(2)}, u32[]{:S(2)}) collective-permute-start(bf16[32,5120]{1,0:T(8,128)(2,1)S(1)} %pad_maximum_fusion.3), channel_id=1, source_target_pairs={{0,2},{1,3},{2,0},{3,1},{4,6},{5,7},{6,4},{7,5},{8,10},{9,11},{10,... | collective-permute-start | bytes 983048 | tf_op jit(solution)/shard_map/ppermute | solution.py:34
  29.3 8.2 %collective-permute-start.12 = (bf16[2176,128]{1,0:T(8,128)(2,1)S(1)}, bf16[2176,128]{1,0:T(8,128)(2,1)S(1)}, u32[]{:S(2)}, u32[]{:S(2)}) collective-permute-start(bf16[2176,128]{1,0:T(8,128)(2,1)S(1)} %pad_maximum_fusion.2.refs_0_), channel_id=1, source_target_pairs={{0,1},{1,0},{2,3},{3,2},{4,5},{5,4},{6,7},{7,6},{8,9},{9,8},{10,11... | collective-permute-start | bytes 1671176 | tf_op jit(solution)/shard_map/ppermute | solution.py:34
  29.4 15.8 %collective-permute-start.11 = (bf16[2176,128]{1,0:T(8,128)(2,1)S(1)}, bf16[2176,128]{1,0:T(8,128)(2,1)S(1)}, u32[]{:S(2)}, u32[]{:S(2)}) collective-permute-start(bf16[2176,128]{1,0:T(8,128)(2,1)S(1)} %pad_maximum_fusion.2.refs_0_), channel_id=1, source_target_pairs={{0,8},{1,9},{2,10},{3,11},{4,12},{5,13},{6,14},{7,15},{8,0},{9,1},... | collective-permute-start | bytes 1671176 | tf_op jit(solution)/shard_map/ppermute | solution.py:34
  34.0 3.5 %copy-start.1 = (s32[256]{0:T(256)S(1)}, s32[256]{0:T(256)}, u32[]{:S(2)}) copy-start(s32[256]{0:T(256)} %lens.5) | copy-start | bytes 3076
  34.0 15.0 %collective-permute-start.7 = (bf16[64,5120]{1,0:T(8,128)(2,1)S(1)}, bf16[64,5120]{1,0:T(8,128)(2,1)S(1)}, u32[]{:S(2)}, u32[]{:S(2)}) collective-permute-start(bf16[64,5120]{1,0:T(8,128)(2,1)S(1)} %pad_maximum_fusion.1), channel_id=1, source_target_pairs={{0,2},{1,3},{2,0},{3,1},{4,6},{5,7},{6,4},{7,5},{8,10},{9,11},{10,... | collective-permute-start | bytes 1966088 | tf_op jit(solution)/shard_map/ppermute | solution.py:34
  37.3 11.8 %collective-permute-start.3 = (bf16[64,5120]{1,0:T(8,128)(2,1)S(1)}, bf16[64,5120]{1,0:T(8,128)(2,1)S(1)}, u32[]{:S(2)}, u32[]{:S(2)}) collective-permute-start(bf16[64,5120]{1,0:T(8,128)(2,1)S(1)} %pad_maximum_fusion), channel_id=1, source_target_pairs={{0,4},{1,5},{2,6},{3,7},{4,0},{5,1},{6,2},{7,3},{8,12},{9,13},{10,... | collective-permute-start | bytes 1966088 | tf_op jit(solution)/shard_map/ppermute | solution.py:34
  45.2 4.0 %collective-permute-start.13 = (bf16[2176,128]{1,0:T(8,128)(2,1)S(1)}, bf16[2176,128]{1,0:T(8,128)(2,1)S(1)}, u32[]{:S(2)}, u32[]{:S(2)}) collective-permute-start(bf16[2176,128]{1,0:T(8,128)(2,1)S(1)} %collective-permute-done.11.refs_0_.refs_2_), channel_id=1, source_target_pairs={{0,1},{1,0},{2,3},{3,2},{4,5},{5,4},{6,7},{7,6},{8,9},{9,8},{10,11... | collective-permute-start | bytes 1671176 | tf_op jit(solution)/shard_map/ppermute | solution.py:34
  45.2 7.3 %slice-start = ((s8[10485760]{0:T(1024)(128)(4,1)}), s8[4194304]{0:T(1024)(128)(4,1)S(1)}, s32[]{:S(2)}) async-start(s8[10485760]{0:T(1024)(128)(4,1)} %bitcast.3), calls=%async_computation.1 | async-start | bytes 8388608
  45.2 7.3 %slice-start.1 = ((s8[10485760]{0:T(1024)(128)(4,1)}), s8[4194304]{0:T(1024)(128)(4,1)S(1)}, s32[]{:S(2)}) async-start(s8[10485760]{0:T(1024)(128)(4,1)} %bitcast.3), calls=%async_computation.2 | async-start | bytes 8388608
  49.1 3.3 %slice-start.2 = ((s8[10485760]{0:T(1024)(128)(4,1)}), s8[2097152]{0:T(1024)(128)(4,1)S(1)}, s32[]{:S(2)}) async-start(s8[10485760]{0:T(1024)(128)(4,1)} %bitcast.3), calls=%async_computation.3 | async-start | bytes 4194304
  49.2 3.3 %collective-permute-start.15 = (bf16[128,5120]{1,0:T(8,128)(2,1)S(1)}, bf16[128,5120]{1,0:T(8,128)(2,1)S(1)}, u32[]{:S(2)}, u32[]{:S(2)}) collective-permute-start(bf16[128,5120]{1,0:T(8,128)(2,1)S(1)} %constant_dynamic-update-slice_fusion.own), channel_id=1, source_target_pairs={{0,1},{1,0},{2,3},{3,2},{4,5},{5,4},{6,7},{7,6},{8,9},{9,8},{10,11... | collective-permute-start | bytes 3932168 | tf_op jit(solution)/shard_map/ppermute | solution.py:34
  49.2 4.9 %collective-permute-start.14 = (bf16[128,5120]{1,0:T(8,128)(2,1)S(1)}, bf16[128,5120]{1,0:T(8,128)(2,1)S(1)}, u32[]{:S(2)}, u32[]{:S(2)}) collective-permute-start(bf16[128,5120]{1,0:T(8,128)(2,1)S(1)} %constant_dynamic-update-slice_fusion.5.own), channel_id=1, source_target_pairs={{0,1},{1,0},{2,3},{3,2},{4,5},{5,4},{6,7},{7,6},{8,9},{9,8},{10,11... | collective-permute-start | bytes 3932168 | tf_op jit(solution)/shard_map/ppermute | solution.py:34

commit v6 on v5

--- a/solution.py
+++ b/solution.py
@@ -25,9 +25,6 @@
     bits = [1 << i for i in range(1, n.bit_length() - 1)]
     far, rest = bits[-1:], bits[:-1]
     return [[16, 2, 4, 8], [16, 8, 2, 4], [16, 4, 8, 2]]
-
-
-TIES = {}
 
 
 def exchange(x, bit, n):
@@ -151,12 +148,8 @@
 
 
 def beam_kernel(own, other, doc, total):
-    @pl.when(pl.program_id(0) == 0)
-    def _():
-        total[...] = jnp.zeros_like(total)
-
     left = jnp.concatenate([own[...], other[...]], axis=0)
-    total[...] += lax.dot_general(left, doc[...], NT, preferred_element_type=jnp.float32)
+    total[...] = lax.dot_general(left, doc[...], NT, preferred_element_type=jnp.float32)
 
 
 def last_kernel(cfg, me_ref, own, other, doc, first, *refs):
@@ -165,38 +158,27 @@
     stride = codes[0].shape[0] // blocks
     beam_kernel(own, other, doc, last)
 
-    @pl.when(pl.program_id(0) == pl.num_programs(0) - 1)
-    def _():
-        me = me_ref[0]
-        lane = ids((8, LANES), 1)
-        nodes = last.shape[1]
-
-        for m in masks[0]:
-            for side in range(2):
-                half, t = divmod(masks[0].index(m), blocks)
-                table = codes[2 * half + side][(t + 1) * stride - 16 : (t + 1) * stride, :].astype(jnp.float32)[:8]
-                low = pltpu.roll(table, LANES - cand_at, axis=1).astype(jnp.int32)
-                table = table.astype(jnp.int32)
-                owner, high = table // parts, table % parts
-                slot = high * 256 + low
-                within, page = slot % LANES, slot // LANES
-                ats = [(side * 2 * blocks + masks[k].index(m)) * 8 for k in (1, 2)]
-                rows = first[ats[0] : ats[0] + 8, :] + last[ats[1] : ats[1] + 8, :]
-                found = jnp.zeros((8, LANES), jnp.float32)
-                for g in range(nodes // LANES):
-                    here = jnp.take_along_axis(rows[:, g * LANES : (g + 1) * LANES], within, axis=1)
-                    found = jnp.where(page == g, here, found)
-                found = jnp.where(owner == me, found, 0.0)
-                out[me ^ (m + side)] = jnp.where(lane < cand_at, found, (scores[0][side * blocks + t] if half == 0 else scores[1 + side][t]))
-
-
-def sum_kernel(rounds, front, cands, parts, beam, maxsim):
-    total = parts[0]
-    for i in range(1, parts.shape[0]):
-        total = total + parts[i]
-    for r in range(rounds):
-        beam[r] = (total if r == 0 else pltpu.roll(total, LANES - r * front, axis=1))[:, :front]
-    maxsim[...] = pltpu.roll(total, LANES - rounds * front, axis=1)[:, :cands]
+    me = me_ref[0]
+    lane = ids((8, LANES), 1)
+    nodes = last.shape[1]
+
+    for m in masks[0]:
+        for side in range(2):
+            half, t = divmod(masks[0].index(m), blocks)
+            table = codes[2 * half + side][(t + 1) * stride - 16 : (t + 1) * stride, :].astype(jnp.float32)[:8]
+            low = pltpu.roll(table, LANES - cand_at, axis=1).astype(jnp.int32)
+            table = table.astype(jnp.int32)
+            owner, high = table // parts, table % parts
+            slot = high * 256 + low
+            within, page = slot % LANES, slot // LANES
+            ats = [(side * 2 * blocks + masks[k].index(m)) * 8 for k in (1, 2)]
+            rows = first[ats[0] : ats[0] + 8, :] + last[ats[1] : ats[1] + 8, :]
+            found = jnp.zeros((8, LANES), jnp.float32)
+            for g in range(nodes // LANES):
+                here = jnp.take_along_axis(rows[:, g * LANES : (g + 1) * LANES], within, axis=1)
+                found = jnp.where(page == g, here, found)
+            found = jnp.where(owner == me, found, 0.0)
+            out[me ^ (m + side)] = jnp.where(lane < cand_at, found, (scores[0][side * blocks + t] if half == 0 else scores[1 + side][t]))
 
 
 def local(n, query_fde, doc_fde, frontier_owner, frontier_slot, query_tokens, passage_tiles, passage_len, cand_owner, cand_slot):
@@ -240,10 +222,7 @@
 
     @functools.cache
     def arrived(k, step):
-        mine = gathered(k, step)
-        if (k, step) in TIES:
-            mine = lax.optimization_barrier((mine, arrived(*TIES[k, step])))[0]
-        return exchange(mine, orders[k][step], n)
+        return exchange(gathered(k, step), orders[k][step], n)
 
     tok = [gathered(0, stages - 1), arrived(0, stages - 1)]
     tok = [(tok[0], exchange(tok[0], 1, n)), tok[1]]
@@ -277,18 +256,16 @@
     maxsim.append(score(late_other))
     a_other, b_other = exchange(a_own, 1, n), exchange(b_own, 1, n)
 
-    block = half
-    steps = half // block
     rows = n * 8
     full = lambda shape: pl.BlockSpec(shape, lambda i, *_: (0,) * len(shape))
-    left = pl.BlockSpec((rows // 2, block), lambda i, *_: (0, i))
-    doc = lambda first: pl.BlockSpec((nodes, block), lambda i, *_: (0, first + i))
+    left = full((rows // 2, half))
+    doc = lambda at: pl.BlockSpec((nodes, half), lambda i, *_: (0, at))
     partial = jax.ShapeDtypeStruct((rows, nodes), jnp.float32)
     cost = pl.CostEstimate(flops=2 * rows * nodes * half, bytes_accessed=2 * (rows + nodes) * half, transcendentals=0)
     first = pl.pallas_call(
         beam_kernel,
         out_shape=partial,
-        grid=(steps,),
+        grid=(1,),
         in_specs=[left, left, doc(0)],
         out_specs=full(partial.shape),
         compiler_params=pltpu.CompilerParams(vmem_limit_bytes=16 << 20),
@@ -301,8 +278,8 @@
         out_shape=jax.ShapeDtypeStruct((n, 8, LANES), jnp.float32),
         grid_spec=pltpu.PrefetchScalarGridSpec(
             num_scalar_prefetch=1,
-            grid=(steps,),
-            in_specs=[left, left, doc(steps)] + [full(x.shape) for x in (first, *codes, *maxsim)],
+            grid=(1,),
+            in_specs=[left, left, doc(1)] + [full(x.shape) for x in (first, *codes, *maxsim)],
             out_specs=full((n, 8, LANES)),
             scratch_shapes=[pltpu.VMEM(partial.shape, jnp.float32)],
         ),
@@ -312,16 +289,9 @@
     )(me.reshape(1), b_own, b_other, doc_fde, first, *codes, *maxsim)
 
     returned = lax.all_to_all(scored, "dom", split_axis=0, concat_axis=0, tiled=True)
-    return pl.pallas_call(
-        functools.partial(sum_kernel, rounds, front, cands),
-        out_shape=(
-            jax.ShapeDtypeStruct((rounds, queries, front), jnp.float32),
-            jax.ShapeDtypeStruct((queries, cands), jnp.float32),
-        ),
-        in_specs=[VMEM],
-        out_specs=(VMEM, VMEM),
-        name="collect",
-    )(returned)
+    total = jnp.sum(returned, axis=0)
+    beam = total[:, :cand_at].reshape(queries, rounds, front).transpose(1, 0, 2)
+    return beam, total[:, cand_at : cand_at + cands]
 
 
 def solution(mesh):

time: 69.5 us -> 69.2 us (level)
  Pallas kernels: 16.4 us -> 14.8 us
  local copies, waits for them, and re-layouts: 1.16 us -> 2.51 us
    pallas_call x2 -> x1, Pallas kernels: 3.15 us -> 1.54 us  [local(): pl.pallas_call(beam_kernel, out_shape=partial, grid=(1,), in_specs=[left,...]
where the time goes in v6:
time: 69.2 us; the launch traced here: 68.9 us
  waiting for transfers between devices  24.3 us (35%)
  Pallas kernels  14.8 us (21%)
  starting transfers between devices  13.6 us (20%)
  blocking collectives  11.6 us (17%)
  local copies, waits for them, and re-layouts  2.51 us (4%)
  other arithmetic  1.14 us (2%)
  between operations  0.92 us (1%)
    ppermute x16, waiting for transfers between devices, exchange(): return lax.ppermute(x, 'dom', [(i, i ^ bit) for i in range(n)])  24.3 us
    ppermute x16, starting transfers between devices, exchange(): return lax.ppermute(x, 'dom', [(i, i ^ bit) for i in range(n)])  13.6 us
    all_to_all x1, blocking collectives, local(): lax.all_to_all(scored, 'dom', split_axis=0, concat_axis=0, tiled=True)  11.6 us
    pallas_call x3, Pallas kernels, local(): pl.pallas_call(functools.partial(maxsim_kernel, cand_at, cands, cap), out...  9.47 us
    pallas_call x1, Pallas kernels, local(): pl.pallas_call(functools.partial(prep_kernel, parts, slots, cap), out_sha...  2.02 us
    pallas_call x1, Pallas kernels, local(): pl.pallas_call(functools.partial(last_kernel, (masks, parts, cand_at, blo...  1.8 us
    pallas_call x1, Pallas kernels, local(): pl.pallas_call(beam_kernel, out_shape=partial, grid=(1,), in_specs=[left,...  1.54 us
  transfers between devices with their start and end apart: 16, of which 10 were waited for; matrix products, arithmetic and copies ran while one was open for 2% of the time, Pallas kernels for 19%

profile of v6, /device:TPU:0, one launch (start us, length us, event | category | flops | bytes accessed | tf_op | source)
XLA Modules:
  0.0 68.9 jit_solution(11328079930504941636)
XLA Ops:
  0.6 0.9 %fusion = (bf16[8,5120]{1,0:T(8,128)(2,1)S(1)}, bf16[8,5120]{1,0:T(8,128)(2,1)S(1)}) fusion(bf16[8,10240]{1,0:T(8,128)(2,1)} %param.9), kind=kLoop, calls=%fused_computation.19 | loop fusion | bytes 327680 | tf_op jit(solution)/shard_map/slice | solution.py:205
  1.6 4.1 %collective-permute-start.4 = (bf16[8,5120]{1,0:T(8,128)(2,1)S(1)}, bf16[8,5120]{1,0:T(8,128)(2,1)S(1)}, u32[]{:S(2)}, u32[]{:S(2)}) collective-permute-start(bf16[8,5120]{1,0:T(8,128)(2,1)S(1)} %get-tuple-element.11), channel_id=1, source_target_pairs={{0,16},{1,17},{2,18},{3,19},{4,20},{5,21},{6,22},{7,23},{8,24},{9,... | collective-permute-start | bytes 245768 | tf_op jit(solution)/shard_map/ppermute | solution.py:31
  5.7 2.0 %pack.1 = bf16[272,128]{1,0:T(8,128)(2,1)} custom-call(s32[3,8,16]{2,1,0:T(8,128)} %fo.1, s32[3,8,16]{2,1,0:T(8,128)} %fs.1, s32[8,32]{1,0:T(8,128)} %bitcast.10, s32[8,32]{1,0:T(8,128)} %cs.1, bf16[256,128]{1,0:T(8,128)(2,1)} %bitcast.8), custom_call_target="tpu_custom_call" | custom-call | tf_op jit(solution)/shard_map/pack/pallas_call | solution.py:207
  7.7 2.9 %collective-permute-start = (bf16[8,5120]{1,0:T(8,128)(2,1)S(1)}, bf16[8,5120]{1,0:T(8,128)(2,1)S(1)}, u32[]{:S(2)}, u32[]{:S(2)}) collective-permute-start(bf16[8,5120]{1,0:T(8,128)(2,1)S(1)} %get-tuple-element.10), channel_id=1, source_target_pairs={{0,16},{1,17},{2,18},{3,19},{4,20},{5,21},{6,22},{7,23},{8,24},{9,... | collective-permute-start | bytes 245768 | tf_op jit(solution)/shard_map/ppermute | solution.py:31
  10.6 5.9 %collective-permute-done.8 = bf16[272,128]{1,0:T(8,128)(2,1)S(1)} collective-permute-done((bf16[272,128]{1,0:T(8,128)(2,1)}, bf16[272,128]{1,0:T(8,128)(2,1)S(1)}, u32[]{:S(2)}, u32[]{:S(2)}) %collective-permute-start.8) | collective-permute-done | bytes 69664 | tf_op jit(solution)/shard_map/ppermute | solution.py:31
  16.6 0.9 %pad_maximum_fusion.8 = bf16[544,128]{1,0:T(8,128)(2,1)S(1)} fusion(bf16[272,128]{1,0:T(8,128)(2,1)S(1)} %collective-permute-done.8, bf16[272,128]{1,0:T(8,128)(2,1)} %pack.1), kind=kLoop, calls=%fused_computation.8 | loop fusion | flops 278528 | bytes 278528 | tf_op jit(solution)/shard_map/concatenate | solution.py:221
  17.5 1.6 %collective-permute-start.9 = (bf16[544,128]{1,0:T(8,128)(2,1)S(1)}, bf16[544,128]{1,0:T(8,128)(2,1)S(1)}, u32[]{:S(2)}, u32[]{:S(2)}) collective-permute-start(bf16[544,128]{1,0:T(8,128)(2,1)S(1)} %pad_maximum_fusion.8), channel_id=1, source_target_pairs={{0,2},{1,3},{2,0},{3,1},{4,6},{5,7},{6,4},{7,5},{8,10},{9,11},{10,... | collective-permute-start | bytes 417800 | tf_op jit(solution)/shard_map/ppermute | solution.py:31
  19.0 1.6 %collective-permute-start.5 = (bf16[16,5120]{1,0:T(8,128)(2,1)S(1)}, bf16[16,5120]{1,0:T(8,128)(2,1)S(1)}, u32[]{:S(2)}, u32[]{:S(2)}) collective-permute-start(bf16[16,5120]{1,0:T(8,128)(2,1)S(1)} %pad_maximum_fusion.7), channel_id=1, source_target_pairs={{0,4},{1,5},{2,6},{3,7},{4,0},{5,1},{6,2},{7,3},{8,12},{9,13},{10,... | collective-permute-start | bytes 491528 | tf_op jit(solution)/shard_map/ppermute | solution.py:31
  20.8 1.8 %collective-permute-done.9 = bf16[544,128]{1,0:T(8,128)(2,1)S(1)} collective-permute-done((bf16[544,128]{1,0:T(8,128)(2,1)S(1)}, bf16[544,128]{1,0:T(8,128)(2,1)S(1)}, u32[]{:S(2)}, u32[]{:S(2)}) %collective-permute-start.9) | collective-permute-done | bytes 139296 | tf_op jit(solution)/shard_map/ppermute | solution.py:31
  22.6 1.6 %collective-permute-start.10 = (bf16[1088,128]{1,0:T(8,128)(2,1)S(1)}, bf16[1088,128]{1,0:T(8,128)(2,1)S(1)}, u32[]{:S(2)}, u32[]{:S(2)}) collective-permute-start(bf16[1088,128]{1,0:T(8,128)(2,1)S(1)} %pad_maximum_fusion.5), channel_id=1, source_target_pairs={{0,4},{1,5},{2,6},{3,7},{4,0},{5,1},{6,2},{7,3},{8,12},{9,13},{10,... | collective-permute-start | bytes 835592 | tf_op jit(solution)/shard_map/ppermute | solution.py:31
  24.2 1.9 %collective-permute-done.5 = bf16[16,5120]{1,0:T(8,128)(2,1)S(1)} collective-permute-done((bf16[16,5120]{1,0:T(8,128)(2,1)S(1)}, bf16[16,5120]{1,0:T(8,128)(2,1)S(1)}, u32[]{:S(2)}, u32[]{:S(2)}) %collective-permute-start.5) | collective-permute-done | bytes 163872 | tf_op jit(solution)/shard_map/ppermute | solution.py:31
  26.1 0.1 collective-permute-start.6
  26.2 1.6 %collective-permute-done.1 = bf16[16,5120]{1,0:T(8,128)(2,1)S(1)} collective-permute-done((bf16[16,5120]{1,0:T(8,128)(2,1)S(1)}, bf16[16,5120]{1,0:T(8,128)(2,1)S(1)}, u32[]{:S(2)}, u32[]{:S(2)}) %collective-permute-start.1) | collective-permute-done | bytes 163872 | tf_op jit(solution)/shard_map/ppermute | solution.py:31
  27.8 0.5 collective-permute-start.2
  28.4 0.8 %collective-permute-done.10 = bf16[1088,128]{1,0:T(8,128)(2,1)S(1)} collective-permute-done((bf16[1088,128]{1,0:T(8,128)(2,1)S(1)}, bf16[1088,128]{1,0:T(8,128)(2,1)S(1)}, u32[]{:S(2)}, u32[]{:S(2)}) %collective-permute-start.10) | collective-permute-done | bytes 278560 | tf_op jit(solution)/shard_map/ppermute | solution.py:31
  29.3 0.1 collective-permute-start.12
  29.3 0.5 collective-permute-start.11
  29.8 4.1 %collective-permute-done.6 = bf16[32,5120]{1,0:T(8,128)(2,1)S(1)} collective-permute-done((bf16[32,5120]{1,0:T(8,128)(2,1)S(1)}, bf16[32,5120]{1,0:T(8,128)(2,1)S(1)}, u32[]{:S(2)}, u32[]{:S(2)}) %collective-permute-start.6) | collective-permute-done | bytes 327712 | tf_op jit(solution)/shard_map/ppermute | solution.py:31
  34.1 3.1 %collective-permute-done.2 = bf16[32,5120]{1,0:T(8,128)(2,1)S(1)} collective-permute-done((bf16[32,5120]{1,0:T(8,128)(2,1)S(1)}, bf16[32,5120]{1,0:T(8,128)(2,1)S(1)}, u32[]{:S(2)}, u32[]{:S(2)}) %collective-permute-start.2) | collective-permute-done | bytes 327712 | tf_op jit(solution)/shard_map/ppermute | solution.py:31
  37.4 4.1 %maxsim.3.refs_4_ = f32[16,8,128]{2,1,0:T(8,128)S(1)} custom-call(s32[1]{0:T(128)} %bitcast.me_ref, s32[256]{0:T(256)S(1)} %copy-done.1, bf16[2176,128]{1,0:T(8,128)(2,1)S(1)} %pad_maximum_fusion.2.refs_0_, bf16[2176,128]{1,0:T(8,128)(2,1)S(1)} %collective-permute-done.12.refs_1_, bf16[256,128,128]{2,1,0:T(8,128)(2,1)S(1)} %copy-done), custom_call_target="tpu_custom_call" | custom-call | flops 2147483648 | bytes 8388608 | tf_op jit(solution)/shard_map/maxsim/pallas_call | solution.py:231
  41.6 3.6 %collective-permute-done.11.refs_0_.refs_2_ = bf16[2176,128]{1,0:T(8,128)(2,1)S(1)} collective-permute-done((bf16[2176,128]{1,0:T(8,128)(2,1)S(1)}, bf16[2176,128]{1,0:T(8,128)(2,1)S(1)}, u32[]{:S(2)}, u32[]{:S(2)}) %collective-permute-start.11) | collective-permute-done | bytes 557088 | tf_op jit(solution)/shard_map/ppermute | solution.py:31
  45.2 2.7 %maxsim.4.refs_5_ = f32[8,8,128]{2,1,0:T(8,128)S(1)} custom-call(s32[1]{0:T(128)} %bitcast.me_ref, s32[256]{0:T(256)S(1)} %copy-done.1, bf16[2176,128]{1,0:T(8,128)(2,1)S(1)} %collective-permute-done.11.refs_0_.refs_2_, bf16[256,128,128]{2,1,0:T(8,128)(2,1)S(1)} %copy-done), custom_call_target="tpu_custom_call" | custom-call | flops 1073741824 | bytes 8388608 | tf_op jit(solution)/shard_map/maxsim/pallas_call | solution.py:231
  47.9 1.2 %collective-permute-done.7 = bf16[64,5120]{1,0:T(8,128)(2,1)S(1)} collective-permute-done((bf16[64,5120]{1,0:T(8,128)(2,1)S(1)}, bf16[64,5120]{1,0:T(8,128)(2,1)S(1)}, u32[]{:S(2)}, u32[]{:S(2)}) %collective-permute-start.7) | collective-permute-done | bytes 655392 | tf_op jit(solution)/shard_map/ppermute | solution.py:31
  49.2 0.5 collective-permute-start.14
  49.7 2.7 %maxsim.5.refs_6_ = f32[8,8,128]{2,1,0:T(8,128)S(1)} custom-call(s32[1]{0:T(128)} %bitcast.me_ref, s32[256]{0:T(256)S(1)} %copy-done.1, bf16[2176,128]{1,0:T(8,128)(2,1)S(1)} %collective-permute-done.13.refs_0_.refs_3_, bf16[256,128,128]{2,1,0:T(8,128)(2,1)S(1)} %copy-done), custom_call_target="tpu_custom_call" | custom-call | flops 1073741824 | bytes 8388608 | tf_op jit(solution)/shard_map/maxsim/pallas_call | solution.py:231
  52.5 1.5 %beam.1.first = f32[256,512]{1,0:T(8,128)S(1)} custom-call(bf16[128,5120]{1,0:T(8,128)(2,1)S(1)} %constant_dynamic-update-slice_fusion.own, bf16[128,5120]{1,0:T(8,128)(2,1)S(1)} %collective-permute-done.15.other, bf16[512,10240]{1,0:T(8,128)(2,1)S(1)} %bitcast.6), custom_call_target="tpu_custom_call" | custom-call | flops 1342177280 | bytes 7864320 | tf_op jit(solution)/shard_map/beam/pallas_call | solution.py:265
  54.0 0.1 collective-permute-done.14.other
  54.1 1.8 %beam_last.1 = f32[32,8,128]{2,1,0:T(8,128)S(1)} custom-call(s32[1]{0:T(128)} %bitcast.me_ref, bf16[128,5120]{1,0:T(8,128)(2,1)S(1)} %constant_dynamic-update-slice_fusion.5.own, bf16[128,5120]{1,0:T(8,128)(2,1)S(1)} %collective-permute-done.14.other, bf16[512,10240]{1,0:T(8,128)(2,1)S(1)} %bitcast.6, f32[256,512]{1,0:T(8,128)S(1)} %beam.1.first, ...), custom_call_target="tpu_custom_call" | custom-call | flops 1342177280 | bytes 7864320 | tf_op jit(solution)/shard_map/beam_last/pallas_call | solution.py:276
  55.9 11.6 %all_to_all.5 = f32[32,8,128]{2,1,0:T(8,128)S(1)} all-to-all(f32[32,8,128]{2,1,0:T(8,128)S(1)} %beam_last.1), channel_id=1, replica_groups=mesh['dom'=32,'rep'=1] {'dom'}, dimensions={0} | all-to-all | bytes 262144 | tf_op jit(solution)/shard_map/all_to_all | solution.py:291
  67.6 0.7 slice.15
  68.2 0.1 reshape.22
  68.3 0.6 copy.12
  (43 shorter events, 0.8 us)
Async XLA Ops:
  1.6 17.5 %collective-permute-start.4 = (bf16[8,5120]{1,0:T(8,128)(2,1)S(1)}, bf16[8,5120]{1,0:T(8,128)(2,1)S(1)}, u32[]{:S(2)}, u32[]{:S(2)}) collective-permute-start(bf16[8,5120]{1,0:T(8,128)(2,1)S(1)} %get-tuple-element.11), channel_id=1, source_target_pairs={{0,16},{1,17},{2,18},{3,19},{4,20},{5,21},{6,22},{7,23},{8,24},{9,... | collective-permute-start | bytes 245768 | tf_op jit(solution)/shard_map/ppermute | solution.py:31
  7.7 14.9 %copy-start.2 = (bf16[272,128]{1,0:T(8,128)(2,1)S(1)}, bf16[272,128]{1,0:T(8,128)(2,1)}, u32[]{:S(2)}) copy-start(bf16[272,128]{1,0:T(8,128)(2,1)} %pack.1) | copy-start | bytes 208900
  7.7 8.9 %collective-permute-start.8 = (bf16[272,128]{1,0:T(8,128)(2,1)}, bf16[272,128]{1,0:T(8,128)(2,1)S(1)}, u32[]{:S(2)}, u32[]{:S(2)}) collective-permute-start(bf16[272,128]{1,0:T(8,128)(2,1)} %pack.1), channel_id=1, source_target_pairs={{0,16},{1,17},{2,18},{3,19},{4,20},{5,21},{6,22},{7,23},{8,24},{9,... | collective-permute-start | bytes 208904 | tf_op jit(solution)/shard_map/ppermute | solution.py:31
  7.7 12.9 %collective-permute-start = (bf16[8,5120]{1,0:T(8,128)(2,1)S(1)}, bf16[8,5120]{1,0:T(8,128)(2,1)S(1)}, u32[]{:S(2)}, u32[]{:S(2)}) collective-permute-start(bf16[8,5120]{1,0:T(8,128)(2,1)S(1)} %get-tuple-element.10), channel_id=1, source_target_pairs={{0,16},{1,17},{2,18},{3,19},{4,20},{5,21},{6,22},{7,23},{8,24},{9,... | collective-permute-start | bytes 245768 | tf_op jit(solution)/shard_map/ppermute | solution.py:31
  17.5 5.1 %collective-permute-start.9 = (bf16[544,128]{1,0:T(8,128)(2,1)S(1)}, bf16[544,128]{1,0:T(8,128)(2,1)S(1)}, u32[]{:S(2)}, u32[]{:S(2)}) collective-permute-start(bf16[544,128]{1,0:T(8,128)(2,1)S(1)} %pad_maximum_fusion.8), channel_id=1, source_target_pairs={{0,2},{1,3},{2,0},{3,1},{4,6},{5,7},{6,4},{7,5},{8,10},{9,11},{10,... | collective-permute-start | bytes 417800 | tf_op jit(solution)/shard_map/ppermute | solution.py:31
  19.0 18.4 %copy-start = (bf16[256,128,128]{2,1,0:T(8,128)(2,1)S(1)}, bf16[256,128,128]{2,1,0:T(8,128)(2,1)}, u32[]{:S(2)}) copy-start(bf16[256,128,128]{2,1,0:T(8,128)(2,1)} %refs_1_.3) | copy-start | bytes 25165828
  19.0 7.0 %collective-permute-start.5 = (bf16[16,5120]{1,0:T(8,128)(2,1)S(1)}, bf16[16,5120]{1,0:T(8,128)(2,1)S(1)}, u32[]{:S(2)}, u32[]{:S(2)}) collective-permute-start(bf16[16,5120]{1,0:T(8,128)(2,1)S(1)} %pad_maximum_fusion.7), channel_id=1, source_target_pairs={{0,4},{1,5},{2,6},{3,7},{4,0},{5,1},{6,2},{7,3},{8,12},{9,13},{10,... | collective-permute-start | bytes 491528 | tf_op jit(solution)/shard_map/ppermute | solution.py:31
  20.6 7.2 %collective-permute-start.1 = (bf16[16,5120]{1,0:T(8,128)(2,1)S(1)}, bf16[16,5120]{1,0:T(8,128)(2,1)S(1)}, u32[]{:S(2)}, u32[]{:S(2)}) collective-permute-start(bf16[16,5120]{1,0:T(8,128)(2,1)S(1)} %pad_maximum_fusion.6), channel_id=1, source_target_pairs={{0,8},{1,9},{2,10},{3,11},{4,12},{5,13},{6,14},{7,15},{8,0},{9,1},... | collective-permute-start | bytes 491528 | tf_op jit(solution)/shard_map/ppermute | solution.py:31
  22.6 6.6 %collective-permute-start.10 = (bf16[1088,128]{1,0:T(8,128)(2,1)S(1)}, bf16[1088,128]{1,0:T(8,128)(2,1)S(1)}, u32[]{:S(2)}, u32[]{:S(2)}) collective-permute-start(bf16[1088,128]{1,0:T(8,128)(2,1)S(1)} %pad_maximum_fusion.5), channel_id=1, source_target_pairs={{0,4},{1,5},{2,6},{3,7},{4,0},{5,1},{6,2},{7,3},{8,12},{9,13},{10,... | collective-permute-start | bytes 835592 | tf_op jit(solution)/shard_map/ppermute | solution.py:31
  26.1 7.9 %collective-permute-start.6 = (bf16[32,5120]{1,0:T(8,128)(2,1)S(1)}, bf16[32,5120]{1,0:T(8,128)(2,1)S(1)}, u32[]{:S(2)}, u32[]{:S(2)}) collective-permute-start(bf16[32,5120]{1,0:T(8,128)(2,1)S(1)} %pad_maximum_fusion.4), channel_id=1, source_target_pairs={{0,8},{1,9},{2,10},{3,11},{4,12},{5,13},{6,14},{7,15},{8,0},{9,1},... | collective-permute-start | bytes 983048 | tf_op jit(solution)/shard_map/ppermute | solution.py:31
  27.8 9.4 %collective-permute-start.2 = (bf16[32,5120]{1,0:T(8,128)(2,1)S(1)}, bf16[32,5120]{1,0:T(8,128)(2,1)S(1)}, u32[]{:S(2)}, u32[]{:S(2)}) collective-permute-start(bf16[32,5120]{1,0:T(8,128)(2,1)S(1)} %pad_maximum_fusion.3), channel_id=1, source_target_pairs={{0,2},{1,3},{2,0},{3,1},{4,6},{5,7},{6,4},{7,5},{8,10},{9,11},{10,... | collective-permute-start | bytes 983048 | tf_op jit(solution)/shard_map/ppermute | solution.py:31
  29.3 8.2 %collective-permute-start.12 = (bf16[2176,128]{1,0:T(8,128)(2,1)S(1)}, bf16[2176,128]{1,0:T(8,128)(2,1)S(1)}, u32[]{:S(2)}, u32[]{:S(2)}) collective-permute-start(bf16[2176,128]{1,0:T(8,128)(2,1)S(1)} %pad_maximum_fusion.2.refs_0_), channel_id=1, source_target_pairs={{0,1},{1,0},{2,3},{3,2},{4,5},{5,4},{6,7},{7,6},{8,9},{9,8},{10,11... | collective-permute-start | bytes 1671176 | tf_op jit(solution)/shard_map/ppermute | solution.py:31
  29.3 15.8 %collective-permute-start.11 = (bf16[2176,128]{1,0:T(8,128)(2,1)S(1)}, bf16[2176,128]{1,0:T(8,128)(2,1)S(1)}, u32[]{:S(2)}, u32[]{:S(2)}) collective-permute-start(bf16[2176,128]{1,0:T(8,128)(2,1)S(1)} %pad_maximum_fusion.2.refs_0_), channel_id=1, source_target_pairs={{0,8},{1,9},{2,10},{3,11},{4,12},{5,13},{6,14},{7,15},{8,0},{9,1},... | collective-permute-start | bytes 1671176 | tf_op jit(solution)/shard_map/ppermute | solution.py:31
  34.0 3.4 %copy-start.1 = (s32[256]{0:T(256)S(1)}, s32[256]{0:T(256)}, u32[]{:S(2)}) copy-start(s32[256]{0:T(256)} %lens.5) | copy-start | bytes 3076
  34.0 15.0 %collective-permute-start.7 = (bf16[64,5120]{1,0:T(8,128)(2,1)S(1)}, bf16[64,5120]{1,0:T(8,128)(2,1)S(1)}, u32[]{:S(2)}, u32[]{:S(2)}) collective-permute-start(bf16[64,5120]{1,0:T(8,128)(2,1)S(1)} %pad_maximum_fusion.1), channel_id=1, source_target_pairs={{0,2},{1,3},{2,0},{3,1},{4,6},{5,7},{6,4},{7,5},{8,10},{9,11},{10,... | collective-permute-start | bytes 1966088 | tf_op jit(solution)/shard_map/ppermute | solution.py:31
  37.3 11.8 %collective-permute-start.3 = (bf16[64,5120]{1,0:T(8,128)(2,1)S(1)}, bf16[64,5120]{1,0:T(8,128)(2,1)S(1)}, u32[]{:S(2)}, u32[]{:S(2)}) collective-permute-start(bf16[64,5120]{1,0:T(8,128)(2,1)S(1)} %pad_maximum_fusion), channel_id=1, source_target_pairs={{0,4},{1,5},{2,6},{3,7},{4,0},{5,1},{6,2},{7,3},{8,12},{9,13},{10,... | collective-permute-start | bytes 1966088 | tf_op jit(solution)/shard_map/ppermute | solution.py:31
  45.2 4.0 %collective-permute-start.13 = (bf16[2176,128]{1,0:T(8,128)(2,1)S(1)}, bf16[2176,128]{1,0:T(8,128)(2,1)S(1)}, u32[]{:S(2)}, u32[]{:S(2)}) collective-permute-start(bf16[2176,128]{1,0:T(8,128)(2,1)S(1)} %collective-permute-done.11.refs_0_.refs_2_), channel_id=1, source_target_pairs={{0,1},{1,0},{2,3},{3,2},{4,5},{5,4},{6,7},{7,6},{8,9},{9,8},{10,11... | collective-permute-start | bytes 1671176 | tf_op jit(solution)/shard_map/ppermute | solution.py:31
  45.2 7.3 %slice-start = ((s8[10485760]{0:T(1024)(128)(4,1)}), s8[4194304]{0:T(1024)(128)(4,1)S(1)}, s32[]{:S(2)}) async-start(s8[10485760]{0:T(1024)(128)(4,1)} %bitcast.5), calls=%async_computation.1 | async-start | bytes 8388608
  45.2 7.3 %slice-start.1 = ((s8[10485760]{0:T(1024)(128)(4,1)}), s8[4194304]{0:T(1024)(128)(4,1)S(1)}, s32[]{:S(2)}) async-start(s8[10485760]{0:T(1024)(128)(4,1)} %bitcast.5), calls=%async_computation.2 | async-start | bytes 8388608
  49.1 3.3 %slice-start.2 = ((s8[10485760]{0:T(1024)(128)(4,1)}), s8[2097152]{0:T(1024)(128)(4,1)S(1)}, s32[]{:S(2)}) async-start(s8[10485760]{0:T(1024)(128)(4,1)} %bitcast.5), calls=%async_computation.3 | async-start | bytes 4194304
  49.2 3.3 %collective-permute-start.15 = (bf16[128,5120]{1,0:T(8,128)(2,1)S(1)}, bf16[128,5120]{1,0:T(8,128)(2,1)S(1)}, u32[]{:S(2)}, u32[]{:S(2)}) collective-permute-start(bf16[128,5120]{1,0:T(8,128)(2,1)S(1)} %constant_dynamic-update-slice_fusion.own), channel_id=1, source_target_pairs={{0,1},{1,0},{2,3},{3,2},{4,5},{5,4},{6,7},{7,6},{8,9},{9,8},{10,11... | collective-permute-start | bytes 3932168 | tf_op jit(solution)/shard_map/ppermute | solution.py:31
  49.2 4.9 %collective-permute-start.14 = (bf16[128,5120]{1,0:T(8,128)(2,1)S(1)}, bf16[128,5120]{1,0:T(8,128)(2,1)S(1)}, u32[]{:S(2)}, u32[]{:S(2)}) collective-permute-start(bf16[128,5120]{1,0:T(8,128)(2,1)S(1)} %constant_dynamic-update-slice_fusion.5.own), channel_id=1, source_target_pairs={{0,1},{1,0},{2,3},{3,2},{4,5},{5,4},{6,7},{7,6},{8,9},{9,8},{10,11... | collective-permute-start | bytes 3932168 | tf_op jit(solution)/shard_map/ppermute | solution.py:31

commit v7 on v6

--- a/solution.py
+++ b/solution.py
@@ -23,8 +23,9 @@
 
 def orders_of(n):
     bits = [1 << i for i in range(1, n.bit_length() - 1)]
-    far, rest = bits[-1:], bits[:-1]
-    return [[16, 2, 4, 8], [16, 8, 2, 4], [16, 4, 8, 2]]
+    far, rest = bits[-1:], bits[-3:-5:-1] + bits[:-4] + bits[-2:-1]
+    assert sorted(far + rest) == bits
+    return [far + rest, far + rest[-1:] + rest[:-1], far + rest[1:] + rest[:1]]
 
 
 def exchange(x, bit, n):

time: 69.2 us -> 69.2 us (level)
  no operation moved by 1% of the time
where the time goes in v7:
time: 69.2 us; the launch traced here: 68.9 us
  waiting for transfers between devices  24.3 us (35%)
  Pallas kernels  14.8 us (21%)
  starting transfers between devices  13.6 us (20%)
  blocking collectives  11.6 us (17%)
  local copies, waits for them, and re-layouts  2.51 us (4%)
  other arithmetic  1.14 us (2%)
  between operations  0.92 us (1%)
    ppermute x16, waiting for transfers between devices, exchange(): return lax.ppermute(x, 'dom', [(i, i ^ bit) for i in range(n)])  24.3 us
    ppermute x16, starting transfers between devices, exchange(): return lax.ppermute(x, 'dom', [(i, i ^ bit) for i in range(n)])  13.6 us
    all_to_all x1, blocking collectives, local(): lax.all_to_all(scored, 'dom', split_axis=0, concat_axis=0, tiled=True)  11.6 us
    pallas_call x3, Pallas kernels, local(): pl.pallas_call(functools.partial(maxsim_kernel, cand_at, cands, cap), out...  9.46 us
    pallas_call x1, Pallas kernels, local(): pl.pallas_call(functools.partial(prep_kernel, parts, slots, cap), out_sha...  2.02 us
    pallas_call x1, Pallas kernels, local(): pl.pallas_call(functools.partial(last_kernel, (masks, parts, cand_at, blo...  1.8 us
    pallas_call x1, Pallas kernels, local(): pl.pallas_call(beam_kernel, out_shape=partial, grid=(1,), in_specs=[left,...  1.54 us
  transfers between devices with their start and end apart: 16, of which 10 were waited for; matrix products, arithmetic and copies ran while one was open for 2% of the time, Pallas kernels for 19%

profile of v7, /device:TPU:0, one launch (start us, length us, event | category | flops | bytes accessed | tf_op | source)
XLA Modules:
  0.0 68.9 jit_solution(6314748519816998806)
XLA Ops:
  0.6 0.9 %fusion = (bf16[8,5120]{1,0:T(8,128)(2,1)S(1)}, bf16[8,5120]{1,0:T(8,128)(2,1)S(1)}) fusion(bf16[8,10240]{1,0:T(8,128)(2,1)} %param.9), kind=kLoop, calls=%fused_computation.19 | loop fusion | bytes 327680 | tf_op jit(solution)/shard_map/slice | solution.py:206
  1.6 4.1 %collective-permute-start.4 = (bf16[8,5120]{1,0:T(8,128)(2,1)S(1)}, bf16[8,5120]{1,0:T(8,128)(2,1)S(1)}, u32[]{:S(2)}, u32[]{:S(2)}) collective-permute-start(bf16[8,5120]{1,0:T(8,128)(2,1)S(1)} %get-tuple-element.11), channel_id=1, source_target_pairs={{0,16},{1,17},{2,18},{3,19},{4,20},{5,21},{6,22},{7,23},{8,24},{9,... | collective-permute-start | bytes 245768 | tf_op jit(solution)/shard_map/ppermute | solution.py:32
  5.7 2.0 %pack.1 = bf16[272,128]{1,0:T(8,128)(2,1)} custom-call(s32[3,8,16]{2,1,0:T(8,128)} %fo.1, s32[3,8,16]{2,1,0:T(8,128)} %fs.1, s32[8,32]{1,0:T(8,128)} %bitcast.10, s32[8,32]{1,0:T(8,128)} %cs.1, bf16[256,128]{1,0:T(8,128)(2,1)} %bitcast.8), custom_call_target="tpu_custom_call" | custom-call | tf_op jit(solution)/shard_map/pack/pallas_call | solution.py:208
  7.7 2.9 %collective-permute-start = (bf16[8,5120]{1,0:T(8,128)(2,1)S(1)}, bf16[8,5120]{1,0:T(8,128)(2,1)S(1)}, u32[]{:S(2)}, u32[]{:S(2)}) collective-permute-start(bf16[8,5120]{1,0:T(8,128)(2,1)S(1)} %get-tuple-element.10), channel_id=1, source_target_pairs={{0,16},{1,17},{2,18},{3,19},{4,20},{5,21},{6,22},{7,23},{8,24},{9,... | collective-permute-start | bytes 245768 | tf_op jit(solution)/shard_map/ppermute | solution.py:32
  10.6 5.9 %collective-permute-done.8 = bf16[272,128]{1,0:T(8,128)(2,1)S(1)} collective-permute-done((bf16[272,128]{1,0:T(8,128)(2,1)}, bf16[272,128]{1,0:T(8,128)(2,1)S(1)}, u32[]{:S(2)}, u32[]{:S(2)}) %collective-permute-start.8) | collective-permute-done | bytes 69664 | tf_op jit(solution)/shard_map/ppermute | solution.py:32
  16.6 0.9 %pad_maximum_fusion.8 = bf16[544,128]{1,0:T(8,128)(2,1)S(1)} fusion(bf16[272,128]{1,0:T(8,128)(2,1)S(1)} %collective-permute-done.8, bf16[272,128]{1,0:T(8,128)(2,1)} %pack.1), kind=kLoop, calls=%fused_computation.8 | loop fusion | flops 278528 | bytes 278528 | tf_op jit(solution)/shard_map/concatenate | solution.py:222
  17.5 1.6 %collective-permute-start.9 = (bf16[544,128]{1,0:T(8,128)(2,1)S(1)}, bf16[544,128]{1,0:T(8,128)(2,1)S(1)}, u32[]{:S(2)}, u32[]{:S(2)}) collective-permute-start(bf16[544,128]{1,0:T(8,128)(2,1)S(1)} %pad_maximum_fusion.8), channel_id=1, source_target_pairs={{0,4},{1,5},{2,6},{3,7},{4,0},{5,1},{6,2},{7,3},{8,12},{9,13},{10,... | collective-permute-start | bytes 417800 | tf_op jit(solution)/shard_map/ppermute | solution.py:32
  19.1 1.6 %collective-permute-start.5 = (bf16[16,5120]{1,0:T(8,128)(2,1)S(1)}, bf16[16,5120]{1,0:T(8,128)(2,1)S(1)}, u32[]{:S(2)}, u32[]{:S(2)}) collective-permute-start(bf16[16,5120]{1,0:T(8,128)(2,1)S(1)} %pad_maximum_fusion.7), channel_id=1, source_target_pairs={{0,2},{1,3},{2,0},{3,1},{4,6},{5,7},{6,4},{7,5},{8,10},{9,11},{10,... | collective-permute-start | bytes 491528 | tf_op jit(solution)/shard_map/ppermute | solution.py:32
  20.8 1.8 %collective-permute-done.9 = bf16[544,128]{1,0:T(8,128)(2,1)S(1)} collective-permute-done((bf16[544,128]{1,0:T(8,128)(2,1)S(1)}, bf16[544,128]{1,0:T(8,128)(2,1)S(1)}, u32[]{:S(2)}, u32[]{:S(2)}) %collective-permute-start.9) | collective-permute-done | bytes 139296 | tf_op jit(solution)/shard_map/ppermute | solution.py:32
  22.6 1.6 %collective-permute-start.10 = (bf16[1088,128]{1,0:T(8,128)(2,1)S(1)}, bf16[1088,128]{1,0:T(8,128)(2,1)S(1)}, u32[]{:S(2)}, u32[]{:S(2)}) collective-permute-start(bf16[1088,128]{1,0:T(8,128)(2,1)S(1)} %pad_maximum_fusion.5), channel_id=1, source_target_pairs={{0,2},{1,3},{2,0},{3,1},{4,6},{5,7},{6,4},{7,5},{8,10},{9,11},{10,... | collective-permute-start | bytes 835592 | tf_op jit(solution)/shard_map/ppermute | solution.py:32
  24.2 1.9 %collective-permute-done.5 = bf16[16,5120]{1,0:T(8,128)(2,1)S(1)} collective-permute-done((bf16[16,5120]{1,0:T(8,128)(2,1)S(1)}, bf16[16,5120]{1,0:T(8,128)(2,1)S(1)}, u32[]{:S(2)}, u32[]{:S(2)}) %collective-permute-start.5) | collective-permute-done | bytes 163872 | tf_op jit(solution)/shard_map/ppermute | solution.py:32
  26.1 0.1 collective-permute-start.6
  26.2 1.6 %collective-permute-done.1 = bf16[16,5120]{1,0:T(8,128)(2,1)S(1)} collective-permute-done((bf16[16,5120]{1,0:T(8,128)(2,1)S(1)}, bf16[16,5120]{1,0:T(8,128)(2,1)S(1)}, u32[]{:S(2)}, u32[]{:S(2)}) %collective-permute-start.1) | collective-permute-done | bytes 163872 | tf_op jit(solution)/shard_map/ppermute | solution.py:32
  27.8 0.5 collective-permute-start.2
  28.3 0.9 %collective-permute-done.10 = bf16[1088,128]{1,0:T(8,128)(2,1)S(1)} collective-permute-done((bf16[1088,128]{1,0:T(8,128)(2,1)S(1)}, bf16[1088,128]{1,0:T(8,128)(2,1)S(1)}, u32[]{:S(2)}, u32[]{:S(2)}) %collective-permute-start.10) | collective-permute-done | bytes 278560 | tf_op jit(solution)/shard_map/ppermute | solution.py:32
  29.3 0.1 collective-permute-start.12
  29.3 0.5 collective-permute-start.11
  29.8 4.1 %collective-permute-done.6 = bf16[32,5120]{1,0:T(8,128)(2,1)S(1)} collective-permute-done((bf16[32,5120]{1,0:T(8,128)(2,1)S(1)}, bf16[32,5120]{1,0:T(8,128)(2,1)S(1)}, u32[]{:S(2)}, u32[]{:S(2)}) %collective-permute-start.6) | collective-permute-done | bytes 327712 | tf_op jit(solution)/shard_map/ppermute | solution.py:32
  34.1 3.1 %collective-permute-done.2 = bf16[32,5120]{1,0:T(8,128)(2,1)S(1)} collective-permute-done((bf16[32,5120]{1,0:T(8,128)(2,1)S(1)}, bf16[32,5120]{1,0:T(8,128)(2,1)S(1)}, u32[]{:S(2)}, u32[]{:S(2)}) %collective-permute-start.2) | collective-permute-done | bytes 327712 | tf_op jit(solution)/shard_map/ppermute | solution.py:32
  37.4 4.1 %maxsim.3.refs_4_ = f32[16,8,128]{2,1,0:T(8,128)S(1)} custom-call(s32[1]{0:T(128)} %bitcast.me_ref, s32[256]{0:T(256)S(1)} %copy-done.1, bf16[2176,128]{1,0:T(8,128)(2,1)S(1)} %pad_maximum_fusion.2.refs_0_, bf16[2176,128]{1,0:T(8,128)(2,1)S(1)} %collective-permute-done.12.refs_1_, bf16[256,128,128]{2,1,0:T(8,128)(2,1)S(1)} %copy-done), custom_call_target="tpu_custom_call" | custom-call | flops 2147483648 | bytes 8388608 | tf_op jit(solution)/shard_map/maxsim/pallas_call | solution.py:232
  41.6 3.6 %collective-permute-done.11.refs_0_.refs_2_ = bf16[2176,128]{1,0:T(8,128)(2,1)S(1)} collective-permute-done((bf16[2176,128]{1,0:T(8,128)(2,1)S(1)}, bf16[2176,128]{1,0:T(8,128)(2,1)S(1)}, u32[]{:S(2)}, u32[]{:S(2)}) %collective-permute-start.11) | collective-permute-done | bytes 557088 | tf_op jit(solution)/shard_map/ppermute | solution.py:32
  45.2 2.7 %maxsim.4.refs_5_ = f32[8,8,128]{2,1,0:T(8,128)S(1)} custom-call(s32[1]{0:T(128)} %bitcast.me_ref, s32[256]{0:T(256)S(1)} %copy-done.1, bf16[2176,128]{1,0:T(8,128)(2,1)S(1)} %collective-permute-done.11.refs_0_.refs_2_, bf16[256,128,128]{2,1,0:T(8,128)(2,1)S(1)} %copy-done), custom_call_target="tpu_custom_call" | custom-call | flops 1073741824 | bytes 8388608 | tf_op jit(solution)/shard_map/maxsim/pallas_call | solution.py:232
  47.9 1.2 %collective-permute-done.7 = bf16[64,5120]{1,0:T(8,128)(2,1)S(1)} collective-permute-done((bf16[64,5120]{1,0:T(8,128)(2,1)S(1)}, bf16[64,5120]{1,0:T(8,128)(2,1)S(1)}, u32[]{:S(2)}, u32[]{:S(2)}) %collective-permute-start.7) | collective-permute-done | bytes 655392 | tf_op jit(solution)/shard_map/ppermute | solution.py:32
  49.2 0.5 collective-permute-start.14
  49.7 2.7 %maxsim.5.refs_6_ = f32[8,8,128]{2,1,0:T(8,128)S(1)} custom-call(s32[1]{0:T(128)} %bitcast.me_ref, s32[256]{0:T(256)S(1)} %copy-done.1, bf16[2176,128]{1,0:T(8,128)(2,1)S(1)} %collective-permute-done.13.refs_0_.refs_3_, bf16[256,128,128]{2,1,0:T(8,128)(2,1)S(1)} %copy-done), custom_call_target="tpu_custom_call" | custom-call | flops 1073741824 | bytes 8388608 | tf_op jit(solution)/shard_map/maxsim/pallas_call | solution.py:232
  52.5 1.5 %beam.1.first = f32[256,512]{1,0:T(8,128)S(1)} custom-call(bf16[128,5120]{1,0:T(8,128)(2,1)S(1)} %constant_dynamic-update-slice_fusion.own, bf16[128,5120]{1,0:T(8,128)(2,1)S(1)} %collective-permute-done.15.other, bf16[512,10240]{1,0:T(8,128)(2,1)S(1)} %bitcast.6), custom_call_target="tpu_custom_call" | custom-call | flops 1342177280 | bytes 7864320 | tf_op jit(solution)/shard_map/beam/pallas_call | solution.py:266
  54.0 0.1 collective-permute-done.14.other
  54.1 1.8 %beam_last.1 = f32[32,8,128]{2,1,0:T(8,128)S(1)} custom-call(s32[1]{0:T(128)} %bitcast.me_ref, bf16[128,5120]{1,0:T(8,128)(2,1)S(1)} %constant_dynamic-update-slice_fusion.5.own, bf16[128,5120]{1,0:T(8,128)(2,1)S(1)} %collective-permute-done.14.other, bf16[512,10240]{1,0:T(8,128)(2,1)S(1)} %bitcast.6, f32[256,512]{1,0:T(8,128)S(1)} %beam.1.first, ...), custom_call_target="tpu_custom_call" | custom-call | flops 1342177280 | bytes 7864320 | tf_op jit(solution)/shard_map/beam_last/pallas_call | solution.py:277
  55.9 11.6 %all_to_all.5 = f32[32,8,128]{2,1,0:T(8,128)S(1)} all-to-all(f32[32,8,128]{2,1,0:T(8,128)S(1)} %beam_last.1), channel_id=1, replica_groups=mesh['dom'=32,'rep'=1] {'dom'}, dimensions={0} | all-to-all | bytes 262144 | tf_op jit(solution)/shard_map/all_to_all | solution.py:292
  67.6 0.7 slice.15
  68.2 0.1 reshape.22
  68.3 0.6 copy.12
  (43 shorter events, 0.8 us)
Async XLA Ops:
  1.6 17.5 %collective-permute-start.4 = (bf16[8,5120]{1,0:T(8,128)(2,1)S(1)}, bf16[8,5120]{1,0:T(8,128)(2,1)S(1)}, u32[]{:S(2)}, u32[]{:S(2)}) collective-permute-start(bf16[8,5120]{1,0:T(8,128)(2,1)S(1)} %get-tuple-element.11), channel_id=1, source_target_pairs={{0,16},{1,17},{2,18},{3,19},{4,20},{5,21},{6,22},{7,23},{8,24},{9,... | collective-permute-start | bytes 245768 | tf_op jit(solution)/shard_map/ppermute | solution.py:32
  7.7 14.9 %copy-start.2 = (bf16[272,128]{1,0:T(8,128)(2,1)S(1)}, bf16[272,128]{1,0:T(8,128)(2,1)}, u32[]{:S(2)}) copy-start(bf16[272,128]{1,0:T(8,128)(2,1)} %pack.1) | copy-start | bytes 208900
  7.7 8.9 %collective-permute-start.8 = (bf16[272,128]{1,0:T(8,128)(2,1)}, bf16[272,128]{1,0:T(8,128)(2,1)S(1)}, u32[]{:S(2)}, u32[]{:S(2)}) collective-permute-start(bf16[272,128]{1,0:T(8,128)(2,1)} %pack.1), channel_id=1, source_target_pairs={{0,16},{1,17},{2,18},{3,19},{4,20},{5,21},{6,22},{7,23},{8,24},{9,... | collective-permute-start | bytes 208904 | tf_op jit(solution)/shard_map/ppermute | solution.py:32
  7.7 12.9 %collective-permute-start = (bf16[8,5120]{1,0:T(8,128)(2,1)S(1)}, bf16[8,5120]{1,0:T(8,128)(2,1)S(1)}, u32[]{:S(2)}, u32[]{:S(2)}) collective-permute-start(bf16[8,5120]{1,0:T(8,128)(2,1)S(1)} %get-tuple-element.10), channel_id=1, source_target_pairs={{0,16},{1,17},{2,18},{3,19},{4,20},{5,21},{6,22},{7,23},{8,24},{9,... | collective-permute-start | bytes 245768 | tf_op jit(solution)/shard_map/ppermute | solution.py:32
  17.5 5.1 %collective-permute-start.9 = (bf16[544,128]{1,0:T(8,128)(2,1)S(1)}, bf16[544,128]{1,0:T(8,128)(2,1)S(1)}, u32[]{:S(2)}, u32[]{:S(2)}) collective-permute-start(bf16[544,128]{1,0:T(8,128)(2,1)S(1)} %pad_maximum_fusion.8), channel_id=1, source_target_pairs={{0,4},{1,5},{2,6},{3,7},{4,0},{5,1},{6,2},{7,3},{8,12},{9,13},{10,... | collective-permute-start | bytes 417800 | tf_op jit(solution)/shard_map/ppermute | solution.py:32
  19.1 18.4 %copy-start = (bf16[256,128,128]{2,1,0:T(8,128)(2,1)S(1)}, bf16[256,128,128]{2,1,0:T(8,128)(2,1)}, u32[]{:S(2)}) copy-start(bf16[256,128,128]{2,1,0:T(8,128)(2,1)} %refs_1_.3) | copy-start | bytes 25165828
  19.1 7.0 %collective-permute-start.5 = (bf16[16,5120]{1,0:T(8,128)(2,1)S(1)}, bf16[16,5120]{1,0:T(8,128)(2,1)S(1)}, u32[]{:S(2)}, u32[]{:S(2)}) collective-permute-start(bf16[16,5120]{1,0:T(8,128)(2,1)S(1)} %pad_maximum_fusion.7), channel_id=1, source_target_pairs={{0,2},{1,3},{2,0},{3,1},{4,6},{5,7},{6,4},{7,5},{8,10},{9,11},{10,... | collective-permute-start | bytes 491528 | tf_op jit(solution)/shard_map/ppermute | solution.py:32
  20.6 7.2 %collective-permute-start.1 = (bf16[16,5120]{1,0:T(8,128)(2,1)S(1)}, bf16[16,5120]{1,0:T(8,128)(2,1)S(1)}, u32[]{:S(2)}, u32[]{:S(2)}) collective-permute-start(bf16[16,5120]{1,0:T(8,128)(2,1)S(1)} %pad_maximum_fusion.6), channel_id=1, source_target_pairs={{0,8},{1,9},{2,10},{3,11},{4,12},{5,13},{6,14},{7,15},{8,0},{9,1},... | collective-permute-start | bytes 491528 | tf_op jit(solution)/shard_map/ppermute | solution.py:32
  22.6 6.6 %collective-permute-start.10 = (bf16[1088,128]{1,0:T(8,128)(2,1)S(1)}, bf16[1088,128]{1,0:T(8,128)(2,1)S(1)}, u32[]{:S(2)}, u32[]{:S(2)}) collective-permute-start(bf16[1088,128]{1,0:T(8,128)(2,1)S(1)} %pad_maximum_fusion.5), channel_id=1, source_target_pairs={{0,2},{1,3},{2,0},{3,1},{4,6},{5,7},{6,4},{7,5},{8,10},{9,11},{10,... | collective-permute-start | bytes 835592 | tf_op jit(solution)/shard_map/ppermute | solution.py:32
  26.1 7.9 %collective-permute-start.6 = (bf16[32,5120]{1,0:T(8,128)(2,1)S(1)}, bf16[32,5120]{1,0:T(8,128)(2,1)S(1)}, u32[]{:S(2)}, u32[]{:S(2)}) collective-permute-start(bf16[32,5120]{1,0:T(8,128)(2,1)S(1)} %pad_maximum_fusion.4), channel_id=1, source_target_pairs={{0,8},{1,9},{2,10},{3,11},{4,12},{5,13},{6,14},{7,15},{8,0},{9,1},... | collective-permute-start | bytes 983048 | tf_op jit(solution)/shard_map/ppermute | solution.py:32
  27.8 9.4 %collective-permute-start.2 = (bf16[32,5120]{1,0:T(8,128)(2,1)S(1)}, bf16[32,5120]{1,0:T(8,128)(2,1)S(1)}, u32[]{:S(2)}, u32[]{:S(2)}) collective-permute-start(bf16[32,5120]{1,0:T(8,128)(2,1)S(1)} %pad_maximum_fusion.3), channel_id=1, source_target_pairs={{0,4},{1,5},{2,6},{3,7},{4,0},{5,1},{6,2},{7,3},{8,12},{9,13},{10,... | collective-permute-start | bytes 983048 | tf_op jit(solution)/shard_map/ppermute | solution.py:32
  29.3 8.1 %collective-permute-start.12 = (bf16[2176,128]{1,0:T(8,128)(2,1)S(1)}, bf16[2176,128]{1,0:T(8,128)(2,1)S(1)}, u32[]{:S(2)}, u32[]{:S(2)}) collective-permute-start(bf16[2176,128]{1,0:T(8,128)(2,1)S(1)} %pad_maximum_fusion.2.refs_0_), channel_id=1, source_target_pairs={{0,1},{1,0},{2,3},{3,2},{4,5},{5,4},{6,7},{7,6},{8,9},{9,8},{10,11... | collective-permute-start | bytes 1671176 | tf_op jit(solution)/shard_map/ppermute | solution.py:32
  29.3 15.8 %collective-permute-start.11 = (bf16[2176,128]{1,0:T(8,128)(2,1)S(1)}, bf16[2176,128]{1,0:T(8,128)(2,1)S(1)}, u32[]{:S(2)}, u32[]{:S(2)}) collective-permute-start(bf16[2176,128]{1,0:T(8,128)(2,1)S(1)} %pad_maximum_fusion.2.refs_0_), channel_id=1, source_target_pairs={{0,8},{1,9},{2,10},{3,11},{4,12},{5,13},{6,14},{7,15},{8,0},{9,1},... | collective-permute-start | bytes 1671176 | tf_op jit(solution)/shard_map/ppermute | solution.py:32
  34.0 3.4 %copy-start.1 = (s32[256]{0:T(256)S(1)}, s32[256]{0:T(256)}, u32[]{:S(2)}) copy-start(s32[256]{0:T(256)} %lens.5) | copy-start | bytes 3076
  34.0 15.0 %collective-permute-start.7 = (bf16[64,5120]{1,0:T(8,128)(2,1)S(1)}, bf16[64,5120]{1,0:T(8,128)(2,1)S(1)}, u32[]{:S(2)}, u32[]{:S(2)}) collective-permute-start(bf16[64,5120]{1,0:T(8,128)(2,1)S(1)} %pad_maximum_fusion.1), channel_id=1, source_target_pairs={{0,4},{1,5},{2,6},{3,7},{4,0},{5,1},{6,2},{7,3},{8,12},{9,13},{10,... | collective-permute-start | bytes 1966088 | tf_op jit(solution)/shard_map/ppermute | solution.py:32
  37.2 11.8 %collective-permute-start.3 = (bf16[64,5120]{1,0:T(8,128)(2,1)S(1)}, bf16[64,5120]{1,0:T(8,128)(2,1)S(1)}, u32[]{:S(2)}, u32[]{:S(2)}) collective-permute-start(bf16[64,5120]{1,0:T(8,128)(2,1)S(1)} %pad_maximum_fusion), channel_id=1, source_target_pairs={{0,2},{1,3},{2,0},{3,1},{4,6},{5,7},{6,4},{7,5},{8,10},{9,11},{10,... | collective-permute-start | bytes 1966088 | tf_op jit(solution)/shard_map/ppermute | solution.py:32
  45.2 4.0 %collective-permute-start.13 = (bf16[2176,128]{1,0:T(8,128)(2,1)S(1)}, bf16[2176,128]{1,0:T(8,128)(2,1)S(1)}, u32[]{:S(2)}, u32[]{:S(2)}) collective-permute-start(bf16[2176,128]{1,0:T(8,128)(2,1)S(1)} %collective-permute-done.11.refs_0_.refs_2_), channel_id=1, source_target_pairs={{0,1},{1,0},{2,3},{3,2},{4,5},{5,4},{6,7},{7,6},{8,9},{9,8},{10,11... | collective-permute-start | bytes 1671176 | tf_op jit(solution)/shard_map/ppermute | solution.py:32
  45.2 7.3 %slice-start = ((s8[10485760]{0:T(1024)(128)(4,1)}), s8[4194304]{0:T(1024)(128)(4,1)S(1)}, s32[]{:S(2)}) async-start(s8[10485760]{0:T(1024)(128)(4,1)} %bitcast.5), calls=%async_computation.1 | async-start | bytes 8388608
  45.2 7.3 %slice-start.1 = ((s8[10485760]{0:T(1024)(128)(4,1)}), s8[4194304]{0:T(1024)(128)(4,1)S(1)}, s32[]{:S(2)}) async-start(s8[10485760]{0:T(1024)(128)(4,1)} %bitcast.5), calls=%async_computation.2 | async-start | bytes 8388608
  49.1 3.3 %slice-start.2 = ((s8[10485760]{0:T(1024)(128)(4,1)}), s8[2097152]{0:T(1024)(128)(4,1)S(1)}, s32[]{:S(2)}) async-start(s8[10485760]{0:T(1024)(128)(4,1)} %bitcast.5), calls=%async_computation.3 | async-start | bytes 4194304
  49.2 3.3 %collective-permute-start.15 = (bf16[128,5120]{1,0:T(8,128)(2,1)S(1)}, bf16[128,5120]{1,0:T(8,128)(2,1)S(1)}, u32[]{:S(2)}, u32[]{:S(2)}) collective-permute-start(bf16[128,5120]{1,0:T(8,128)(2,1)S(1)} %constant_dynamic-update-slice_fusion.own), channel_id=1, source_target_pairs={{0,1},{1,0},{2,3},{3,2},{4,5},{5,4},{6,7},{7,6},{8,9},{9,8},{10,11... | collective-permute-start | bytes 3932168 | tf_op jit(solution)/shard_map/ppermute | solution.py:32
  49.2 4.9 %collective-permute-start.14 = (bf16[128,5120]{1,0:T(8,128)(2,1)S(1)}, bf16[128,5120]{1,0:T(8,128)(2,1)S(1)}, u32[]{:S(2)}, u32[]{:S(2)}) collective-permute-start(bf16[128,5120]{1,0:T(8,128)(2,1)S(1)} %constant_dynamic-update-slice_fusion.5.own), channel_id=1, source_target_pairs={{0,1},{1,0},{2,3},{3,2},{4,5},{5,4},{6,7},{7,6},{8,9},{9,8},{10,11... | collective-permute-start | bytes 3932168 | tf_op jit(solution)/shard_map/ppermute | solution.py:32

commit v8 on v7

--- a/solution.py
+++ b/solution.py
@@ -85,13 +85,13 @@
     out[rows:, :] = jnp.concatenate([codes, table], axis=0).astype(jnp.bfloat16)
 
 
-def maxsim_kernel(cand_at, cands, cap, me_ref, lens, *refs):
+def maxsim_kernel(cand_at, cands, cap, lens, *refs):
     *sides, tiles, out, listed, lst, sem = refs
     blocks = out.shape[0] // len(sides)
     stride = sides[0].shape[0] // blocks
     pt = tiles.shape[1]
     qt = (stride - 16) // 8
-    start = me_ref[0] * cap
+    start = lens[tiles.shape[0]] * cap
     row, lane = ids((8, LANES), 0), ids((8, LANES), 1)
     group = start // LANES
     for side, ref in enumerate(sides):
@@ -229,11 +229,12 @@
     tok = [(tok[0], exchange(tok[0], 1, n)), tok[1]]
 
     pt = passage_tiles.shape[1]
+    scalars = jnp.concatenate([passage_len, me.reshape(1)])
     score = lambda *sides: pl.pallas_call(
             functools.partial(maxsim_kernel, cand_at, cands, cap),
             out_shape=jax.ShapeDtypeStruct((n // 4 * len(sides), 8, LANES), jnp.float32),
             grid_spec=pltpu.PrefetchScalarGridSpec(
-                num_scalar_prefetch=2,
+                num_scalar_prefetch=1,
                 grid=(),
                 in_specs=[VMEM] * (len(sides) + 1),
                 out_specs=VMEM,
@@ -246,7 +247,7 @@
             compiler_params=pltpu.CompilerParams(vmem_limit_bytes=16 << 20),
             cost_estimate=pl.CostEstimate(flops=4 * len(sides) * slots * pt * qt * dim, bytes_accessed=8 << 20, transcendentals=0),
             name="maxsim",
-        )(me.reshape(1), passage_len, *sides, passage_tiles)
+        )(scalars, *sides, passage_tiles)
 
     early = score(*tok[0])
     late, early = lax.optimization_barrier((tok[1], early))
@@ -291,7 +292,7 @@
 
     returned = lax.all_to_all(scored, "dom", split_axis=0, concat_axis=0, tiled=True)
     total = jnp.sum(returned, axis=0)
-    beam = total[:, :cand_at].reshape(queries, rounds, front).transpose(1, 0, 2)
+    beam = jnp.stack([total[:, r * front : (r + 1) * front] for r in range(rounds)])
     return beam, total[:, cand_at : cand_at + cands]
 
 

time: 69.2 us -> 69.2 us (level)
  other arithmetic: 1.14 us -> 2.46 us
  waiting for transfers between devices: 24.3 us -> 23.6 us
    ppermute x16, waiting for transfers between devices: 24.3 us -> 23.6 us  [exchange(): return lax.ppermute(x, 'dom', [(i, i ^ bit) for i in range(n)])]
  transfers between devices with their start and end apart: 16 -> 16, of which waited for: 10 -> 10; matrix products, arithmetic and copies ran while one was open for 2% -> 3% of each run, Pallas kernels for 19% -> 19%
where the time goes in v8:
time: 69.2 us; the launch traced here: 68.9 us
  waiting for transfers between devices  23.6 us (34%)
  Pallas kernels  14.9 us (22%)
  starting transfers between devices  13.6 us (20%)
  blocking collectives  11.6 us (17%)
  other arithmetic  2.46 us (4%)
  local copies, waits for them, and re-layouts  1.89 us (3%)
  between operations  0.9 us (1%)
    ppermute x16, waiting for transfers between devices, exchange(): return lax.ppermute(x, 'dom', [(i, i ^ bit) for i in range(n)])  23.6 us
    ppermute x16, starting transfers between devices, exchange(): return lax.ppermute(x, 'dom', [(i, i ^ bit) for i in range(n)])  13.6 us
    all_to_all x1, blocking collectives, local(): lax.all_to_all(scored, 'dom', split_axis=0, concat_axis=0, tiled=True)  11.6 us
    pallas_call x3, Pallas kernels, local(): pl.pallas_call(functools.partial(maxsim_kernel, cand_at, cands, cap), out...  9.51 us
    pallas_call x1, Pallas kernels, local(): pl.pallas_call(functools.partial(prep_kernel, parts, slots, cap), out_sha...  2.02 us
    pallas_call x1, Pallas kernels, local(): pl.pallas_call(functools.partial(last_kernel, (masks, parts, cand_at, blo...  1.79 us
    pallas_call x1, Pallas kernels, local(): pl.pallas_call(beam_kernel, out_shape=partial, grid=(1,), in_specs=[left,...  1.54 us
  transfers between devices with their start and end apart: 16, of which 10 were waited for; matrix products, arithmetic and copies ran while one was open for 3% of the time, Pallas kernels for 19%

profile of v8, /device:TPU:0, one launch (start us, length us, event | category | flops | bytes accessed | tf_op | source)
XLA Modules:
  0.0 68.9 jit_solution(10775484862473590747)
XLA Ops:
  0.6 0.9 %fusion = (bf16[8,5120]{1,0:T(8,128)(2,1)S(1)}, bf16[8,5120]{1,0:T(8,128)(2,1)S(1)}) fusion(bf16[8,10240]{1,0:T(8,128)(2,1)} %param.9), kind=kLoop, calls=%fused_computation.24 | loop fusion | bytes 327680 | tf_op jit(solution)/shard_map/slice | solution.py:206
  1.6 4.1 %collective-permute-start.4 = (bf16[8,5120]{1,0:T(8,128)(2,1)S(1)}, bf16[8,5120]{1,0:T(8,128)(2,1)S(1)}, u32[]{:S(2)}, u32[]{:S(2)}) collective-permute-start(bf16[8,5120]{1,0:T(8,128)(2,1)S(1)} %get-tuple-element.11), channel_id=1, source_target_pairs={{0,16},{1,17},{2,18},{3,19},{4,20},{5,21},{6,22},{7,23},{8,24},{9,... | collective-permute-start | bytes 245768 | tf_op jit(solution)/shard_map/ppermute | solution.py:32
  5.7 2.0 %pack.1 = bf16[272,128]{1,0:T(8,128)(2,1)} custom-call(s32[3,8,16]{2,1,0:T(8,128)} %fo.1, s32[3,8,16]{2,1,0:T(8,128)} %fs.1, s32[8,32]{1,0:T(8,128)} %bitcast.12, s32[8,32]{1,0:T(8,128)} %cs.1, bf16[256,128]{1,0:T(8,128)(2,1)} %bitcast.11), custom_call_target="tpu_custom_call" | custom-call | tf_op jit(solution)/shard_map/pack/pallas_call | solution.py:208
  7.7 2.9 %collective-permute-start = (bf16[8,5120]{1,0:T(8,128)(2,1)S(1)}, bf16[8,5120]{1,0:T(8,128)(2,1)S(1)}, u32[]{:S(2)}, u32[]{:S(2)}) collective-permute-start(bf16[8,5120]{1,0:T(8,128)(2,1)S(1)} %get-tuple-element.10), channel_id=1, source_target_pairs={{0,16},{1,17},{2,18},{3,19},{4,20},{5,21},{6,22},{7,23},{8,24},{9,... | collective-permute-start | bytes 245768 | tf_op jit(solution)/shard_map/ppermute | solution.py:32
  10.6 0.7 pad_add_fusion.lens
  11.3 5.2 %collective-permute-done.8 = bf16[272,128]{1,0:T(8,128)(2,1)S(1)} collective-permute-done((bf16[272,128]{1,0:T(8,128)(2,1)}, bf16[272,128]{1,0:T(8,128)(2,1)S(1)}, u32[]{:S(2)}, u32[]{:S(2)}) %collective-permute-start.8) | collective-permute-done | bytes 69664 | tf_op jit(solution)/shard_map/ppermute | solution.py:32
  16.6 0.9 %pad_maximum_fusion.8 = bf16[544,128]{1,0:T(8,128)(2,1)S(1)} fusion(bf16[272,128]{1,0:T(8,128)(2,1)S(1)} %collective-permute-done.8, bf16[272,128]{1,0:T(8,128)(2,1)} %pack.1), kind=kLoop, calls=%fused_computation.8 | loop fusion | flops 278528 | bytes 278528 | tf_op jit(solution)/shard_map/concatenate | solution.py:222
  17.5 1.6 %collective-permute-start.9 = (bf16[544,128]{1,0:T(8,128)(2,1)S(1)}, bf16[544,128]{1,0:T(8,128)(2,1)S(1)}, u32[]{:S(2)}, u32[]{:S(2)}) collective-permute-start(bf16[544,128]{1,0:T(8,128)(2,1)S(1)} %pad_maximum_fusion.8), channel_id=1, source_target_pairs={{0,4},{1,5},{2,6},{3,7},{4,0},{5,1},{6,2},{7,3},{8,12},{9,13},{10,... | collective-permute-start | bytes 417800 | tf_op jit(solution)/shard_map/ppermute | solution.py:32
  19.1 1.6 %collective-permute-start.5 = (bf16[16,5120]{1,0:T(8,128)(2,1)S(1)}, bf16[16,5120]{1,0:T(8,128)(2,1)S(1)}, u32[]{:S(2)}, u32[]{:S(2)}) collective-permute-start(bf16[16,5120]{1,0:T(8,128)(2,1)S(1)} %pad_maximum_fusion.7), channel_id=1, source_target_pairs={{0,2},{1,3},{2,0},{3,1},{4,6},{5,7},{6,4},{7,5},{8,10},{9,11},{10,... | collective-permute-start | bytes 491528 | tf_op jit(solution)/shard_map/ppermute | solution.py:32
  20.8 1.8 %collective-permute-done.9 = bf16[544,128]{1,0:T(8,128)(2,1)S(1)} collective-permute-done((bf16[544,128]{1,0:T(8,128)(2,1)S(1)}, bf16[544,128]{1,0:T(8,128)(2,1)S(1)}, u32[]{:S(2)}, u32[]{:S(2)}) %collective-permute-start.9) | collective-permute-done | bytes 139296 | tf_op jit(solution)/shard_map/ppermute | solution.py:32
  22.6 1.6 %collective-permute-start.10 = (bf16[1088,128]{1,0:T(8,128)(2,1)S(1)}, bf16[1088,128]{1,0:T(8,128)(2,1)S(1)}, u32[]{:S(2)}, u32[]{:S(2)}) collective-permute-start(bf16[1088,128]{1,0:T(8,128)(2,1)S(1)} %pad_maximum_fusion.5), channel_id=1, source_target_pairs={{0,2},{1,3},{2,0},{3,1},{4,6},{5,7},{6,4},{7,5},{8,10},{9,11},{10,... | collective-permute-start | bytes 835592 | tf_op jit(solution)/shard_map/ppermute | solution.py:32
  24.2 1.9 %collective-permute-done.5 = bf16[16,5120]{1,0:T(8,128)(2,1)S(1)} collective-permute-done((bf16[16,5120]{1,0:T(8,128)(2,1)S(1)}, bf16[16,5120]{1,0:T(8,128)(2,1)S(1)}, u32[]{:S(2)}, u32[]{:S(2)}) %collective-permute-start.5) | collective-permute-done | bytes 163872 | tf_op jit(solution)/shard_map/ppermute | solution.py:32
  26.2 1.6 %collective-permute-done.1 = bf16[16,5120]{1,0:T(8,128)(2,1)S(1)} collective-permute-done((bf16[16,5120]{1,0:T(8,128)(2,1)S(1)}, bf16[16,5120]{1,0:T(8,128)(2,1)S(1)}, u32[]{:S(2)}, u32[]{:S(2)}) %collective-permute-start.1) | collective-permute-done | bytes 163872 | tf_op jit(solution)/shard_map/ppermute | solution.py:32
  27.8 0.5 collective-permute-start.2
  28.3 0.9 %collective-permute-done.10 = bf16[1088,128]{1,0:T(8,128)(2,1)S(1)} collective-permute-done((bf16[1088,128]{1,0:T(8,128)(2,1)S(1)}, bf16[1088,128]{1,0:T(8,128)(2,1)S(1)}, u32[]{:S(2)}, u32[]{:S(2)}) %collective-permute-start.10) | collective-permute-done | bytes 278560 | tf_op jit(solution)/shard_map/ppermute | solution.py:32
  29.3 0.1 collective-permute-start.12
  29.3 0.5 collective-permute-start.11
  29.8 4.1 %collective-permute-done.6 = bf16[32,5120]{1,0:T(8,128)(2,1)S(1)} collective-permute-done((bf16[32,5120]{1,0:T(8,128)(2,1)S(1)}, bf16[32,5120]{1,0:T(8,128)(2,1)S(1)}, u32[]{:S(2)}, u32[]{:S(2)}) %collective-permute-start.6) | collective-permute-done | bytes 327712 | tf_op jit(solution)/shard_map/ppermute | solution.py:32
  34.1 3.1 %collective-permute-done.2 = bf16[32,5120]{1,0:T(8,128)(2,1)S(1)} collective-permute-done((bf16[32,5120]{1,0:T(8,128)(2,1)S(1)}, bf16[32,5120]{1,0:T(8,128)(2,1)S(1)}, u32[]{:S(2)}, u32[]{:S(2)}) %collective-permute-start.2) | collective-permute-done | bytes 327712 | tf_op jit(solution)/shard_map/ppermute | solution.py:32
  37.4 4.1 %maxsim.3.refs_4_ = f32[16,8,128]{2,1,0:T(8,128)S(1)} custom-call(s32[257]{0:T(512)S(1)} %pad_add_fusion.lens, bf16[2176,128]{1,0:T(8,128)(2,1)S(1)} %pad_maximum_fusion.2.refs_0_, bf16[2176,128]{1,0:T(8,128)(2,1)S(1)} %collective-permute-done.12.refs_1_, bf16[256,128,128]{2,1,0:T(8,128)(2,1)S(1)} %copy-done), custom_call_target="tpu_custom_call" | custom-call | flops 2147483648 | bytes 8388608 | tf_op jit(solution)/shard_map/maxsim/pallas_call | solution.py:233
  41.6 3.6 %collective-permute-done.11.refs_0_.refs_2_ = bf16[2176,128]{1,0:T(8,128)(2,1)S(1)} collective-permute-done((bf16[2176,128]{1,0:T(8,128)(2,1)S(1)}, bf16[2176,128]{1,0:T(8,128)(2,1)S(1)}, u32[]{:S(2)}, u32[]{:S(2)}) %collective-permute-start.11) | collective-permute-done | bytes 557088 | tf_op jit(solution)/shard_map/ppermute | solution.py:32
  45.2 2.7 %maxsim.4.refs_5_ = f32[8,8,128]{2,1,0:T(8,128)S(1)} custom-call(s32[257]{0:T(512)S(1)} %pad_add_fusion.lens, bf16[2176,128]{1,0:T(8,128)(2,1)S(1)} %collective-permute-done.11.refs_0_.refs_2_, bf16[256,128,128]{2,1,0:T(8,128)(2,1)S(1)} %copy-done), custom_call_target="tpu_custom_call" | custom-call | flops 1073741824 | bytes 8388608 | tf_op jit(solution)/shard_map/maxsim/pallas_call | solution.py:233
  47.9 1.2 %collective-permute-done.7 = bf16[64,5120]{1,0:T(8,128)(2,1)S(1)} collective-permute-done((bf16[64,5120]{1,0:T(8,128)(2,1)S(1)}, bf16[64,5120]{1,0:T(8,128)(2,1)S(1)}, u32[]{:S(2)}, u32[]{:S(2)}) %collective-permute-start.7) | collective-permute-done | bytes 655392 | tf_op jit(solution)/shard_map/ppermute | solution.py:32
  49.2 0.5 collective-permute-start.14
  49.7 2.7 %maxsim.5.refs_6_ = f32[8,8,128]{2,1,0:T(8,128)S(1)} custom-call(s32[257]{0:T(512)S(1)} %pad_add_fusion.lens, bf16[2176,128]{1,0:T(8,128)(2,1)S(1)} %collective-permute-done.13.refs_0_.refs_3_, bf16[256,128,128]{2,1,0:T(8,128)(2,1)S(1)} %copy-done), custom_call_target="tpu_custom_call" | custom-call | flops 1073741824 | bytes 8388608 | tf_op jit(solution)/shard_map/maxsim/pallas_call | solution.py:233
  52.5 1.5 %beam.1.first = f32[256,512]{1,0:T(8,128)S(1)} custom-call(bf16[128,5120]{1,0:T(8,128)(2,1)S(1)} %constant_dynamic-update-slice_fusion.own, bf16[128,5120]{1,0:T(8,128)(2,1)S(1)} %collective-permute-done.15.other, bf16[512,10240]{1,0:T(8,128)(2,1)S(1)} %bitcast.10), custom_call_target="tpu_custom_call" | custom-call | flops 1342177280 | bytes 7864320 | tf_op jit(solution)/shard_map/beam/pallas_call | solution.py:267
  54.0 0.1 collective-permute-done.14.other
  54.1 1.8 %beam_last.1 = f32[32,8,128]{2,1,0:T(8,128)S(1)} custom-call(s32[1]{0:T(128)} %bitcast.me_ref, bf16[128,5120]{1,0:T(8,128)(2,1)S(1)} %constant_dynamic-update-slice_fusion.5.own, bf16[128,5120]{1,0:T(8,128)(2,1)S(1)} %collective-permute-done.14.other, bf16[512,10240]{1,0:T(8,128)(2,1)S(1)} %bitcast.10, f32[256,512]{1,0:T(8,128)S(1)} %beam.1.first, ...), custom_call_target="tpu_custom_call" | custom-call | flops 1342177280 | bytes 7864320 | tf_op jit(solution)/shard_map/beam_last/pallas_call | solution.py:278
  55.9 11.6 %all_to_all.5 = f32[32,8,128]{2,1,0:T(8,128)S(1)} all-to-all(f32[32,8,128]{2,1,0:T(8,128)S(1)} %beam_last.1), channel_id=1, replica_groups=mesh['dom'=32,'rep'=1] {'dom'}, dimensions={0} | all-to-all | bytes 262144 | tf_op jit(solution)/shard_map/all_to_all | solution.py:293
  67.6 0.1 slice_bitcast_fusion.2
  67.6 0.7 slice.23
  68.3 0.6 pad_maximum_fusion.9
  (42 shorter events, 0.9 us)
Async XLA Ops:
  1.6 17.5 %collective-permute-start.4 = (bf16[8,5120]{1,0:T(8,128)(2,1)S(1)}, bf16[8,5120]{1,0:T(8,128)(2,1)S(1)}, u32[]{:S(2)}, u32[]{:S(2)}) collective-permute-start(bf16[8,5120]{1,0:T(8,128)(2,1)S(1)} %get-tuple-element.11), channel_id=1, source_target_pairs={{0,16},{1,17},{2,18},{3,19},{4,20},{5,21},{6,22},{7,23},{8,24},{9,... | collective-permute-start | bytes 245768 | tf_op jit(solution)/shard_map/ppermute | solution.py:32
  7.7 14.9 %copy-start.1 = (bf16[272,128]{1,0:T(8,128)(2,1)S(1)}, bf16[272,128]{1,0:T(8,128)(2,1)}, u32[]{:S(2)}) copy-start(bf16[272,128]{1,0:T(8,128)(2,1)} %pack.1) | copy-start | bytes 208900
  7.7 8.9 %collective-permute-start.8 = (bf16[272,128]{1,0:T(8,128)(2,1)}, bf16[272,128]{1,0:T(8,128)(2,1)S(1)}, u32[]{:S(2)}, u32[]{:S(2)}) collective-permute-start(bf16[272,128]{1,0:T(8,128)(2,1)} %pack.1), channel_id=1, source_target_pairs={{0,16},{1,17},{2,18},{3,19},{4,20},{5,21},{6,22},{7,23},{8,24},{9,... | collective-permute-start | bytes 208904 | tf_op jit(solution)/shard_map/ppermute | solution.py:32
  7.7 12.9 %collective-permute-start = (bf16[8,5120]{1,0:T(8,128)(2,1)S(1)}, bf16[8,5120]{1,0:T(8,128)(2,1)S(1)}, u32[]{:S(2)}, u32[]{:S(2)}) collective-permute-start(bf16[8,5120]{1,0:T(8,128)(2,1)S(1)} %get-tuple-element.10), channel_id=1, source_target_pairs={{0,16},{1,17},{2,18},{3,19},{4,20},{5,21},{6,22},{7,23},{8,24},{9,... | collective-permute-start | bytes 245768 | tf_op jit(solution)/shard_map/ppermute | solution.py:32
  17.5 5.1 %collective-permute-start.9 = (bf16[544,128]{1,0:T(8,128)(2,1)S(1)}, bf16[544,128]{1,0:T(8,128)(2,1)S(1)}, u32[]{:S(2)}, u32[]{:S(2)}) collective-permute-start(bf16[544,128]{1,0:T(8,128)(2,1)S(1)} %pad_maximum_fusion.8), channel_id=1, source_target_pairs={{0,4},{1,5},{2,6},{3,7},{4,0},{5,1},{6,2},{7,3},{8,12},{9,13},{10,... | collective-permute-start | bytes 417800 | tf_op jit(solution)/shard_map/ppermute | solution.py:32
  19.1 18.4 %copy-start = (bf16[256,128,128]{2,1,0:T(8,128)(2,1)S(1)}, bf16[256,128,128]{2,1,0:T(8,128)(2,1)}, u32[]{:S(2)}) copy-start(bf16[256,128,128]{2,1,0:T(8,128)(2,1)} %refs_1_.3) | copy-start | bytes 25165828
  19.1 7.0 %collective-permute-start.5 = (bf16[16,5120]{1,0:T(8,128)(2,1)S(1)}, bf16[16,5120]{1,0:T(8,128)(2,1)S(1)}, u32[]{:S(2)}, u32[]{:S(2)}) collective-permute-start(bf16[16,5120]{1,0:T(8,128)(2,1)S(1)} %pad_maximum_fusion.7), channel_id=1, source_target_pairs={{0,2},{1,3},{2,0},{3,1},{4,6},{5,7},{6,4},{7,5},{8,10},{9,11},{10,... | collective-permute-start | bytes 491528 | tf_op jit(solution)/shard_map/ppermute | solution.py:32
  20.6 7.2 %collective-permute-start.1 = (bf16[16,5120]{1,0:T(8,128)(2,1)S(1)}, bf16[16,5120]{1,0:T(8,128)(2,1)S(1)}, u32[]{:S(2)}, u32[]{:S(2)}) collective-permute-start(bf16[16,5120]{1,0:T(8,128)(2,1)S(1)} %pad_maximum_fusion.6), channel_id=1, source_target_pairs={{0,8},{1,9},{2,10},{3,11},{4,12},{5,13},{6,14},{7,15},{8,0},{9,1},... | collective-permute-start | bytes 491528 | tf_op jit(solution)/shard_map/ppermute | solution.py:32
  22.6 6.6 %collective-permute-start.10 = (bf16[1088,128]{1,0:T(8,128)(2,1)S(1)}, bf16[1088,128]{1,0:T(8,128)(2,1)S(1)}, u32[]{:S(2)}, u32[]{:S(2)}) collective-permute-start(bf16[1088,128]{1,0:T(8,128)(2,1)S(1)} %pad_maximum_fusion.5), channel_id=1, source_target_pairs={{0,2},{1,3},{2,0},{3,1},{4,6},{5,7},{6,4},{7,5},{8,10},{9,11},{10,... | collective-permute-start | bytes 835592 | tf_op jit(solution)/shard_map/ppermute | solution.py:32
  26.1 7.9 %collective-permute-start.6 = (bf16[32,5120]{1,0:T(8,128)(2,1)S(1)}, bf16[32,5120]{1,0:T(8,128)(2,1)S(1)}, u32[]{:S(2)}, u32[]{:S(2)}) collective-permute-start(bf16[32,5120]{1,0:T(8,128)(2,1)S(1)} %pad_maximum_fusion.4), channel_id=1, source_target_pairs={{0,8},{1,9},{2,10},{3,11},{4,12},{5,13},{6,14},{7,15},{8,0},{9,1},... | collective-permute-start | bytes 983048 | tf_op jit(solution)/shard_map/ppermute | solution.py:32
  27.8 9.4 %collective-permute-start.2 = (bf16[32,5120]{1,0:T(8,128)(2,1)S(1)}, bf16[32,5120]{1,0:T(8,128)(2,1)S(1)}, u32[]{:S(2)}, u32[]{:S(2)}) collective-permute-start(bf16[32,5120]{1,0:T(8,128)(2,1)S(1)} %pad_maximum_fusion.3), channel_id=1, source_target_pairs={{0,4},{1,5},{2,6},{3,7},{4,0},{5,1},{6,2},{7,3},{8,12},{9,13},{10,... | collective-permute-start | bytes 983048 | tf_op jit(solution)/shard_map/ppermute | solution.py:32
  29.3 8.1 %collective-permute-start.12 = (bf16[2176,128]{1,0:T(8,128)(2,1)S(1)}, bf16[2176,128]{1,0:T(8,128)(2,1)S(1)}, u32[]{:S(2)}, u32[]{:S(2)}) collective-permute-start(bf16[2176,128]{1,0:T(8,128)(2,1)S(1)} %pad_maximum_fusion.2.refs_0_), channel_id=1, source_target_pairs={{0,1},{1,0},{2,3},{3,2},{4,5},{5,4},{6,7},{7,6},{8,9},{9,8},{10,11... | collective-permute-start | bytes 1671176 | tf_op jit(solution)/shard_map/ppermute | solution.py:32
  29.3 15.8 %collective-permute-start.11 = (bf16[2176,128]{1,0:T(8,128)(2,1)S(1)}, bf16[2176,128]{1,0:T(8,128)(2,1)S(1)}, u32[]{:S(2)}, u32[]{:S(2)}) collective-permute-start(bf16[2176,128]{1,0:T(8,128)(2,1)S(1)} %pad_maximum_fusion.2.refs_0_), channel_id=1, source_target_pairs={{0,8},{1,9},{2,10},{3,11},{4,12},{5,13},{6,14},{7,15},{8,0},{9,1},... | collective-permute-start | bytes 1671176 | tf_op jit(solution)/shard_map/ppermute | solution.py:32
  34.0 15.0 %collective-permute-start.7 = (bf16[64,5120]{1,0:T(8,128)(2,1)S(1)}, bf16[64,5120]{1,0:T(8,128)(2,1)S(1)}, u32[]{:S(2)}, u32[]{:S(2)}) collective-permute-start(bf16[64,5120]{1,0:T(8,128)(2,1)S(1)} %pad_maximum_fusion.1), channel_id=1, source_target_pairs={{0,4},{1,5},{2,6},{3,7},{4,0},{5,1},{6,2},{7,3},{8,12},{9,13},{10,... | collective-permute-start | bytes 1966088 | tf_op jit(solution)/shard_map/ppermute | solution.py:32
  37.2 11.8 %collective-permute-start.3 = (bf16[64,5120]{1,0:T(8,128)(2,1)S(1)}, bf16[64,5120]{1,0:T(8,128)(2,1)S(1)}, u32[]{:S(2)}, u32[]{:S(2)}) collective-permute-start(bf16[64,5120]{1,0:T(8,128)(2,1)S(1)} %pad_maximum_fusion), channel_id=1, source_target_pairs={{0,2},{1,3},{2,0},{3,1},{4,6},{5,7},{6,4},{7,5},{8,10},{9,11},{10,... | collective-permute-start | bytes 1966088 | tf_op jit(solution)/shard_map/ppermute | solution.py:32
  45.2 4.0 %collective-permute-start.13 = (bf16[2176,128]{1,0:T(8,128)(2,1)S(1)}, bf16[2176,128]{1,0:T(8,128)(2,1)S(1)}, u32[]{:S(2)}, u32[]{:S(2)}) collective-permute-start(bf16[2176,128]{1,0:T(8,128)(2,1)S(1)} %collective-permute-done.11.refs_0_.refs_2_), channel_id=1, source_target_pairs={{0,1},{1,0},{2,3},{3,2},{4,5},{5,4},{6,7},{7,6},{8,9},{9,8},{10,11... | collective-permute-start | bytes 1671176 | tf_op jit(solution)/shard_map/ppermute | solution.py:32
  45.2 7.3 %slice-start = ((s8[10485760]{0:T(1024)(128)(4,1)}), s8[4194304]{0:T(1024)(128)(4,1)S(1)}, s32[]{:S(2)}) async-start(s8[10485760]{0:T(1024)(128)(4,1)} %bitcast.9), calls=%async_computation.1 | async-start | bytes 8388608
  45.2 7.3 %slice-start.1 = ((s8[10485760]{0:T(1024)(128)(4,1)}), s8[4194304]{0:T(1024)(128)(4,1)S(1)}, s32[]{:S(2)}) async-start(s8[10485760]{0:T(1024)(128)(4,1)} %bitcast.9), calls=%async_computation.2 | async-start | bytes 8388608
  49.1 3.3 %slice-start.2 = ((s8[10485760]{0:T(1024)(128)(4,1)}), s8[2097152]{0:T(1024)(128)(4,1)S(1)}, s32[]{:S(2)}) async-start(s8[10485760]{0:T(1024)(128)(4,1)} %bitcast.9), calls=%async_computation.3 | async-start | bytes 4194304
  49.2 3.3 %collective-permute-start.15 = (bf16[128,5120]{1,0:T(8,128)(2,1)S(1)}, bf16[128,5120]{1,0:T(8,128)(2,1)S(1)}, u32[]{:S(2)}, u32[]{:S(2)}) collective-permute-start(bf16[128,5120]{1,0:T(8,128)(2,1)S(1)} %constant_dynamic-update-slice_fusion.own), channel_id=1, source_target_pairs={{0,1},{1,0},{2,3},{3,2},{4,5},{5,4},{6,7},{7,6},{8,9},{9,8},{10,11... | collective-permute-start | bytes 3932168 | tf_op jit(solution)/shard_map/ppermute | solution.py:32
  49.2 4.9 %collective-permute-start.14 = (bf16[128,5120]{1,0:T(8,128)(2,1)S(1)}, bf16[128,5120]{1,0:T(8,128)(2,1)S(1)}, u32[]{:S(2)}, u32[]{:S(2)}) collective-permute-start(bf16[128,5120]{1,0:T(8,128)(2,1)S(1)} %constant_dynamic-update-slice_fusion.5.own), channel_id=1, source_target_pairs={{0,1},{1,0},{2,3},{3,2},{4,5},{5,4},{6,7},{7,6},{8,9},{9,8},{10,11... | collective-permute-start | bytes 3932168 | tf_op jit(solution)/shard_map/ppermute | solution.py:32
